TPU v7x, 32 devices: a whole 2x2x4 slice. The times are simulated.
32 devices in a mesh: gx: 2 (over x), gy: 4 (over z), gz: 4 (over y, core).
Axes of the slice: x: 2, y: 2, z: 4, core: 2. Of those that a mesh axis runs over, the one named last changes fastest.
Arguments:
- fields: float32 [12, 16, 32, 512], P(None, 'gx', 'gy', 'gz'), as said below
- reacting: int32 [16, 32, 512], P('gx', 'gy', 'gz'), may hold values from 0 to 1, as said below
- panel_map: int32 [2, 16, 512], P(None, 'gx', 'gz'), may hold values from 0 to 255, as said below
- layer_one: bfloat16 [1600, 12], replicated, may hold values from -4 to 4
- layer_two: bfloat16 [800, 1600], replicated, may hold values from -0.21875 to 0.21875
- layer_three: bfloat16 [400, 800], replicated, may hold values from -0.3125 to 0.3125
- layer_four: bfloat16 [12, 400], replicated, may hold values from -0.3125 to 0.3125
Outputs:
- new_fields: float32 [12, 16, 32, 512], P(None, 'gx', 'gy', 'gz')
- impulse: float32 [256], P(('gx', 'gy', 'gz'))
Inputs may be any that keep to these rules, and one draw needn't show every extreme that they name: `fields`: component 0 (density) lies between 0.3 and 3.3; the velocities (components 1 to 3 over component 0) between -1.2 and 1.2; the pressure 0.4 (component 4 - |momentum|^2 / (2 density)) between 0.3 and 5; components 5 to 11 are 0.01 to 0.14 times component 0. Each device's aligned block of 8 x 8 x 128 cells holds at most 128 reacting cells. The blocks that share their ranges along the second and third dimensions hold exactly 64 reacting cells each on average, and one in eight of them, and at least one, hold exactly 128. `panel_map`: every panel is a patch of 8 x 8 cells of one wall, shifted by 4 cells along the first dimension and closed around it; panels are numbered in a random order and each number is used once.
All inputs are finite; a program needn't handle non-finite values.
Results may differ from a plain program's by a relative error of at most 0.0014.
Values may be sent and summed in bfloat16 or wider, within the bound.
No kernel may reach another device: no remote copies, remote signals or barrier semaphores. Data moves between devices by JAX's collectives and lax.ppermute only.
A program may use at most 64 MiB of HBM per device.

v0:
```python
import jax
import jax.numpy as jnp
from jax import lax
from jax.sharding import PartitionSpec as P

BAL = 64
COMPS = 12
PATCH = 8


HEAT_RATIO = 1.4
TIME_STEP = 0.1
CHEM_STEP = 0.25
WENO_EPS = 1e-06


def extended(array, sides, width):
    for axis, dim in sides:
        size, length = (lax.axis_size(axis), array.shape[dim])
        up = [(i, (i + 1) % size) for i in range(size - 1)]
        down = [(j, i) for i, j in up]
        last = lax.slice_in_dim(array, length - width, length, axis=dim)
        initial = lax.slice_in_dim(array, 0, width, axis=dim)
        before = lax.ppermute(last, axis, up)
        after = lax.ppermute(initial, axis, down)
        array = jnp.concatenate([before, array, after], axis=dim)
    return array


def take_slab(array_in, begin_at, length_of, flux_axis):
    return lax.slice_in_dim(array_in, begin_at, begin_at + length_of, axis=flux_axis)


def weno_face(upwind_two, upwind_one, center, downwind_one, downwind_two):
    cand_zero = (2.0 * upwind_two - 7.0 * upwind_one + 11.0 * center) / 6.0
    cand_one = (-upwind_one + 5.0 * center + 2.0 * downwind_one) / 6.0
    cand_two = (2.0 * center + 5.0 * downwind_one - downwind_two) / 6.0
    smooth_zero = (
        13.0 / 12.0 * (upwind_two - 2.0 * upwind_one + center) ** 2
        + 0.25 * (upwind_two - 4.0 * upwind_one + 3.0 * center) ** 2
    )
    smooth_one = (
        13.0 / 12.0 * (upwind_one - 2.0 * center + downwind_one) ** 2
        + 0.25 * (upwind_one - downwind_one) ** 2
    )
    smooth_two = (
        13.0 / 12.0 * (center - 2.0 * downwind_one + downwind_two) ** 2
        + 0.25 * (3.0 * center - 4.0 * downwind_one + downwind_two) ** 2
    )
    weight_zero = 0.1 / (WENO_EPS + smooth_zero) ** 2
    weight_one = 0.6 / (WENO_EPS + smooth_one) ** 2
    weight_two = 0.3 / (WENO_EPS + smooth_two) ** 2
    weight_sum = weight_zero + weight_one + weight_two
    return (weight_zero * cand_zero + weight_one * cand_one + weight_two * cand_two) / weight_sum


def to_recon(fields):
    density = fields[0]
    velocity = fields[1:4] / density[None]
    pressure = (HEAT_RATIO - 1.0) * (
        fields[4] - 0.5 * density * jnp.sum(velocity * velocity, axis=0)
    )
    fractions = fields[5:] / density[None]
    return jnp.concatenate(
        [jnp.log(density)[None], velocity, jnp.log(pressure)[None], fractions], axis=0
    )


def normal_of(normal, ndims):
    return (jnp.arange(3) == normal).reshape((3,) + (1,) * (ndims - 1))


def side_terms(recon, normal):
    density = jnp.exp(recon[0])
    velocity = recon[1:4]
    pressure = jnp.exp(recon[4])
    fractions = recon[5:]
    speed_n = velocity[normal]
    energy = pressure / (HEAT_RATIO - 1.0) + 0.5 * density * jnp.sum(velocity * velocity, axis=0)
    conserved = jnp.concatenate(
        [density[None], density[None] * velocity, energy[None], density[None] * fractions], axis=0
    )
    mass_flux = density * speed_n
    normal_mask = normal_of(normal, recon.ndim)
    momentum_flux = mass_flux[None] * velocity + jnp.where(normal_mask, pressure[None], 0.0)
    flux_terms = jnp.concatenate(
        [
            mass_flux[None],
            momentum_flux,
            ((energy + pressure) * speed_n)[None],
            mass_flux[None] * fractions,
        ],
        axis=0,
    )
    sound_speed = jnp.sqrt(HEAT_RATIO * pressure / density)
    return (
        density,
        velocity,
        pressure,
        fractions,
        energy,
        conserved,
        flux_terms,
        speed_n,
        sound_speed,
    )


def star_state(
    density, velocity, pressure, fractions, energy, speed_n, wave_speed, contact, normal_mask
):
    relative = wave_speed - speed_n
    factor = density * relative / (wave_speed - contact)
    star_velocity = jnp.where(normal_mask, contact[None], velocity)
    star_energy = energy / density + (contact - speed_n) * (
        contact + pressure / (density * relative)
    )
    return jnp.concatenate(
        [
            factor[None],
            factor[None] * star_velocity,
            (factor * star_energy)[None],
            factor[None] * fractions,
        ],
        axis=0,
    )


def hllc_flux(left_recon, right_recon, normal):
    (
        left_density,
        left_velocity,
        left_pressure,
        left_fractions,
        left_energy,
        left_cons,
        left_flux,
        left_speed,
        left_sound,
    ) = side_terms(left_recon, normal)
    (
        right_density,
        right_velocity,
        right_pressure,
        right_fractions,
        right_energy,
        right_cons,
        right_flux,
        right_speed,
        right_sound,
    ) = side_terms(right_recon, normal)
    wave_left = jnp.minimum(left_speed - left_sound, right_speed - right_sound)
    wave_right = jnp.maximum(left_speed + left_sound, right_speed + right_sound)
    left_rel = wave_left - left_speed
    right_rel = wave_right - right_speed
    contact = (
        right_pressure
        - left_pressure
        + left_density * left_speed * left_rel
        - right_density * right_speed * right_rel
    ) / (left_density * left_rel - right_density * right_rel)
    normal_mask = normal_of(normal, left_recon.ndim)
    star_left = star_state(
        left_density,
        left_velocity,
        left_pressure,
        left_fractions,
        left_energy,
        left_speed,
        wave_left,
        contact,
        normal_mask,
    )
    star_right = star_state(
        right_density,
        right_velocity,
        right_pressure,
        right_fractions,
        right_energy,
        right_speed,
        wave_right,
        contact,
        normal_mask,
    )
    left_star_flux = left_flux + wave_left[None] * (star_left - left_cons)
    right_star_flux = right_flux + wave_right[None] * (star_right - right_cons)
    return jnp.where(
        wave_left[None] >= 0,
        left_flux,
        jnp.where(
            contact[None] >= 0,
            left_star_flux,
            jnp.where(wave_right[None] > 0, right_star_flux, right_flux),
        ),
    )


def face_flux(padded, normal):
    flux_axis = normal + 1
    face_count = padded.shape[flux_axis] - 5
    stencil = [take_slab(padded, offset, face_count, flux_axis) for offset in range(6)]
    left_state = weno_face(stencil[0], stencil[1], stencil[2], stencil[3], stencil[4])
    right_state = weno_face(stencil[5], stencil[4], stencil[3], stencil[2], stencil[1])
    return hllc_flux(left_state, right_state, normal)


def mirror_walls(padded, normal, at_first, at_last):
    flux_axis = normal + 1
    cell_count = padded.shape[flux_axis] - 6
    flip_sign = (
        jnp.where(jnp.arange(padded.shape[0]) == 1 + normal, -1.0, 1.0)
        .astype(padded.dtype)
        .reshape((-1, 1, 1, 1))
    )
    ghost_low = jnp.flip(take_slab(padded, 3, 3, flux_axis), flux_axis) * flip_sign
    ghost_high = jnp.flip(take_slab(padded, cell_count, 3, flux_axis), flux_axis) * flip_sign
    low_side = jnp.where(at_first, ghost_low, take_slab(padded, 0, 3, flux_axis))
    high_side = jnp.where(at_last, ghost_high, take_slab(padded, cell_count + 3, 3, flux_axis))
    return jnp.concatenate(
        [low_side, take_slab(padded, 3, cell_count, flux_axis), high_side], axis=flux_axis
    )


def chem_rates(features, layer_one, layer_two, layer_three, layer_four):
    hidden_one = jax.nn.gelu(
        jnp.dot(layer_one, features, preferred_element_type=jnp.float32)
    ).astype(jnp.bfloat16)
    hidden_two = jax.nn.gelu(
        jnp.dot(layer_two, hidden_one, preferred_element_type=jnp.float32)
    ).astype(jnp.bfloat16)
    hidden_three = jax.nn.gelu(
        jnp.dot(layer_three, hidden_two, preferred_element_type=jnp.float32)
    ).astype(jnp.bfloat16)
    return jnp.dot(layer_four, hidden_three, preferred_element_type=jnp.float32).astype(
        jnp.bfloat16
    )


def body(fields, reacting, panel_map, layer_one, layer_two, layer_three, layer_four):
    recon_fields = to_recon(fields)
    gx_count = lax.axis_size("gx")
    gy_count = lax.axis_size("gy")
    gz_count = lax.axis_size("gz")
    at_first = (lax.axis_index("gx") == 0, lax.axis_index("gy") == 0, lax.axis_index("gz") == 0)
    at_last = (
        lax.axis_index("gx") == gx_count - 1,
        lax.axis_index("gy") == gy_count - 1,
        lax.axis_index("gz") == gz_count - 1,
    )
    line_fields = (
        extended(recon_fields.astype(jnp.bfloat16), (("gx", 1),), 3).astype(recon_fields.dtype),
        extended(recon_fields, (("gy", 2),), 3),
        extended(recon_fields.astype(jnp.bfloat16), (("gz", 3),), 3).astype(recon_fields.dtype),
    )
    update = jnp.zeros_like(fields)
    push_low = None
    push_high = None
    for normal in range(3):
        line_block = mirror_walls(line_fields[normal], normal, at_first[normal], at_last[normal])
        face_fluxes = face_flux(line_block, normal)
        cell_count = face_fluxes.shape[normal + 1] - 1
        change = take_slab(face_fluxes, 1, cell_count, normal + 1) - take_slab(
            face_fluxes, 0, cell_count, normal + 1
        )
        update = update + change
        if normal == 1:
            push_low = face_fluxes[2, :, 0, :]
            push_high = face_fluxes[2, :, cell_count, :]
    cell_total = reacting.size
    react_flags = reacting.reshape(cell_total)
    capacity = BAL * min(4, gx_count)
    per_peer = capacity // gx_count
    row_rank = jnp.cumsum(react_flags) - 1
    slot_index = jnp.where(
        react_flags == 1, row_rank % gx_count * per_peer + row_rank // gx_count, capacity
    )
    flat_features = recon_fields.reshape(COMPS, cell_total).astype(jnp.bfloat16)
    packed = (
        jnp.zeros((COMPS, capacity), jnp.bfloat16).at[:, slot_index].set(flat_features, mode="drop")
    )
    rate_packed = chem_rates(packed, layer_one, layer_two, layer_three, layer_four)
    gathered = rate_packed[:, jnp.where(react_flags == 1, slot_index, 0)]
    source = jnp.where(react_flags[None, :] == 1, gathered.astype(jnp.float32), 0.0).reshape(
        fields.shape
    )
    new_fields = fields - TIME_STEP * update + CHEM_STEP * source
    on_low = lax.axis_index("gy") == 0
    on_high = lax.axis_index("gy") == gy_count - 1
    push_values = jnp.concatenate(
        [
            jnp.where(on_low, push_low, 0.0).reshape(-1),
            jnp.where(on_high, push_high, 0.0).reshape(-1),
        ]
    )
    panel_ids = jnp.concatenate([panel_map[0].reshape(-1), panel_map[1].reshape(-1)])
    panels_all = 2 * (fields.shape[1] * gx_count // PATCH) * (fields.shape[3] * gz_count // PATCH)
    own_panels = panels_all // (gx_count * gy_count * gz_count)
    partial_loads = jax.ops.segment_sum(push_values, panel_ids, num_segments=panels_all)
    totals = lax.psum(partial_loads, ("gx", "gy", "gz"))
    flat_index = (
        lax.axis_index("gx") * gy_count + lax.axis_index("gy")
    ) * gz_count + lax.axis_index("gz")
    result = lax.dynamic_slice_in_dim(totals, flat_index * own_panels, own_panels)
    impulse = result / float(PATCH * PATCH)
    return (new_fields, impulse)


def solution(mesh):
    return jax.shard_map(
        body,
        mesh=mesh,
        in_specs=(
            P(None, "gx", "gy", "gz"),
            P("gx", "gy", "gz"),
            P(None, "gx", "gz"),
            P(),
            P(),
            P(),
            P(),
        ),
        out_specs=(P(None, "gx", "gy", "gz"), P(("gx", "gy", "gz"))),
        check_vma=False,
    )
```

profile of v0, /device:TPU:0, one launch (start us, length us, event | category | flops | bytes accessed | tf_op | source)
XLA Modules:
  0.0 187.7 jit_solution(13884582673707735908)
XLA Ops:
  2.9 5.5 %collective-permute-start = (bf16[12,3,8,128]{3,1,2,0:T(4,128)(2,1)}, bf16[12,3,8,128]{3,1,2,0:T(4,128)(2,1)}, u32[]{:S(2)}, u32[]{:S(2)}) collective-permute-start(bf16[12,3,8,128]{3,1,2,0:T(4,128)(2,1)} %get-tuple-element.136), channel_id=1, source_target_pairs={{0,16},{1,17},{2,18},{3,19},{4,20},{5,21},{6,22},{7,23},{8,24},{9,... | collective-permute-start | bytes 221192 | tf_op jit(solution)/shard_map/ppermute | solution.py:24
  8.4 1.3 collective-permute-start.1
  10.4 4.3 %collective-permute-start.2 = (f32[12,8,3,128]{3,1,2,0:T(8,128)}, f32[12,8,3,128]{3,1,2,0:T(8,128)}, u32[]{:S(2)}, u32[]{:S(2)}) collective-permute-start(f32[12,8,3,128]{3,1,2,0:T(8,128)} %get-tuple-element.135), channel_id=1, source_target_pairs={{0,4},{4,8},{8,12},{1,5},{5,9},{9,13},{2,6},{6,10},{10,14},{3,7},{... | collective-permute-start | bytes 442376 | tf_op jit(solution)/shard_map/ppermute | solution.py:24
  14.9 2.0 %collective-permute-start.4 = (bf16[12,8,8,3]{3,1,2,0:T(8,128)(2,1)S(1)}, bf16[12,8,8,3]{3,1,2,0:T(8,128)(2,1)}, u32[]{:S(2)}, u32[]{:S(2)}) collective-permute-start(bf16[12,8,8,3]{3,1,2,0:T(8,128)(2,1)S(1)} %get-tuple-element.138), channel_id=1, source_target_pairs={{0,1},{1,2},{2,3},{4,5},{5,6},{6,7},{8,9},{9,10},{10,11},{12,13},{... | collective-permute-start | bytes 13832 | tf_op jit(solution)/shard_map/ppermute | solution.py:24
  21.4 1.8 copy.43
  24.9 21.1 %scatter_custom_fusion = bf16[12,128]{0,1:T(8,128)(2,1)S(1)} fusion(s32[8192]{0:T(1024)S(1)} %bitcast.220, bf16[8192,12]{1,0:T(8,128)(2,1)} %copy.43, bf16[]{:T(256)} %constant.77.clone.1), kind=kCustom, calls=%fused_computation.369 | custom fusion | bytes 3584 | tf_op jit(solution)/shard_map/scatter | solution.py:279
  46.1 1.9 %fusion.117 = bf16[800,128]{1,0:T(8,128)(2,1)} fusion(bf16[800,1600]{1,0:T(8,128)(2,1)S(1)} %copy-done, bf16[12,128]{0,1:T(8,128)(2,1)S(1)} %scatter_custom_fusion, bf16[1600,12]{0,1:T(8,128)(2,1)S(1)} %copy-done.19), kind=kOutput, calls=%fused_computation.175 | convolution fusion | flops 335360000 | bytes 2806272 | tf_op jit(solution)/shard_map/dot_general | solution.py:229
  48.0 1.7 fusion
  50.4 29.4 %gather_fusion = bf16[8192,12]{1,0:T(8,128)(2,1)} fusion(bf16[12,128]{0,1:T(8,128)(2,1)S(1)} %copy.44, s32[8192]{0:T(1024)S(1)} %broadcast_clamp_fusion), kind=kCustom, calls=%fused_computation | custom fusion | bytes 425984 | tf_op jit(solution)/shard_map/gather | solution.py:282
  79.9 3.8 %convert_element_type.44 = f32[8192,12]{1,0:T(8,128)} convert(bf16[8192,12]{1,0:T(8,128)(2,1)} %gather_fusion) | non-fusion elementwise | flops 98304 | bytes 589824 | tf_op jit(solution)/shard_map/convert_element_type | solution.py:283
  83.7 3.6 %copy.46 = f32[12,8,8,128]{3,1,2,0:T(8,128)} copy(f32[12,8,8,128]{0,3,2,1:T(8,128)} %bitcast.177) | data formatting | bytes 786432 | tf_op jit(solution)/shard_map/convert_element_type | solution.py:283
  87.3 1.5 collective-permute-start.3
  88.7 1.4 maximum_convert_fusion.1
  92.1 1.9 %rev.25 = f32[12,8,8,3]{3,1,2,0:T(8,128)} reverse(f32[12,8,8,3]{3,1,2,0:T(8,128)} %get-tuple-element.106), dimensions={3} | reverse | bytes 18432 | tf_op jit(solution)/shard_map/jit(_flip)/rev | solution.py:215
  94.0 1.9 %rev.26 = f32[12,8,8,3]{3,1,2,0:T(8,128)} reverse(f32[12,8,8,3]{3,1,2,0:T(8,128)} %get-tuple-element.105), dimensions={3} | reverse | bytes 18432 | tf_op jit(solution)/shard_map/jit(_flip)/rev | solution.py:216
  95.9 1.4 slice_select_fusion
  97.3 4.1 %add_divide_fusion = (f32[12,8,8,129]{3,1,2,0:T(8,128)S(1)}, f32[12,8,8,129]{3,1,2,0:T(8,128)S(1)}) fusion(f32[12,8,8,3]{3,1,2,0:T(8,128)S(1)} %get-tuple-element.67, f32[12,8,8,128]{3,1,2,0:T(8,128)S(1)} %copy-done.8, f32[12,8,8,3]{3,1,2,0:T(8,128)S(1)} %get-tuple-element.68), kind=kLoop, calls=%fused_computation.63 | loop fusion | flops 13374720 | bytes 1204224 | tf_op jit(solution)/shard_map/div | solution.py:54
  102.8 1.4 fusion.20
  107.0 1.8 rev.21
  108.8 1.8 rev.22
  111.8 6.6 %add_divide_fusion.1 = (f32[12,9,8,128]{3,1,2,0:T(8,128)S(1)}, f32[12,9,8,128]{3,1,2,0:T(8,128)S(1)}) fusion(f32[12,3,8,128]{3,1,2,0:T(4,128)S(1)} %get-tuple-element.61, f32[12,8,8,128]{3,1,2,0:T(8,128)} %slice.357, f32[12,3,8,128]{3,1,2,0:T(4,128)S(1)} %get-tuple-element.62), kind=kLoop, calls=%fused_computation.90 | loop fusion | flops 14929920 | bytes 1572864 | tf_op jit(solution)/shard_map/div | solution.py:54
  121.7 1.9 %add_divide_fusion.2 = (f32[12,8,9,128]{3,1,2,0:T(8,128)S(1)}, f32[12,8,9,128]{3,1,2,0:T(8,128)S(1)}) fusion(f32[12,8,11,128]{3,1,2,0:T(8,128)S(1)} %get-tuple-element.132, f32[12,8,11,128]{3,1,2,0:T(8,128)S(1)} %get-tuple-element.133), kind=kLoop, calls=%fused_computation.141 | loop fusion | flops 13713408 | bytes 3538944 | tf_op jit(solution)/shard_map/div | solution.py:54
  126.8 14.8 %scatter_custom_fusion.1 = f32[256]{0:T(256)S(1)} fusion(s32[2048]{0:T(1024)} %pad_add_fusion, f32[2048]{0:T(1024)S(1)} %pad_maximum_fusion.9, f32[]{:T(128)} %constant.54.clone.1), kind=kCustom, calls=%fused_computation.388 | custom fusion | flops 2048 | bytes 1536 | tf_op jit(solution)/shard_map/scatter-add | solution.py:298
  141.6 45.5 %psum.7 = f32[256]{0:T(256)S(1)} all-reduce(f32[256]{0:T(256)S(1)} %scatter_custom_fusion.1), channel_id=1, replica_groups=mesh['gx'=2,'gy'=4,'gz'=4] {'gx','gy','gz'}, use_global_device_ids=true, to_apply=%region_11.12 | all-reduce | flops 256 | bytes 2048 | tf_op jit(solution)/shard_map/psum | solution.py:299
  (133 shorter events, 24.0 us)
Async XLA Ops:
  0.6 45.4 %copy-start = (bf16[800,1600]{1,0:T(8,128)(2,1)S(1)}, bf16[800,1600]{1,0:T(8,128)(2,1)}, u32[]{:S(2)}) copy-start(bf16[800,1600]{1,0:T(8,128)(2,1)} %param.11) | copy-start | bytes 7680004
  1.9 13.0 %copy-start.9 = (f32[1,8,8,128]{3,1,2,0:T(8,128)}, f32[1,8,8,128]{3,1,2,0:T(8,128)S(1)}, u32[]{:S(2)}) copy-start(f32[1,8,8,128]{3,1,2,0:T(8,128)S(1)} %get-tuple-element.131) | copy-start | bytes 98308
  2.0 19.1 %copy-start.3 = (f32[7,8,8,128]{3,1,2,0:T(8,128)}, f32[7,8,8,128]{3,1,2,0:T(8,128)S(1)}, u32[]{:S(2)}) copy-start(f32[7,8,8,128]{3,1,2,0:T(8,128)S(1)} %get-tuple-element.13) | copy-start | bytes 688132
  2.0 19.1 %copy-start.11 = (f32[1,8,8,128]{3,1,2,0:T(8,128)}, f32[1,8,8,128]{3,1,2,0:T(8,128)S(1)}, u32[]{:S(2)}) copy-start(f32[1,8,8,128]{3,1,2,0:T(8,128)S(1)} %get-tuple-element.11) | copy-start | bytes 98308
  2.1 12.6 %copy-start.1 = (bf16[12,8,8,128]{3,1,2,0:T(8,128)(2,1)}, bf16[12,8,8,128]{3,1,2,0:T(8,128)(2,1)S(1)}, u32[]{:S(2)}) copy-start(bf16[12,8,8,128]{3,1,2,0:T(8,128)(2,1)S(1)} %fusion.183) | copy-start | bytes 589828
  2.9 101.3 %collective-permute-start = (bf16[12,3,8,128]{3,1,2,0:T(4,128)(2,1)}, bf16[12,3,8,128]{3,1,2,0:T(4,128)(2,1)}, u32[]{:S(2)}, u32[]{:S(2)}) collective-permute-start(bf16[12,3,8,128]{3,1,2,0:T(4,128)(2,1)} %get-tuple-element.136), channel_id=1, source_target_pairs={{0,16},{1,17},{2,18},{3,19},{4,20},{5,21},{6,22},{7,23},{8,24},{9,... | collective-permute-start | bytes 221192 | tf_op jit(solution)/shard_map/ppermute | solution.py:24
  8.4 95.8 %collective-permute-start.1 = (bf16[12,3,8,128]{3,1,2,0:T(4,128)(2,1)}, bf16[12,3,8,128]{3,1,2,0:T(4,128)(2,1)}, u32[]{:S(2)}, u32[]{:S(2)}) collective-permute-start(bf16[12,3,8,128]{3,1,2,0:T(4,128)(2,1)} %get-tuple-element.137), channel_id=1, source_target_pairs={{16,0},{17,1},{18,2},{19,3},{20,4},{21,5},{22,6},{23,7},{24,8},{25... | collective-permute-start | bytes 221192 | tf_op jit(solution)/shard_map/ppermute | solution.py:25
  10.4 12.8 %copy-start.13 = (s32[8,8,128]{2,1,0:T(8,128)S(1)}, s32[8,8,128]{2,1,0:T(8,128)}, u32[]{:S(2)}) copy-start(s32[8,8,128]{2,1,0:T(8,128)} %param.8) | copy-start | bytes 98308
  10.4 109.8 %collective-permute-start.2 = (f32[12,8,3,128]{3,1,2,0:T(8,128)}, f32[12,8,3,128]{3,1,2,0:T(8,128)}, u32[]{:S(2)}, u32[]{:S(2)}) collective-permute-start(f32[12,8,3,128]{3,1,2,0:T(8,128)} %get-tuple-element.135), channel_id=1, source_target_pairs={{0,4},{4,8},{8,12},{1,5},{5,9},{9,13},{2,6},{6,10},{10,14},{3,7},{... | collective-permute-start | bytes 442376 | tf_op jit(solution)/shard_map/ppermute | solution.py:24
  14.9 72.4 %collective-permute-start.4 = (bf16[12,8,8,3]{3,1,2,0:T(8,128)(2,1)S(1)}, bf16[12,8,8,3]{3,1,2,0:T(8,128)(2,1)}, u32[]{:S(2)}, u32[]{:S(2)}) collective-permute-start(bf16[12,8,8,3]{3,1,2,0:T(8,128)(2,1)S(1)} %get-tuple-element.138), channel_id=1, source_target_pairs={{0,1},{1,2},{2,3},{4,5},{5,6},{6,7},{8,9},{9,10},{10,11},{12,13},{... | collective-permute-start | bytes 13832 | tf_op jit(solution)/shard_map/ppermute | solution.py:24
  16.8 71.9 %collective-permute-start.5 = (bf16[12,8,8,3]{3,1,2,0:T(8,128)(2,1)S(1)}, bf16[12,8,8,3]{3,1,2,0:T(8,128)(2,1)}, u32[]{:S(2)}, u32[]{:S(2)}) collective-permute-start(bf16[12,8,8,3]{3,1,2,0:T(8,128)(2,1)S(1)} %get-tuple-element.139), channel_id=1, source_target_pairs={{1,0},{2,1},{3,2},{5,4},{6,5},{7,6},{9,8},{10,9},{11,10},{13,12},{... | collective-permute-start | bytes 13832 | tf_op jit(solution)/shard_map/ppermute | solution.py:25
  20.9 3.4 %copy-start.14 = (s32[2,8,128]{2,1,0:T(8,128)S(1)}, s32[2,8,128]{2,1,0:T(8,128)}, u32[]{:S(2)}) copy-start(s32[2,8,128]{2,1,0:T(8,128)} %param.9) | copy-start | bytes 24580
  20.9 25.1 %copy-start.19 = (bf16[1600,12]{0,1:T(8,128)(2,1)S(1)}, bf16[1600,12]{0,1:T(8,128)(2,1)}, u32[]{:S(2)}) copy-start(bf16[1600,12]{0,1:T(8,128)(2,1)} %param.10) | copy-start | bytes 115204
  46.1 2.0 %copy-start.20 = (bf16[12,400]{1,0:T(8,128)(2,1)S(1)}, bf16[12,400]{1,0:T(8,128)(2,1)}, u32[]{:S(2)}) copy-start(bf16[12,400]{1,0:T(8,128)(2,1)} %param.13) | copy-start | bytes 28804
  87.3 33.0 %collective-permute-start.3 = (f32[12,8,3,128]{3,1,2,0:T(8,128)}, f32[12,8,3,128]{3,1,2,0:T(8,128)}, u32[]{:S(2)}, u32[]{:S(2)}) collective-permute-start(f32[12,8,3,128]{3,1,2,0:T(8,128)} %get-tuple-element.134), channel_id=1, source_target_pairs={{4,0},{8,4},{12,8},{5,1},{9,5},{13,9},{6,2},{10,6},{14,10},{7,3},{... | collective-permute-start | bytes 442376 | tf_op jit(solution)/shard_map/ppermute | solution.py:25
  95.9 1.4 copy-start.8
  102.0 0.7 copy-start.18
  102.8 1.4 copy-start.2
  119.7 1.8 copy-start.4
  119.7 1.8 copy-start.10
  119.8 1.8 copy-start.12
  124.3 1.1 copy-start.5
  124.3 1.2 copy-start.6
  124.3 1.3 copy-start.7
  (3 other events, 2.0 us)
where the time goes:
time: 189 us; the launch traced here: 188 us
  local copies, waits for them, and re-layouts  73.3 us (39%)
  other arithmetic  48.1 us (25%)
  blocking collectives  45.5 us (24%)
  starting transfers between devices  15.8 us (8%)
  matrix products  3.61 us (2%)
    psum x1, blocking collectives, body(): totals = lax.psum(partial_loads, ('gx', 'gy', 'gz'))  45.5 us
    gather x1, local copies, waits for them, and re-layouts, body(): gathered = rate_packed[:, jnp.where(react_flags == 1, slot_index, 0)]  29.4 us
    scatter x1, local copies, waits for them, and re-layouts, body(): jnp.zeros((COMPS, capacity), jnp.bfloat16).at[:, slot_index]  21.1 us
    scatter-add x1, other arithmetic, body(): jax.ops.segment_sum(push_values, panel_ids, num_segments=panels_all)  14.8 us
    div x3, other arithmetic, weno_face(): (weight_zero * cand_zero + weight_one * cand_one + weight_two * cand_two)...  12.6 us
    ppermute x3, starting transfers between devices, extended(): before = lax.ppermute(last, axis, up)  11.7 us
    slice x5, local copies, waits for them, and re-layouts, take_slab(): lax.slice_in_dim(array_in, begin_at, begin_at + length_of, axis=flux_axis)  4.32 us
    unnamed x46, local copies, waits for them, and re-layouts  4.23 us
  transfers between devices with their start and end apart: 6, of which 0 were waited for; matrix products, arithmetic and copies ran while one was open for 54% of the time, Pallas kernels for 0%

commit v1 on v0

v1 whole, which is shorter than its diff:
```python
import jax
import jax.numpy as jnp
from jax import lax
from jax.experimental import pallas as pl
from jax.experimental.pallas import tpu as pltpu
from jax.sharding import PartitionSpec as P

BAL = 64
COMPS = 12
PATCH = 8

HEAT_RATIO = 1.4
TIME_STEP = 0.1
CHEM_STEP = 0.25
WENO_EPS = 1e-06
EPS = WENO_EPS * 4.0 / 36.0
AXES = ("gx", "gy", "gz")
F32 = jnp.float32
BF16 = jnp.bfloat16
VM = pl.BlockSpec(memory_space=pltpu.VMEM)
SM = pl.BlockSpec(memory_space=pltpu.SMEM)


def weno_line(v):
    n = len(v)
    d = [(v[j + 1] - v[j]) * (1.0 / 6.0) for j in range(n - 1)]
    d3 = [3.0 * x for x in d]
    q = {}
    for e in range(1, n - 1):
        s = d[e] - d[e - 1]
        q[e] = (13.0 / 3.0) * (s * s) + EPS
    upper, lower = {}, {}
    for e in range(2, n - 2):
        dm, dp = d[e - 1], d[e]
        t0 = d3[e - 1] - d[e - 2]
        t1 = dm + dp
        t2 = d3[e] - d[e + 1]
        b0 = q[e - 1] + t0 * t0
        b1 = q[e] + t1 * t1
        b2 = q[e + 1] + t2 * t2
        m01, m02, m12 = b0 * b1, b0 * b2, b1 * b2
        s01, s02, s12 = m01 * m01, m02 * m02, m12 * m12
        w1, w01, w12 = 6.0 * s02, 3.0 * s01, 3.0 * s12
        if e < n - 3:
            num = s12 * (t0 + t0 - dm) + w1 * (t1 + dp) + w01 * (t2 + dp)
            upper[e] = v[e] + num / (s12 + w1 + w01)
        if e > 2:
            num = s01 * (t2 + t2 - dp) + w1 * (t1 + dm) + w12 * (t0 + dm)
            lower[e] = v[e] - num / (s01 + w1 + w12)
    return upper, lower


def weno_one(v):
    d = [(v[j + 1] - v[j]) * (1.0 / 6.0) for j in range(4)]
    s = [d[j + 1] - d[j] for j in range(3)]
    q = [(13.0 / 3.0) * (x * x) + EPS for x in s]
    dm, dp = d[1], d[2]
    t0, t1, t2 = 3.0 * dm - d[0], dm + dp, 3.0 * dp - d[3]
    b0, b1, b2 = q[0] + t0 * t0, q[1] + t1 * t1, q[2] + t2 * t2
    m01, m02, m12 = b0 * b1, b0 * b2, b1 * b2
    w0, w1, w2 = m12 * m12, 6.0 * (m02 * m02), 3.0 * (m01 * m01)
    num = w0 * (t0 + t0 - dm) + w1 * (t1 + dp) + w2 * (t2 + dp)
    return v[2] + num / (w0 + w1 + w2)


def hllc(left, right, normal):
    n = 1 + normal

    def side(x):
        rho = jnp.exp(x[0])
        g = jnp.exp(0.5 * (x[4] - x[0]))
        h = g * g
        return rho, h, rho * h, (HEAT_RATIO**0.5) * g, x[n]

    rho_l, h_l, p_l, c_l, u_l = side(left)
    rho_r, h_r, p_r, c_r, u_r = side(right)
    s_l = jnp.minimum(u_l - c_l, u_r - c_r)
    s_r = jnp.maximum(u_l + c_l, u_r + c_r)
    m_l = rho_l * (s_l - u_l)
    m_r = rho_r * (s_r - u_r)
    s = (p_r - p_l + u_l * m_l - u_r * m_r) / (m_l - m_r)
    use_l = (s >= 0) | (s_l >= 0)
    pick = [jnp.where(use_l, a, b) for a, b in zip(left, right)]
    rho = jnp.where(use_l, rho_l, rho_r)
    h = jnp.where(use_l, h_l, h_r)
    p = jnp.where(use_l, p_l, p_r)
    wave = jnp.where(use_l, s_l, s_r)
    act = jnp.where(use_l, jnp.minimum(s_l, 0.0), jnp.maximum(s_r, 0.0))
    u = pick[n]
    rel = s - u
    ratio = rel / (wave - s)
    mass = rho * (u + act * ratio)
    k = rho * act * (1.0 + ratio) * rel
    square = pick[1] * pick[1] + pick[2] * pick[2] + pick[3] * pick[3]
    enthalpy = (1.0 / (HEAT_RATIO - 1.0) + 1.0) * h + 0.5 * square
    flux = [mass * x for x in pick]
    flux[0] = mass
    flux[n] = flux[n] + (p + k)
    flux[4] = enthalpy * mass + k * s
    return flux


def rows8(index):
    return pl.ds(pl.multiple_of(index * 8, 8), 8)


def face_states(load_line, left_ref, right_ref, faces):
    def one(c, carry):
        upper, lower = weno_line(load_line(c))
        for f in range(faces):
            left_ref[rows8(c * faces + f), :] = upper[f + 2]
            right_ref[rows8(c * faces + f), :] = lower[f + 3]
        return carry

    lax.fori_loop(0, COMPS, one, 0)


def line_changes(left_ref, right_ref, faces, normal, emit):
    before = None
    for f in range(faces):
        left = [left_ref[pl.ds((c * faces + f) * 8, 8), :] for c in range(COMPS)]
        right = [right_ref[pl.ds((c * faces + f) * 8, 8), :] for c in range(COMPS)]
        flux = hllc(left, right, normal)
        if before is not None:
            for c in range(COMPS):
                emit(c, f - 1, flux[c] - before[c])
        before = flux


def half_lanes(shape):
    return lax.broadcasted_iota(jnp.int32, shape, 1) < 64


def swap_halves(x):
    return pltpu.roll(x, 64, 1)


def pack_kernel(pair_x, flags, f_ref, map_ref, r_ref, zt_ref, *refs):
    refs = list(refs)
    x_refs = [refs.pop(0) for _ in range(1 if pair_x else 2)]
    ylo_ref, yhi_ref, zlo_ref, zhi_ref, table_ref, buf = refs
    planes, ylen = 8, 8
    for x in range(planes):
        def at(c):
            return f_ref[pl.ds(c * 64 + x * 8, 8), :]

        rho = at(0)
        inv = 1.0 / rho
        u = [at(c) * inv for c in (1, 2, 3)]
        p = (HEAT_RATIO - 1.0) * (
            at(4) - 0.5 * rho * (u[0] * u[0] + u[1] * u[1] + u[2] * u[2])
        )
        out = [jnp.log(rho)] + u + [jnp.log(p)] + [at(c) * inv for c in range(5, COMPS)]
        for c in range(COMPS):
            r_ref[pl.ds(c * 64 + x * 8, 8), :] = out[c]
    for c in range(0, COMPS, 2):
        lo = jnp.concatenate([r_ref[pl.ds((c + i) * 64, 24), :] for i in (0, 1)], axis=0)
        hi = jnp.concatenate([r_ref[pl.ds((c + i) * 64 + 40, 24), :] for i in (0, 1)], axis=0)
        if pair_x:
            both = [jnp.where(flags[0] == 1, hi, lo)]
        else:
            both = [lo, hi]
        for ref, x in zip(x_refs, both):
            ref[pl.ds(c * 24, 48), :] = x.astype(BF16)
        def row(i, y):
            return r_ref[pl.ds((c + i) * 64 + y, 8, stride=8), :]

        ylo_ref[pl.ds(c * 24, 48), :] = jnp.concatenate(
            [row(i, y) for i in (0, 1) for y in range(3)], axis=0
        ).astype(BF16)
        yhi_ref[pl.ds(c * 24, 48), :] = jnp.concatenate(
            [row(i, y) for i in (0, 1) for y in range(ylen - 3, ylen)], axis=0
        ).astype(BF16)
    low = half_lanes((64, 128))
    for c in range(0, COMPS, 2):
        t = jnp.transpose(r_ref[pl.ds(c * 64, 128), :])
        top, bottom = t[:64], t[64:]
        even = jnp.where(low, top, swap_halves(bottom))
        odd = jnp.where(low, swap_halves(top), bottom)
        for i, x in ((0, even), (1, odd)):
            zt_ref[pl.ds((c + i) * 64, 64), :] = x
            zlo_ref[pl.ds((c + i) * 3, 3), :] = x[:3]
            zhi_ref[pl.ds((c + i) * 3, 3), :] = x[61:]
    pushes = []
    for wall in range(2):
        rows = (0, 1, 2) if wall == 0 else (ylen - 1, ylen - 2, ylen - 3)
        state = []
        for c in (0, 2, 4):
            a = [r_ref[pl.ds(c * 64 + y, 8, stride=8), :] for y in rows]
            sign = -1.0 if c == 2 else 1.0
            state.append(weno_one([a[2], a[1], a[0], sign * a[0], sign * a[1]]))
        rho = jnp.exp(state[0])
        p = jnp.exp(state[2])
        out_speed = -state[1] if wall == 0 else state[1]
        speed = jnp.abs(out_speed) + jnp.sqrt(HEAT_RATIO * p / rho)
        push = p + rho * out_speed * (out_speed + speed)
        x = jnp.where(flags[2 + wall] == 1, push, 0.0)
        for s in (1, 2, 4):
            x = x + pltpu.roll(x, 128 - s, 1)
        for s in (1, 2):
            x = x + pltpu.roll(x, 8 - s, 0)
        pushes.append(x)
    ids = map_ref[...].astype(F32)
    tall = jnp.concatenate(pushes + [ids, jnp.zeros((96, 128), F32)], axis=0)
    buf[...] = jnp.transpose(tall)
    groups = [buf[pl.ds(64 * g, 8, stride=8), :] for g in range(2)]
    lane = lax.broadcasted_iota(jnp.int32, (8, 128), 1).astype(F32)
    columns = []
    for g in groups:
        for col in (0, 4, 8, 12):
            columns.append(
                (
                    jnp.broadcast_to(g[:, col : col + 1], (8, 128)),
                    jnp.broadcast_to(g[:, 16 + col : 17 + col], (8, 128)),
                )
            )
    for j in range(table_ref.shape[0]):
        total = jnp.zeros((8, 128), F32)
        for load, panel in columns:
            total = total + jnp.where(panel == lane + 128.0 * j, load, 0.0)
        table_ref[pl.ds(j, 1), :] = jnp.sum(total, axis=0, keepdims=True)


def pack(fields, panels, flags, pair_x, table_rows):
    halo = jax.ShapeDtypeStruct((COMPS * 24, 128), BF16)
    edge = jax.ShapeDtypeStruct((COMPS * 3, 128), F32)
    whole = jax.ShapeDtypeStruct((COMPS * 64, 128), F32)
    outs = [whole, whole] + [halo] * (1 if pair_x else 2) + [halo, halo, edge, edge]
    outs.append(jax.ShapeDtypeStruct((table_rows, 128), F32))
    return pl.pallas_call(
        lambda *a: pack_kernel(pair_x, *a),
        out_shape=outs,
        in_specs=[SM, VM, VM],
        out_specs=[VM] * len(outs),
        scratch_shapes=[pltpu.VMEM((128, 128), F32)],
        name="pack",
    )(flags, fields, panels)


def chem_kernel(slots, r_ref, react_ref, w1_ref, w2_ref, w3_ref, w4_ref, out_ref):
    def dot(a, b):
        return jnp.dot(a, b, preferred_element_type=F32)

    def iota(shape, dim):
        return lax.broadcasted_iota(jnp.int32, shape, dim)

    def where1(mask):
        return jnp.where(mask, 1.0, 0.0).astype(BF16)

    react = react_ref[...].astype(F32)
    react_b = react.astype(BF16)
    upper = where1(iota((128, 128), 0) <= iota((128, 128), 1))
    within = dot(react_b, upper)
    count = dot(react_b, jnp.ones((128, 128), BF16))
    below = where1(iota((64, 64), 1) < iota((64, 64), 0))
    offset = dot(below, count.astype(BF16))
    rank = (react * (within + offset)).astype(BF16)
    slot_lane = iota((64, slots), 1).astype(F32)
    off_col, cnt_col = offset[:, :1], count[:, :1]
    row_slot = where1((slot_lane >= off_col) & (slot_lane < off_col + cnt_col))
    nt = (((1,), (1,)), ((), ()))
    count_row = lax.dot_general(
        jnp.ones((8, 128), BF16), react_b, nt, preferred_element_type=F32
    )
    offset_row = lax.dot_general(
        count_row.astype(BF16), below, nt, preferred_element_type=F32
    )
    slot_sub = iota((slots, 64), 0).astype(F32)
    slot_row = where1(
        (slot_sub >= offset_row[:1]) & (slot_sub < offset_row[:1] + count_row[:1])
    )
    lane_hit = dot(slot_row, rank) == iota((slots, 128), 0).astype(F32) + 1.0
    feat = jnp.zeros((slots, 128), F32)
    for c in range(COMPS):
        rows = dot(slot_row, r_ref[pl.ds(c * 64, 64), :].astype(BF16))
        hit = jnp.where(lane_hit, rows, 0.0).astype(BF16)
        feat = feat + dot(hit, where1(iota((128, 128), 1) == c))
    h = jnp.transpose(feat)[:COMPS].astype(BF16)
    for w_ref in (w1_ref, w2_ref, w3_ref):
        h = jax.nn.gelu(dot(w_ref[...], h)).astype(BF16)
    rates = dot(w4_ref[...], h)
    rates = jnp.concatenate([rates, jnp.zeros((128 - COMPS, slots), F32)], axis=0)
    rates_t = jnp.transpose(rates).astype(BF16)
    for c in range(COMPS):
        spread = dot(rates_t, where1(iota((128, 128), 0) == c))
        spread = jnp.where(lane_hit, spread, 0.0).astype(BF16)
        out_ref[pl.ds(c * 64, 64), :] = dot(row_slot, spread)


def chem(recon, react, layers, slots):
    return pl.pallas_call(
        lambda *a: chem_kernel(slots, *a),
        out_shape=jax.ShapeDtypeStruct(recon.shape, F32),
        in_specs=[VM] * 6,
        out_specs=VM,
        name="chem",
    )(recon, react, *layers)


def halo_lines(ref, scratch, own, sign_comp, at_wall, order):
    for c in range(0, COMPS, 2):
        block = ref[pl.ds(c * 24, 48), :].astype(F32)
        for i in (0, 1):
            for k in range(3):
                mirror = own(c + i, order[k])
                if c + i == sign_comp:
                    mirror = -mirror
                got = block[(i * 3 + k) * 8 : (i * 3 + k + 1) * 8]
                scratch[pl.ds(((c + i) * 3 + k) * 8, 8), :] = jnp.where(at_wall, mirror, got)


def flux_x_kernel(flags, r_ref, lo_ref, hi_ref, out_ref, lo_s, hi_s, left, right):
    def own(c, x):
        return r_ref[pl.ds(c * 64 + x * 8, 8), :]

    halo_lines(lo_ref, lo_s, own, 1, flags[0] == 1, (2, 1, 0))
    halo_lines(hi_ref, hi_s, own, 1, flags[1] == 1, (7, 6, 5))

    def line(c):
        return (
            [lo_s[rows8(c * 3 + k), :] for k in range(3)]
            + [r_ref[rows8(c * 8 + x), :] for x in range(8)]
            + [hi_s[rows8(c * 3 + k), :] for k in range(3)]
        )

    face_states(line, left, right, 9)

    def emit(c, x, change):
        out_ref[pl.ds(c * 64 + x * 8, 8), :] = change

    line_changes(left, right, 9, 0, emit)


def flux_y_kernel(flags, r_ref, lo_ref, hi_ref, acc_ref, out_ref, lo_s, hi_s, left, right):
    def own(c, y):
        return r_ref[pl.ds(c * 64 + y, 8, stride=8), :]

    halo_lines(lo_ref, lo_s, own, 2, flags[2] == 1, (2, 1, 0))
    halo_lines(hi_ref, hi_s, own, 2, flags[3] == 1, (7, 6, 5))

    def line(c):
        return (
            [lo_s[rows8(c * 3 + k), :] for k in range(3)]
            + [r_ref[pl.ds(c * 64 + y, 8, stride=8), :] for y in range(8)]
            + [hi_s[rows8(c * 3 + k), :] for k in range(3)]
        )

    face_states(line, left, right, 9)

    def emit(c, y, change):
        at = pl.ds(c * 64 + y, 8, stride=8)
        out_ref[at, :] = acc_ref[at, :] + change

    line_changes(left, right, 9, 1, emit)


def flux_z_kernel(
    flags, f_ref, zt_ref, lo_ref, hi_ref, acc_ref, src_ref, out_ref, ext, left, right, back
):
    low3, low = half_lanes((3, 128)), half_lanes((64, 128))
    for c in range(COMPS):
        sign = -1.0 if c == 3 else 1.0
        own = zt_ref[pl.ds(c * 64, 64), :]
        first, last = own[:3], own[61:]
        mirror_lo = sign * jnp.concatenate([first[2:3], first[1:2], first[0:1]], axis=0)
        mirror_hi = sign * jnp.concatenate([last[2:3], last[1:2], last[0:1]], axis=0)
        below = jnp.where(flags[4] == 1, mirror_lo, swap_halves(lo_ref[pl.ds(c * 3, 3), :]))
        above = jnp.where(flags[5] == 1, mirror_hi, swap_halves(hi_ref[pl.ds(c * 3, 3), :]))
        ext[pl.ds(c * 72, 3), :] = jnp.where(low3, below, swap_halves(last))
        ext[pl.ds(c * 72 + 3, 64), :] = own
        ext[pl.ds(c * 72 + 67, 3), :] = jnp.where(low3, swap_halves(first), above)

    def line(c):
        return [ext[pl.ds(c * 72 + e, 8, stride=8), :] for e in range(14)]

    face_states(line, left, right, 9)

    def emit(c, z, change):
        back[pl.ds(c * 64 + z, 8, stride=8), :] = change

    line_changes(left, right, 9, 2, emit)
    for c in range(0, COMPS, 2):
        even, odd = back[pl.ds(c * 64, 64), :], back[pl.ds(c * 64 + 64, 64), :]
        t = jnp.concatenate(
            [jnp.where(low, even, swap_halves(odd)), jnp.where(low, swap_halves(even), odd)],
            axis=0,
        )
        at = pl.ds(c * 64, 128)
        change = acc_ref[at, :] + jnp.transpose(t)
        out_ref[at, :] = f_ref[at, :] - TIME_STEP * change + CHEM_STEP * src_ref[at, :]


def state_scratch():
    return [pltpu.VMEM((COMPS * 9 * 8, 128), F32)] * 2


def halo_scratch():
    return [pltpu.VMEM((COMPS * 24, 128), F32)] * 2


def flux_x(flags, recon, lo, hi):
    return pl.pallas_call(
        flux_x_kernel,
        out_shape=jax.ShapeDtypeStruct(recon.shape, F32),
        in_specs=[SM] + [VM] * 3,
        out_specs=VM,
        scratch_shapes=halo_scratch() + state_scratch(),
        name="flux_x",
    )(flags, recon, lo, hi)


def flux_y(flags, recon, lo, hi, acc):
    return pl.pallas_call(
        flux_y_kernel,
        out_shape=jax.ShapeDtypeStruct(recon.shape, F32),
        in_specs=[SM] + [VM] * 4,
        out_specs=VM,
        scratch_shapes=halo_scratch() + state_scratch(),
        name="flux_y",
    )(flags, recon, lo, hi, acc)


def flux_z(flags, fields, turned, lo, hi, acc, source):
    return pl.pallas_call(
        flux_z_kernel,
        out_shape=jax.ShapeDtypeStruct(fields.shape, F32),
        in_specs=[SM] + [VM] * 6,
        out_specs=VM,
        scratch_shapes=[pltpu.VMEM((COMPS * 72, 128), F32)]
        + state_scratch()
        + [pltpu.VMEM(fields.shape, F32)],
        name="flux_z",
    )(flags, fields, turned, lo, hi, acc, source)


def sum_over(table, axis):
    size = lax.axis_size(axis)
    if size & (size - 1):
        return lax.psum(table, axis)
    step = 1
    while step < size:
        table = table + lax.ppermute(table, axis, [(i, i ^ step) for i in range(size)])
        step *= 2
    return table


def body(fields, reacting, panel_map, layer_one, layer_two, layer_three, layer_four):
    shape = fields.shape
    sizes = [lax.axis_size(a) for a in AXES]
    index = [lax.axis_index(a) for a in AXES]
    flags = jnp.stack(
        [f.astype(jnp.int32) for i, n in zip(index, sizes) for f in (i == 0, i == n - 1)]
    )
    pair_x = sizes[0] == 2
    panels_all = 2 * (shape[1] * sizes[0] // PATCH) * (shape[3] * sizes[2] // PATCH)
    flat = fields.reshape(-1, shape[3])
    packed = pack(flat, panel_map.reshape(-1, shape[3]), flags, pair_x, panels_all // 128)
    recon, turned = packed[:2]
    y_lo, y_hi, z_lo, z_hi, table = packed[-5:]

    def move(x, axis, up):
        n = lax.axis_size(axis)
        pairs = [(i, i + 1) if up else (i + 1, i) for i in range(n - 1)]
        return lax.ppermute(x, axis, pairs)

    if pair_x:
        x_below = x_above = lax.ppermute(packed[2], "gx", [(0, 1), (1, 0)])
    else:
        x_below, x_above = move(packed[3], "gx", True), move(packed[2], "gx", False)
    y_below, y_above = move(y_hi, "gy", True), move(y_lo, "gy", False)
    z_below, z_above = move(z_hi, "gz", True), move(z_lo, "gz", False)
    layers = (layer_one, layer_two, layer_three, layer_four)
    slots = BAL * min(4, sizes[0])
    source = chem(recon, reacting.reshape(-1, shape[3]), layers, slots)
    acc = flux_x(flags, recon, x_below, x_above)
    acc = flux_y(flags, recon, y_below, y_above, acc)
    new = flux_z(flags, flat, turned, z_below, z_above, acc, source)
    for axis in ("gx", "gz", "gy"):
        table = sum_over(table, axis)
    own = panels_all // (sizes[0] * sizes[1] * sizes[2])
    place = (index[0] * sizes[1] + index[1]) * sizes[2] + index[2]
    result = lax.dynamic_slice_in_dim(table.reshape(-1), place * own, own)
    return new.reshape(shape), result / float(PATCH * PATCH)


def solution(mesh):
    return jax.shard_map(
        body,
        mesh=mesh,
        in_specs=(
            P(None, "gx", "gy", "gz"),
            P("gx", "gy", "gz"),
            P(None, "gx", "gz"),
            P(),
            P(),
            P(),
            P(),
        ),
        out_specs=(P(None, "gx", "gy", "gz"), P(("gx", "gy", "gz"))),
        check_vma=False,
    )
```

time: 189 us -> 53.6 us (0.28)
  the two profiles are of different devices: /device:TPU:0 before, /device:TPU:1 now
where the time goes in v1:
time: 53.6 us; the launch traced here: 53.3 us
  starting transfers between devices  23.5 us (44%)
  Pallas kernels  20.1 us (38%)
  local copies, waits for them, and re-layouts  4.38 us (8%)
  waiting for transfers between devices  2.82 us (5%)
  other arithmetic  1.78 us (3%)
  between operations  0.73 us (1%)
    ppermute x5, starting transfers between devices, sum_over(): lax.ppermute(table, axis, [(i, i ^ step) for i in range(size)])  11.6 us
    ppermute x4, starting transfers between devices, move(): return lax.ppermute(x, axis, pairs)  10.6 us
    pallas_call x1, Pallas kernels, chem(): pl.pallas_call(lambda *a: chem_kernel(slots, *a), out_shape=jax.ShapeDtyp...  7.65 us
    unnamed x13, local copies, waits for them, and re-layouts  4.27 us
    pallas_call x1, Pallas kernels, flux_z(): pl.pallas_call(flux_z_kernel, out_shape=jax.ShapeDtypeStruct(fields.shape...  3.66 us
    pallas_call x1, Pallas kernels, flux_y(): pl.pallas_call(flux_y_kernel, out_shape=jax.ShapeDtypeStruct(recon.shape,...  3.3 us
    pallas_call x1, Pallas kernels, flux_x(): pl.pallas_call(flux_x_kernel, out_shape=jax.ShapeDtypeStruct(recon.shape,...  2.94 us
    ppermute x5, waiting for transfers between devices, sum_over(): lax.ppermute(table, axis, [(i, i ^ step) for i in range(size)])  2.81 us
  transfers between devices with their start and end apart: 10, of which 3 were waited for; matrix products, arithmetic and copies ran while one was open for 4% of the time, Pallas kernels for 26%

profile of v1, /device:TPU:1, one launch (start us, length us, event | category | flops | bytes accessed | tf_op | source)
XLA Modules:
  0.0 53.3 jit_solution(16351475487009564490)
XLA Ops:
  1.3 2.5 %pack.1 = (f32[768,128]{1,0:T(8,128)}, f32[768,128]{1,0:T(8,128)}, bf16[288,128]{1,0:T(8,128)(2,1)}, bf16[288,128]{1,0:T(8,128)(2,1)}, bf16[288,128]{1,0:T(8,128...) custom-call(s32[6]{0:T(128)} %stack.36.a_0_.flags, f32[768,128]{1,0:T(8,128)} %bitcast.12, ...), custom_call_target="tpu_custom_call" | custom-call | tf_op jit(solution)/shard_map/pack/pallas_call | solution.py:230
  3.8 2.1 %collective-permute-start.5 = (f32[2,128]{1,0:T(2,128)}, f32[2,128]{1,0:T(2,128)S(1)}, u32[]{:S(2)}, u32[]{:S(2)}) collective-permute-start(f32[2,128]{1,0:T(2,128)} %get-tuple-element.17), channel_id=1, source_target_pairs={{0,16},{16,0},{1,17},{17,1},{2,18},{18,2},{3,19},{19,3},{4,20},{20... | collective-permute-start | bytes 3080 | tf_op jit(solution)/shard_map/ppermute | solution.py:442
  5.9 1.0 %collective-permute-done.5 = f32[2,128]{1,0:T(2,128)S(1)} collective-permute-done((f32[2,128]{1,0:T(2,128)}, f32[2,128]{1,0:T(2,128)S(1)}, u32[]{:S(2)}, u32[]{:S(2)}) %collective-permute-start.5) | collective-permute-done | bytes 1056 | tf_op jit(solution)/shard_map/ppermute | solution.py:442
  6.9 0.6 %add.24 = f32[2,128]{1,0:T(2,128)S(1)} add(f32[2,128]{1,0:T(2,128)} %get-tuple-element.17, f32[2,128]{1,0:T(2,128)S(1)} %collective-permute-done.5) | non-fusion elementwise | flops 256 | bytes 3072 | tf_op jit(solution)/shard_map/add | solution.py:442
  7.6 1.7 %collective-permute-start.6 = (f32[2,128]{1,0:T(2,128)S(1)}, f32[2,128]{1,0:T(2,128)S(1)}, u32[]{:S(2)}, u32[]{:S(2)}) collective-permute-start(f32[2,128]{1,0:T(2,128)S(1)} %add.24), channel_id=1, source_target_pairs={{0,1},{1,0},{2,3},{3,2},{4,5},{5,4},{6,7},{7,6},{8,9},{9,8},{10,11... | collective-permute-start | bytes 3080 | tf_op jit(solution)/shard_map/ppermute | solution.py:442
  9.3 0.8 %collective-permute-done.6 = f32[2,128]{1,0:T(2,128)S(1)} collective-permute-done((f32[2,128]{1,0:T(2,128)S(1)}, f32[2,128]{1,0:T(2,128)S(1)}, u32[]{:S(2)}, u32[]{:S(2)}) %collective-permute-start.6) | collective-permute-done | bytes 1056 | tf_op jit(solution)/shard_map/ppermute | solution.py:442
  10.1 1.8 %collective-permute-start.7 = (f32[2,128]{1,0:T(2,128)S(1)}, f32[2,128]{1,0:T(2,128)S(1)}, u32[]{:S(2)}, u32[]{:S(2)}) collective-permute-start(f32[2,128]{1,0:T(2,128)S(1)} %add.25), channel_id=1, source_target_pairs={{0,2},{1,3},{2,0},{3,1},{4,6},{5,7},{6,4},{7,5},{8,10},{9,11},{10,... | collective-permute-start | bytes 3080 | tf_op jit(solution)/shard_map/ppermute | solution.py:442
  11.8 1.0 %collective-permute-done.7 = f32[2,128]{1,0:T(2,128)S(1)} collective-permute-done((f32[2,128]{1,0:T(2,128)S(1)}, f32[2,128]{1,0:T(2,128)S(1)}, u32[]{:S(2)}, u32[]{:S(2)}) %collective-permute-start.7) | collective-permute-done | bytes 1056 | tf_op jit(solution)/shard_map/ppermute | solution.py:442
  12.8 1.5 %collective-permute-start.8 = (f32[2,128]{1,0:T(2,128)S(1)}, f32[2,128]{1,0:T(2,128)S(1)}, u32[]{:S(2)}, u32[]{:S(2)}) collective-permute-start(f32[2,128]{1,0:T(2,128)S(1)} %add.26), channel_id=1, source_target_pairs={{0,4},{4,0},{8,12},{12,8},{1,5},{5,1},{9,13},{13,9},{2,6},{6,2},{1... | collective-permute-start | bytes 3080 | tf_op jit(solution)/shard_map/ppermute | solution.py:442
  14.3 1.2 %collective-permute-start.4 = (bf16[288,128]{1,0:T(8,128)(2,1)}, bf16[288,128]{1,0:T(8,128)(2,1)S(1)}, u32[]{:S(2)}, u32[]{:S(2)}) collective-permute-start(bf16[288,128]{1,0:T(8,128)(2,1)} %get-tuple-element.16), channel_id=1, source_target_pairs={{0,16},{16,0},{1,17},{17,1},{2,18},{18,2},{3,19},{19,3},{4,20},{20... | collective-permute-start | bytes 221192 | tf_op jit(solution)/shard_map/ppermute | solution.py:467
  15.5 2.1 %collective-permute-start.2 = (bf16[288,128]{1,0:T(8,128)(2,1)}, bf16[288,128]{1,0:T(8,128)(2,1)S(1)}, u32[]{:S(2)}, u32[]{:S(2)}) collective-permute-start(bf16[288,128]{1,0:T(8,128)(2,1)} %get-tuple-element.14), channel_id=1, source_target_pairs={{0,4},{4,8},{8,12},{1,5},{5,9},{9,13},{2,6},{6,10},{10,14},{3,7},{... | collective-permute-start | bytes 221192 | tf_op jit(solution)/shard_map/ppermute | solution.py:464
  17.6 1.3 %collective-permute-start.3 = (bf16[288,128]{1,0:T(8,128)(2,1)}, bf16[288,128]{1,0:T(8,128)(2,1)S(1)}, u32[]{:S(2)}, u32[]{:S(2)}) collective-permute-start(bf16[288,128]{1,0:T(8,128)(2,1)} %get-tuple-element.15), channel_id=1, source_target_pairs={{4,0},{8,4},{12,8},{5,1},{9,5},{13,9},{6,2},{10,6},{14,10},{7,3},{... | collective-permute-start | bytes 221192 | tf_op jit(solution)/shard_map/ppermute | solution.py:464
  18.9 5.4 %collective-permute-start = (f32[36,128]{1,0:T(8,128)}, f32[36,128]{1,0:T(8,128)S(1)}, u32[]{:S(2)}, u32[]{:S(2)}) collective-permute-start(f32[36,128]{1,0:T(8,128)} %get-tuple-element.11), channel_id=1, source_target_pairs={{0,1},{1,2},{2,3},{4,5},{5,6},{6,7},{8,9},{9,10},{10,11},{12,13},{... | collective-permute-start | bytes 55304 | tf_op jit(solution)/shard_map/ppermute | solution.py:464
  24.3 4.6 %collective-permute-start.9 = (f32[2,128]{1,0:T(2,128)S(1)}, f32[2,128]{1,0:T(2,128)S(1)}, u32[]{:S(2)}, u32[]{:S(2)}) collective-permute-start(f32[2,128]{1,0:T(2,128)S(1)} %add.27), channel_id=1, source_target_pairs={{0,8},{4,12},{8,0},{12,4},{1,9},{5,13},{9,1},{13,5},{2,10},{6,14},... | collective-permute-start | bytes 3080 | tf_op jit(solution)/shard_map/ppermute | solution.py:442
  28.9 1.8 %copy.9.a_2_ = bf16[1600,12]{1,0:T(8,128)(2,1)} copy(bf16[1600,12]{0,1:T(8,128)(2,1)} %param.10) | data formatting | bytes 76800 | tf_op args[3]
  30.7 7.7 %chem.1.src_ref = f32[768,128]{1,0:T(8,128)} custom-call(f32[768,128]{1,0:T(8,128)} %get-tuple-element.13.r_ref.a_0_, s32[64,128]{1,0:T(8,128)} %bitcast.15, bf16[1600,12]{1,0:T(8,128)(2,1)} %copy.9.a_2_, bf16[800,1600]{1,0:T(8,128)(2,1)} %a_3_.1, bf16[400,800]{1,0:T(8,128)(2,1)} %a_4_.1, bf16[12,400]{1,0:T(8,128)(2,1)} %a_5_.1), custom_call_target="tpu_custom_call" | custom-call | tf_op jit(solution)/shard_map/chem/pallas_call | solution.py:291
  38.3 1.9 %collective-permute-start.1 = (f32[36,128]{1,0:T(8,128)S(1)}, f32[36,128]{1,0:T(8,128)S(1)}, u32[]{:S(2)}, u32[]{:S(2)}) collective-permute-start(f32[36,128]{1,0:T(8,128)S(1)} %copy-done.5), channel_id=1, source_target_pairs={{1,0},{2,1},{3,2},{5,4},{6,5},{7,6},{9,8},{10,9},{11,10},{13,12},{... | collective-permute-start | bytes 55304 | tf_op jit(solution)/shard_map/ppermute | solution.py:464
  40.3 0.6 %dynamic-slice_multiply_fusion = f32[8]{0:T(128)} fusion(f32[256]{0:T(256)S(1)} %add_bitcast_fusion, s32[]{:T(128)S(6)} %select_n.3), kind=kLoop, calls=%fused_computation.1 | loop fusion | flops 8 | bytes 68 | tf_op jit(solution)/shard_map/div | solution.py:483
  40.9 0.6 %copy-done = bf16[288,128]{1,0:T(8,128)(2,1)} copy-done((bf16[288,128]{1,0:T(8,128)(2,1)}, bf16[288,128]{1,0:T(8,128)(2,1)S(1)}, u32[]{:S(2)}) %copy-start) | copy-done | bytes 73752
  41.5 2.9 %flux_x.1.acc_ref = f32[768,128]{1,0:T(8,128)} custom-call(s32[6]{0:T(128)} %stack.36.a_0_.flags, f32[768,128]{1,0:T(8,128)} %get-tuple-element.13.r_ref.a_0_, bf16[288,128]{1,0:T(8,128)(2,1)} %copy-done, bf16[288,128]{1,0:T(8,128)(2,1)} %copy-done), custom_call_target="tpu_custom_call" | custom-call | tf_op jit(solution)/shard_map/flux_x/pallas_call | solution.py:402
  44.4 0.6 %copy-done.1 = bf16[288,128]{1,0:T(8,128)(2,1)} copy-done((bf16[288,128]{1,0:T(8,128)(2,1)}, bf16[288,128]{1,0:T(8,128)(2,1)S(1)}, u32[]{:S(2)}) %copy-start.1) | copy-done | bytes 73752
  45.1 0.6 %copy-done.2 = bf16[288,128]{1,0:T(8,128)(2,1)} copy-done((bf16[288,128]{1,0:T(8,128)(2,1)}, bf16[288,128]{1,0:T(8,128)(2,1)S(1)}, u32[]{:S(2)}) %copy-start.2) | copy-done | bytes 73752
  45.7 3.3 %flux_y.1.acc_ref = f32[768,128]{1,0:T(8,128)} custom-call(s32[6]{0:T(128)} %stack.36.a_0_.flags, f32[768,128]{1,0:T(8,128)} %get-tuple-element.13.r_ref.a_0_, bf16[288,128]{1,0:T(8,128)(2,1)} %copy-done.1, bf16[288,128]{1,0:T(8,128)(2,1)} %copy-done.2, f32[768,128]{1,0:T(8,128)} %flux_x.1.acc_ref), custom_call_target="tpu_custom_call" | custom-call | tf_op jit(solution)/shard_map/flux_y/pallas_call | solution.py:413
  49.6 3.7 %flux_z.1 = f32[768,128]{1,0:T(8,128)} custom-call(s32[6]{0:T(128)} %stack.36.a_0_.flags, f32[768,128]{1,0:T(8,128)} %bitcast.13, f32[768,128]{1,0:T(8,128)} %get-tuple-element.10.zt_ref, f32[36,128]{1,0:T(8,128)} %copy-done.3, f32[36,128]{1,0:T(8,128)} %copy-done.4, f32[768,128]{1,0:T(8,128)} %flux_y.1.acc_ref, f32[768,128]{1,0:T(8,128)} %chem.1.src_ref), custom_call_target="tpu_custom_call" | custom-call | tf_op jit(solution)/shard_map/flux_z/pallas_call | solution.py:424
  (22 shorter events, 1.3 us)
Async XLA Ops:
  3.8 34.5 %copy-start.5 = (f32[36,128]{1,0:T(8,128)S(1)}, f32[36,128]{1,0:T(8,128)}, u32[]{:S(2)}) copy-start(f32[36,128]{1,0:T(8,128)} %get-tuple-element.12) | copy-start | bytes 55300
  3.8 3.1 %collective-permute-start.5 = (f32[2,128]{1,0:T(2,128)}, f32[2,128]{1,0:T(2,128)S(1)}, u32[]{:S(2)}, u32[]{:S(2)}) collective-permute-start(f32[2,128]{1,0:T(2,128)} %get-tuple-element.17), channel_id=1, source_target_pairs={{0,16},{16,0},{1,17},{17,1},{2,18},{18,2},{3,19},{19,3},{4,20},{20... | collective-permute-start | bytes 3080 | tf_op jit(solution)/shard_map/ppermute | solution.py:442
  7.6 2.5 %collective-permute-start.6 = (f32[2,128]{1,0:T(2,128)S(1)}, f32[2,128]{1,0:T(2,128)S(1)}, u32[]{:S(2)}, u32[]{:S(2)}) collective-permute-start(f32[2,128]{1,0:T(2,128)S(1)} %add.24), channel_id=1, source_target_pairs={{0,1},{1,0},{2,3},{3,2},{4,5},{5,4},{6,7},{7,6},{8,9},{9,8},{10,11... | collective-permute-start | bytes 3080 | tf_op jit(solution)/shard_map/ppermute | solution.py:442
  10.1 2.7 %collective-permute-start.7 = (f32[2,128]{1,0:T(2,128)S(1)}, f32[2,128]{1,0:T(2,128)S(1)}, u32[]{:S(2)}, u32[]{:S(2)}) collective-permute-start(f32[2,128]{1,0:T(2,128)S(1)} %add.25), channel_id=1, source_target_pairs={{0,2},{1,3},{2,0},{3,1},{4,6},{5,7},{6,4},{7,5},{8,10},{9,11},{10,... | collective-permute-start | bytes 3080 | tf_op jit(solution)/shard_map/ppermute | solution.py:442
  12.8 11.5 %collective-permute-start.8 = (f32[2,128]{1,0:T(2,128)S(1)}, f32[2,128]{1,0:T(2,128)S(1)}, u32[]{:S(2)}, u32[]{:S(2)}) collective-permute-start(f32[2,128]{1,0:T(2,128)S(1)} %add.26), channel_id=1, source_target_pairs={{0,4},{4,0},{8,12},{12,8},{1,5},{5,1},{9,13},{13,9},{2,6},{6,2},{1... | collective-permute-start | bytes 3080 | tf_op jit(solution)/shard_map/ppermute | solution.py:442
  14.3 26.5 %collective-permute-start.4 = (bf16[288,128]{1,0:T(8,128)(2,1)}, bf16[288,128]{1,0:T(8,128)(2,1)S(1)}, u32[]{:S(2)}, u32[]{:S(2)}) collective-permute-start(bf16[288,128]{1,0:T(8,128)(2,1)} %get-tuple-element.16), channel_id=1, source_target_pairs={{0,16},{16,0},{1,17},{17,1},{2,18},{18,2},{3,19},{19,3},{4,20},{20... | collective-permute-start | bytes 221192 | tf_op jit(solution)/shard_map/ppermute | solution.py:467
  15.5 28.9 %collective-permute-start.2 = (bf16[288,128]{1,0:T(8,128)(2,1)}, bf16[288,128]{1,0:T(8,128)(2,1)S(1)}, u32[]{:S(2)}, u32[]{:S(2)}) collective-permute-start(bf16[288,128]{1,0:T(8,128)(2,1)} %get-tuple-element.14), channel_id=1, source_target_pairs={{0,4},{4,8},{8,12},{1,5},{5,9},{9,13},{2,6},{6,10},{10,14},{3,7},{... | collective-permute-start | bytes 221192 | tf_op jit(solution)/shard_map/ppermute | solution.py:464
  17.6 26.8 %collective-permute-start.3 = (bf16[288,128]{1,0:T(8,128)(2,1)}, bf16[288,128]{1,0:T(8,128)(2,1)S(1)}, u32[]{:S(2)}, u32[]{:S(2)}) collective-permute-start(bf16[288,128]{1,0:T(8,128)(2,1)} %get-tuple-element.15), channel_id=1, source_target_pairs={{4,0},{8,4},{12,8},{5,1},{9,5},{13,9},{6,2},{10,6},{14,10},{7,3},{... | collective-permute-start | bytes 221192 | tf_op jit(solution)/shard_map/ppermute | solution.py:464
  18.9 30.1 %collective-permute-start = (f32[36,128]{1,0:T(8,128)}, f32[36,128]{1,0:T(8,128)S(1)}, u32[]{:S(2)}, u32[]{:S(2)}) collective-permute-start(f32[36,128]{1,0:T(8,128)} %get-tuple-element.11), channel_id=1, source_target_pairs={{0,1},{1,2},{2,3},{4,5},{5,6},{6,7},{8,9},{9,10},{10,11},{12,13},{... | collective-permute-start | bytes 55304 | tf_op jit(solution)/shard_map/ppermute | solution.py:464
  24.3 14.0 %collective-permute-start.9 = (f32[2,128]{1,0:T(2,128)S(1)}, f32[2,128]{1,0:T(2,128)S(1)}, u32[]{:S(2)}, u32[]{:S(2)}) collective-permute-start(f32[2,128]{1,0:T(2,128)S(1)} %add.27), channel_id=1, source_target_pairs={{0,8},{4,12},{8,0},{12,4},{1,9},{5,13},{9,1},{13,5},{2,10},{6,14},... | collective-permute-start | bytes 3080 | tf_op jit(solution)/shard_map/ppermute | solution.py:442
  38.3 10.7 %collective-permute-start.1 = (f32[36,128]{1,0:T(8,128)S(1)}, f32[36,128]{1,0:T(8,128)S(1)}, u32[]{:S(2)}, u32[]{:S(2)}) collective-permute-start(f32[36,128]{1,0:T(8,128)S(1)} %copy-done.5), channel_id=1, source_target_pairs={{1,0},{2,1},{3,2},{5,4},{6,5},{7,6},{9,8},{10,9},{11,10},{13,12},{... | collective-permute-start | bytes 55304 | tf_op jit(solution)/shard_map/ppermute | solution.py:464
  40.9 0.6 %copy-start = (bf16[288,128]{1,0:T(8,128)(2,1)}, bf16[288,128]{1,0:T(8,128)(2,1)S(1)}, u32[]{:S(2)}) copy-start(bf16[288,128]{1,0:T(8,128)(2,1)S(1)} %collective-permute-done.4.lo_ref.hi_ref) | copy-start | bytes 221188
  44.4 0.6 %copy-start.1 = (bf16[288,128]{1,0:T(8,128)(2,1)}, bf16[288,128]{1,0:T(8,128)(2,1)S(1)}, u32[]{:S(2)}) copy-start(bf16[288,128]{1,0:T(8,128)(2,1)S(1)} %collective-permute-done.2.lo_ref) | copy-start | bytes 221188
  45.1 0.6 %copy-start.2 = (bf16[288,128]{1,0:T(8,128)(2,1)}, bf16[288,128]{1,0:T(8,128)(2,1)S(1)}, u32[]{:S(2)}) copy-start(bf16[288,128]{1,0:T(8,128)(2,1)S(1)} %collective-permute-done.3.hi_ref) | copy-start | bytes 221188
  49.0 0.6 %copy-start.3 = (f32[36,128]{1,0:T(8,128)}, f32[36,128]{1,0:T(8,128)S(1)}, u32[]{:S(2)}) copy-start(f32[36,128]{1,0:T(8,128)S(1)} %collective-permute-done.lo_ref) | copy-start | bytes 55300
  49.0 0.6 %copy-start.4 = (f32[36,128]{1,0:T(8,128)}, f32[36,128]{1,0:T(8,128)S(1)}, u32[]{:S(2)}) copy-start(f32[36,128]{1,0:T(8,128)S(1)} %collective-permute-done.1.hi_ref) | copy-start | bytes 55300

commit v2 on v1

--- a/solution.py
+++ b/solution.py
@@ -17,8 +17,10 @@
 AXES = ("gx", "gy", "gz")
 F32 = jnp.float32
 BF16 = jnp.bfloat16
+GRANT = pltpu.CompilerParams(vmem_limit_bytes=12 * 2**20)
 VM = pl.BlockSpec(memory_space=pltpu.VMEM)
 SM = pl.BlockSpec(memory_space=pltpu.SMEM)
+ANY = pl.BlockSpec(memory_space=pl.ANY)
 
 
 def weno_line(v):
@@ -135,12 +137,23 @@
     return pltpu.roll(x, 64, 1)
 
 
-def pack_kernel(pair_x, flags, f_ref, map_ref, r_ref, zt_ref, *refs):
-    refs = list(refs)
-    x_refs = [refs.pop(0) for _ in range(1 if pair_x else 2)]
-    ylo_ref, yhi_ref, zlo_ref, zhi_ref, table_ref, buf = refs
-    planes, ylen = 8, 8
-    for x in range(planes):
+def split3(x):
+    hi = x.astype(BF16).astype(F32)
+    mid = (x - hi).astype(BF16).astype(F32)
+    return hi, mid, x - hi - mid
+
+
+def pack_kernel(pair_x, flags, f_hbm, map_hbm, r_ref, zt_ref, *refs):
+    x_refs, refs = refs[:2 - pair_x], refs[2 - pair_x :]
+    y_refs, z_refs, table_ref, buf, f_ref, map_ref, sems = refs[:2], refs[2:4], *refs[4:]
+    copies = [
+        pltpu.make_async_copy(f_hbm, f_ref, sems.at[0]),
+        pltpu.make_async_copy(map_hbm, map_ref, sems.at[1]),
+    ]
+    for copy in copies:
+        copy.start()
+    copies[0].wait()
+    for x in range(8):
         def at(c):
             return f_ref[pl.ds(c * 64 + x * 8, 8), :]
 
@@ -153,37 +166,9 @@
         out = [jnp.log(rho)] + u + [jnp.log(p)] + [at(c) * inv for c in range(5, COMPS)]
         for c in range(COMPS):
             r_ref[pl.ds(c * 64 + x * 8, 8), :] = out[c]
-    for c in range(0, COMPS, 2):
-        lo = jnp.concatenate([r_ref[pl.ds((c + i) * 64, 24), :] for i in (0, 1)], axis=0)
-        hi = jnp.concatenate([r_ref[pl.ds((c + i) * 64 + 40, 24), :] for i in (0, 1)], axis=0)
-        if pair_x:
-            both = [jnp.where(flags[0] == 1, hi, lo)]
-        else:
-            both = [lo, hi]
-        for ref, x in zip(x_refs, both):
-            ref[pl.ds(c * 24, 48), :] = x.astype(BF16)
-        def row(i, y):
-            return r_ref[pl.ds((c + i) * 64 + y, 8, stride=8), :]
-
-        ylo_ref[pl.ds(c * 24, 48), :] = jnp.concatenate(
-            [row(i, y) for i in (0, 1) for y in range(3)], axis=0
-        ).astype(BF16)
-        yhi_ref[pl.ds(c * 24, 48), :] = jnp.concatenate(
-            [row(i, y) for i in (0, 1) for y in range(ylen - 3, ylen)], axis=0
-        ).astype(BF16)
-    low = half_lanes((64, 128))
-    for c in range(0, COMPS, 2):
-        t = jnp.transpose(r_ref[pl.ds(c * 64, 128), :])
-        top, bottom = t[:64], t[64:]
-        even = jnp.where(low, top, swap_halves(bottom))
-        odd = jnp.where(low, swap_halves(top), bottom)
-        for i, x in ((0, even), (1, odd)):
-            zt_ref[pl.ds((c + i) * 64, 64), :] = x
-            zlo_ref[pl.ds((c + i) * 3, 3), :] = x[:3]
-            zhi_ref[pl.ds((c + i) * 3, 3), :] = x[61:]
     pushes = []
     for wall in range(2):
-        rows = (0, 1, 2) if wall == 0 else (ylen - 1, ylen - 2, ylen - 3)
+        rows = (0, 1, 2) if wall == 0 else (7, 6, 5)
         state = []
         for c in (0, 2, 4):
             a = [r_ref[pl.ds(c * 64 + y, 8, stride=8), :] for y in rows]
@@ -200,6 +185,7 @@
         for s in (1, 2):
             x = x + pltpu.roll(x, 8 - s, 0)
         pushes.append(x)
+    copies[1].wait()
     ids = map_ref[...].astype(F32)
     tall = jnp.concatenate(pushes + [ids, jnp.zeros((96, 128), F32)], axis=0)
     buf[...] = jnp.transpose(tall)
@@ -214,39 +200,93 @@
                     jnp.broadcast_to(g[:, 16 + col : 17 + col], (8, 128)),
                 )
             )
+    table = []
     for j in range(table_ref.shape[0]):
         total = jnp.zeros((8, 128), F32)
         for load, panel in columns:
             total = total + jnp.where(panel == lane + 128.0 * j, load, 0.0)
-        table_ref[pl.ds(j, 1), :] = jnp.sum(total, axis=0, keepdims=True)
+        table.append(jnp.sum(total, axis=0, keepdims=True))
+        table_ref[pl.ds(j, 1), :] = table[j]
+    for c in range(0, COMPS, 2):
+        def row(i, y):
+            return r_ref[pl.ds((c + i) * 64 + y, 8, stride=8), :]
+
+        lo = jnp.concatenate([r_ref[pl.ds((c + i) * 64, 24), :] for i in (0, 1)], axis=0)
+        hi = jnp.concatenate([r_ref[pl.ds((c + i) * 64 + 40, 24), :] for i in (0, 1)], axis=0)
+        store_layers(x_refs, c, lo, hi, flags[6])
+        lo = jnp.concatenate([row(i, y) for i in (0, 1) for y in range(3)], axis=0)
+        hi = jnp.concatenate([row(i, y) for i in (0, 1) for y in range(5, 8)], axis=0)
+        store_layers(y_refs, c, lo, hi, flags[7])
+    for ref in (*x_refs, *y_refs):
+        rows = ref.shape[0] - COMPS * 24
+        if rows:
+            pieces = [piece[j] for piece in zip(*map(split3, table)) for j in range(len(table))]
+            if rows > len(pieces):
+                pieces.append(jnp.zeros((rows - len(pieces), 128), F32))
+            ref[pl.ds(COMPS * 24, rows), :] = jnp.concatenate(pieces, axis=0).astype(BF16)
+    low = half_lanes((64, 128))
+    for c in range(0, COMPS, 2):
+        t = jnp.transpose(r_ref[pl.ds(c * 64, 128), :])
+        top, bottom = t[:64], t[64:]
+        even = jnp.where(low, top, swap_halves(bottom))
+        odd = jnp.where(low, swap_halves(top), bottom)
+        for i, x in ((0, even), (1, odd)):
+            zt_ref[pl.ds((c + i) * 64, 64), :] = x
+            for m, ref in enumerate(z_refs):
+                up = flags[8] == m
+                ref[pl.ds((c + i) * 3, 3), :] = jnp.where(up, x[61:], x[:3])
+    for ref in z_refs:
+        rows = ref.shape[0] - COMPS * 3
+        ref[pl.ds(COMPS * 3, rows), :] = jnp.zeros((rows, 128), F32)
+
+
+def store_layers(refs, c, lo, hi, parity):
+    for m, ref in enumerate(refs):
+        ref[pl.ds(c * 24, 48), :] = jnp.where(parity == m, hi, lo).astype(BF16)
 
 
 def pack(fields, panels, flags, pair_x, table_rows):
-    halo = jax.ShapeDtypeStruct((COMPS * 24, 128), BF16)
-    edge = jax.ShapeDtypeStruct((COMPS * 3, 128), F32)
+    load_rows = -(-3 * table_rows // 16) * 16
+    layer_x = jax.ShapeDtypeStruct((COMPS * 24 + (load_rows if pair_x else 0), 128), BF16)
+    layer_y = jax.ShapeDtypeStruct((COMPS * 24 + load_rows, 128), BF16)
+    edge = jax.ShapeDtypeStruct((40 + -(-table_rows // 8) * 8, 128), F32)
     whole = jax.ShapeDtypeStruct((COMPS * 64, 128), F32)
-    outs = [whole, whole] + [halo] * (1 if pair_x else 2) + [halo, halo, edge, edge]
+    outs = [whole, whole] + [layer_x] * (2 - pair_x) + [layer_y] * 2 + [edge] * 2
     outs.append(jax.ShapeDtypeStruct((table_rows, 128), F32))
     return pl.pallas_call(
-        lambda *a: pack_kernel(pair_x, *a),
+        lambda *a: pack_kernel(int(pair_x), *a),
         out_shape=outs,
-        in_specs=[SM, VM, VM],
+        in_specs=[SM, ANY, ANY],
         out_specs=[VM] * len(outs),
-        scratch_shapes=[pltpu.VMEM((128, 128), F32)],
+        scratch_shapes=[
+            pltpu.VMEM((128, 128), F32),
+            pltpu.VMEM(fields.shape, F32),
+            pltpu.VMEM(panels.shape, jnp.int32),
+            pltpu.SemaphoreType.DMA((2,)),
+        ],
+        compiler_params=GRANT,
+        cost_estimate=cost(2),
         name="pack",
     )(flags, fields, panels)
 
 
-def chem_kernel(slots, r_ref, react_ref, w1_ref, w2_ref, w3_ref, w4_ref, out_ref):
-    def dot(a, b):
-        return jnp.dot(a, b, preferred_element_type=F32)
-
-    def iota(shape, dim):
-        return lax.broadcasted_iota(jnp.int32, shape, dim)
-
-    def where1(mask):
-        return jnp.where(mask, 1.0, 0.0).astype(BF16)
-
+def cost(us):
+    return pl.CostEstimate(flops=0, transcendentals=0, bytes_accessed=int(us * 3.5e6))
+
+
+def dot(a, b):
+    return jnp.dot(a, b, preferred_element_type=F32)
+
+
+def iota(shape, dim):
+    return lax.broadcasted_iota(jnp.int32, shape, dim)
+
+
+def where1(mask):
+    return jnp.where(mask, 1.0, 0.0).astype(BF16)
+
+
+def chem_in_kernel(slots, r_ref, react_ref, w1_ref, h_ref, row_ref, hit_ref):
     react = react_ref[...].astype(F32)
     react_b = react.astype(BF16)
     upper = where1(iota((128, 128), 0) <= iota((128, 128), 1))
@@ -257,7 +297,7 @@
     rank = (react * (within + offset)).astype(BF16)
     slot_lane = iota((64, slots), 1).astype(F32)
     off_col, cnt_col = offset[:, :1], count[:, :1]
-    row_slot = where1((slot_lane >= off_col) & (slot_lane < off_col + cnt_col))
+    row_ref[...] = where1((slot_lane >= off_col) & (slot_lane < off_col + cnt_col))
     nt = (((1,), (1,)), ((), ()))
     count_row = lax.dot_general(
         jnp.ones((8, 128), BF16), react_b, nt, preferred_element_type=F32
@@ -270,36 +310,79 @@
         (slot_sub >= offset_row[:1]) & (slot_sub < offset_row[:1] + count_row[:1])
     )
     lane_hit = dot(slot_row, rank) == iota((slots, 128), 0).astype(F32) + 1.0
+    hit_ref[...] = where1(lane_hit)
     feat = jnp.zeros((slots, 128), F32)
     for c in range(COMPS):
         rows = dot(slot_row, r_ref[pl.ds(c * 64, 64), :].astype(BF16))
         hit = jnp.where(lane_hit, rows, 0.0).astype(BF16)
         feat = feat + dot(hit, where1(iota((128, 128), 1) == c))
-    h = jnp.transpose(feat)[:COMPS].astype(BF16)
-    for w_ref in (w1_ref, w2_ref, w3_ref):
-        h = jax.nn.gelu(dot(w_ref[...], h)).astype(BF16)
-    rates = dot(w4_ref[...], h)
+    feat = jnp.transpose(feat)[:COMPS].astype(BF16)
+    tn = (((0,), (0,)), ((), ()))
+    one = lax.dot_general(w1_ref[...], feat, tn, preferred_element_type=F32)
+    h_ref[...] = jax.nn.gelu(one).astype(BF16)
+
+
+def chem_in(recon, react, layer_one, slots):
+    return pl.pallas_call(
+        lambda *a: chem_in_kernel(slots, *a),
+        out_shape=[
+            jax.ShapeDtypeStruct((layer_one.shape[1], slots), BF16),
+            jax.ShapeDtypeStruct((64, slots), BF16),
+            jax.ShapeDtypeStruct((slots, 128), BF16),
+        ],
+        in_specs=[VM] * 3,
+        out_specs=[VM] * 3,
+        compiler_params=GRANT,
+        cost_estimate=cost(2),
+        name="chem_in",
+    )(recon, react, layer_one)
+
+
+def chem_mid_kernel(h_ref, w2_ref, w3_ref, out_ref):
+    two = jax.nn.gelu(dot(w2_ref[...], h_ref[...])).astype(BF16)
+    out_ref[...] = jax.nn.gelu(dot(w3_ref[...], two)).astype(BF16)
+
+
+def chem_mid(hidden, layer_two, layer_three):
+    return pl.pallas_call(
+        chem_mid_kernel,
+        out_shape=jax.ShapeDtypeStruct((layer_three.shape[0], hidden.shape[1]), BF16),
+        in_specs=[VM] * 3,
+        out_specs=VM,
+        compiler_params=GRANT,
+        cost_estimate=cost(2),
+        name="chem_mid",
+    )(hidden, layer_two, layer_three)
+
+
+def chem_out_kernel(h_ref, w4_ref, row_ref, hit_ref, out_ref):
+    rates = dot(w4_ref[...], h_ref[...])
+    slots = rates.shape[1]
     rates = jnp.concatenate([rates, jnp.zeros((128 - COMPS, slots), F32)], axis=0)
     rates_t = jnp.transpose(rates).astype(BF16)
+    hit, row_slot = hit_ref[...].astype(F32), row_ref[...]
     for c in range(COMPS):
-        spread = dot(rates_t, where1(iota((128, 128), 0) == c))
-        spread = jnp.where(lane_hit, spread, 0.0).astype(BF16)
-        out_ref[pl.ds(c * 64, 64), :] = dot(row_slot, spread)
-
-
-def chem(recon, react, layers, slots):
+        spread = hit * dot(rates_t, where1(iota((128, 128), 0) == c))
+        out_ref[pl.ds(c * 64, 64), :] = dot(row_slot, spread.astype(BF16))
+
+
+def chem_out(hidden, layer_four, row_slot, hit):
     return pl.pallas_call(
-        lambda *a: chem_kernel(slots, *a),
-        out_shape=jax.ShapeDtypeStruct(recon.shape, F32),
-        in_specs=[VM] * 6,
+        chem_out_kernel,
+        out_shape=jax.ShapeDtypeStruct((COMPS * 64, 128), F32),
+        in_specs=[VM] * 4,
         out_specs=VM,
-        name="chem",
-    )(recon, react, *layers)
-
-
-def halo_lines(ref, scratch, own, sign_comp, at_wall, order):
+        compiler_params=GRANT,
+        cost_estimate=cost(2),
+        name="chem_out",
+    )(hidden, layer_four, row_slot, hit)
+
+
+def halo_lines(refs, scratch, own, sign_comp, at_wall, order, second):
     for c in range(0, COMPS, 2):
-        block = ref[pl.ds(c * 24, 48), :].astype(F32)
+        block = refs[0][pl.ds(c * 24, 48), :].astype(F32)
+        if len(refs) == 2:
+            block = jnp.where(second, refs[1][pl.ds(c * 24, 48), :].astype(F32), block)
         for i in (0, 1):
             for k in range(3):
                 mirror = own(c + i, order[k])
@@ -309,12 +392,14 @@
                 scratch[pl.ds(((c + i) * 3 + k) * 8, 8), :] = jnp.where(at_wall, mirror, got)
 
 
-def flux_x_kernel(flags, r_ref, lo_ref, hi_ref, out_ref, lo_s, hi_s, left, right):
+def flux_x_kernel(count, flags, r_ref, *refs):
+    layers, (out_ref, token, lo_s, hi_s, left, right) = refs[:count], refs[count:]
+
     def own(c, x):
         return r_ref[pl.ds(c * 64 + x * 8, 8), :]
 
-    halo_lines(lo_ref, lo_s, own, 1, flags[0] == 1, (2, 1, 0))
-    halo_lines(hi_ref, hi_s, own, 1, flags[1] == 1, (7, 6, 5))
+    halo_lines(layers, lo_s, own, 1, flags[0] == 1, (2, 1, 0), flags[6] == 0)
+    halo_lines(layers, hi_s, own, 1, flags[1] == 1, (7, 6, 5), flags[6] == 1)
 
     def line(c):
         return (
@@ -329,14 +414,21 @@
         out_ref[pl.ds(c * 64 + x * 8, 8), :] = change
 
     line_changes(left, right, 9, 0, emit)
-
-
-def flux_y_kernel(flags, r_ref, lo_ref, hi_ref, acc_ref, out_ref, lo_s, hi_s, left, right):
+    token[...] = jnp.zeros(token.shape, F32)
+
+
+def flux_y_kernel(
+    count, flags, f_hbm, r_ref, acc_ref, src_ref, *refs
+):
+    layers, (out_ref, lo_s, hi_s, left, right, f_ref, sem) = refs[:count], refs[count:]
+    copy = pltpu.make_async_copy(f_hbm, f_ref, sem)
+    copy.start()
+
     def own(c, y):
         return r_ref[pl.ds(c * 64 + y, 8, stride=8), :]
 
-    halo_lines(lo_ref, lo_s, own, 2, flags[2] == 1, (2, 1, 0))
-    halo_lines(hi_ref, hi_s, own, 2, flags[3] == 1, (7, 6, 5))
+    halo_lines(layers, lo_s, own, 2, flags[2] == 1, (2, 1, 0), flags[7] == 0)
+    halo_lines(layers, hi_s, own, 2, flags[3] == 1, (7, 6, 5), flags[7] == 1)
 
     def line(c):
         return (
@@ -346,26 +438,35 @@
         )
 
     face_states(line, left, right, 9)
+    copy.wait()
 
     def emit(c, y, change):
         at = pl.ds(c * 64 + y, 8, stride=8)
-        out_ref[at, :] = acc_ref[at, :] + change
+        out_ref[at, :] = (
+            f_ref[at, :] - TIME_STEP * (acc_ref[at, :] + change) + CHEM_STEP * src_ref[at, :]
+        )
 
     line_changes(left, right, 9, 1, emit)
 
 
-def flux_z_kernel(
-    flags, f_ref, zt_ref, lo_ref, hi_ref, acc_ref, src_ref, out_ref, ext, left, right, back
-):
+def flux_z_kernel(count, flags, zt_ref, acc_ref, *refs):
+    layers, (out_ref, token, ext, left, right, back) = refs[:count], refs[count:]
     low3, low = half_lanes((3, 128)), half_lanes((64, 128))
+
+    def got(c, second):
+        x = layers[0][pl.ds(c * 3, 3), :]
+        if count == 2:
+            x = jnp.where(second, layers[1][pl.ds(c * 3, 3), :], x)
+        return swap_halves(x)
+
     for c in range(COMPS):
         sign = -1.0 if c == 3 else 1.0
         own = zt_ref[pl.ds(c * 64, 64), :]
         first, last = own[:3], own[61:]
         mirror_lo = sign * jnp.concatenate([first[2:3], first[1:2], first[0:1]], axis=0)
         mirror_hi = sign * jnp.concatenate([last[2:3], last[1:2], last[0:1]], axis=0)
-        below = jnp.where(flags[4] == 1, mirror_lo, swap_halves(lo_ref[pl.ds(c * 3, 3), :]))
-        above = jnp.where(flags[5] == 1, mirror_hi, swap_halves(hi_ref[pl.ds(c * 3, 3), :]))
+        below = jnp.where(flags[4] == 1, mirror_lo, got(c, flags[8] == 0))
+        above = jnp.where(flags[5] == 1, mirror_hi, got(c, flags[8] == 1))
         ext[pl.ds(c * 72, 3), :] = jnp.where(low3, below, swap_halves(last))
         ext[pl.ds(c * 72 + 3, 64), :] = own
         ext[pl.ds(c * 72 + 67, 3), :] = jnp.where(low3, swap_halves(first), above)
@@ -386,8 +487,8 @@
             axis=0,
         )
         at = pl.ds(c * 64, 128)
-        change = acc_ref[at, :] + jnp.transpose(t)
-        out_ref[at, :] = f_ref[at, :] - TIME_STEP * change + CHEM_STEP * src_ref[at, :]
+        out_ref[at, :] = acc_ref[at, :] + jnp.transpose(t)
+    token[...] = jnp.zeros(token.shape, F32)
 
 
 def state_scratch():
@@ -398,39 +499,59 @@
     return [pltpu.VMEM((COMPS * 24, 128), F32)] * 2
 
 
-def flux_x(flags, recon, lo, hi):
+def token_shape(table):
+    return jax.ShapeDtypeStruct(table.shape, F32)
+
+
+def flux_x(flags, recon, layers, table):
     return pl.pallas_call(
-        flux_x_kernel,
+        lambda *a: flux_x_kernel(len(layers), *a),
+        out_shape=[jax.ShapeDtypeStruct(recon.shape, F32), token_shape(table)],
+        in_specs=[SM] + [VM] * (1 + len(layers)),
+        out_specs=[VM] * 2,
+        scratch_shapes=halo_scratch() + state_scratch(),
+        compiler_params=GRANT,
+        cost_estimate=cost(2),
+        name="flux_x",
+    )(flags, recon, *layers)
+
+
+def flux_y(flags, fields, recon, acc, source, layers):
+    return pl.pallas_call(
+        lambda *a: flux_y_kernel(len(layers), *a),
         out_shape=jax.ShapeDtypeStruct(recon.shape, F32),
-        in_specs=[SM] + [VM] * 3,
+        in_specs=[SM, ANY] + [VM] * (3 + len(layers)),
         out_specs=VM,
-        scratch_shapes=halo_scratch() + state_scratch(),
-        name="flux_x",
-    )(flags, recon, lo, hi)
-
-
-def flux_y(flags, recon, lo, hi, acc):
+        scratch_shapes=halo_scratch()
+        + state_scratch()
+        + [pltpu.VMEM(fields.shape, F32), pltpu.SemaphoreType.DMA],
+        compiler_params=GRANT,
+        cost_estimate=cost(2),
+        name="flux_y",
+    )(flags, fields, recon, acc, source, *layers)
+
+
+def flux_z(flags, turned, acc, layers, table):
     return pl.pallas_call(
-        flux_y_kernel,
-        out_shape=jax.ShapeDtypeStruct(recon.shape, F32),
-        in_specs=[SM] + [VM] * 4,
-        out_specs=VM,
-        scratch_shapes=halo_scratch() + state_scratch(),
-        name="flux_y",
-    )(flags, recon, lo, hi, acc)
-
-
-def flux_z(flags, fields, turned, lo, hi, acc, source):
-    return pl.pallas_call(
-        flux_z_kernel,
-        out_shape=jax.ShapeDtypeStruct(fields.shape, F32),
-        in_specs=[SM] + [VM] * 6,
-        out_specs=VM,
+        lambda *a: flux_z_kernel(len(layers), *a),
+        out_shape=[jax.ShapeDtypeStruct(acc.shape, F32), token_shape(table)],
+        in_specs=[SM] + [VM] * (2 + len(layers)),
+        out_specs=[VM] * 2,
         scratch_shapes=[pltpu.VMEM((COMPS * 72, 128), F32)]
         + state_scratch()
-        + [pltpu.VMEM(fields.shape, F32)],
+        + [pltpu.VMEM(acc.shape, F32)],
+        compiler_params=GRANT,
+        cost_estimate=cost(3),
         name="flux_z",
-    )(flags, fields, turned, lo, hi, acc, source)
+    )(flags, turned, acc, *layers)
+
+
+def swap(x, axis, second):
+    n = lax.axis_size(axis)
+    pairs = [(i, i + 1) for i in range(int(second), n - 1, 2)]
+    if second and n == 4:
+        pairs.append((0, n - 1))
+    return lax.ppermute(x, axis, [(a, b) for a, b in pairs] + [(b, a) for a, b in pairs])
 
 
 def sum_over(table, axis):
@@ -444,39 +565,65 @@
     return table
 
 
+def split_table(table):
+    hi = lax.reduce_precision(table, 8, 7)
+    mid = lax.reduce_precision(table - hi, 8, 7)
+    return jnp.concatenate([hi, mid, table - hi - mid], axis=0).astype(BF16)
+
+
+def join_table(rows, height):
+    rows = rows[: 3 * height].astype(F32)
+    return rows[:height] + rows[height : 2 * height] + rows[2 * height :]
+
+
 def body(fields, reacting, panel_map, layer_one, layer_two, layer_three, layer_four):
     shape = fields.shape
     sizes = [lax.axis_size(a) for a in AXES]
     index = [lax.axis_index(a) for a in AXES]
-    flags = jnp.stack(
-        [f.astype(jnp.int32) for i, n in zip(index, sizes) for f in (i == 0, i == n - 1)]
-    )
+    flags = [f for i, n in zip(index, sizes) for f in (i == 0, i == n - 1)]
+    flags = jnp.stack([f.astype(jnp.int32) for f in flags] + [i % 2 for i in index])
     pair_x = sizes[0] == 2
     panels_all = 2 * (shape[1] * sizes[0] // PATCH) * (shape[3] * sizes[2] // PATCH)
+    height = panels_all // 128
     flat = fields.reshape(-1, shape[3])
-    packed = pack(flat, panel_map.reshape(-1, shape[3]), flags, pair_x, panels_all // 128)
-    recon, turned = packed[:2]
-    y_lo, y_hi, z_lo, z_hi, table = packed[-5:]
-
-    def move(x, axis, up):
-        n = lax.axis_size(axis)
-        pairs = [(i, i + 1) if up else (i + 1, i) for i in range(n - 1)]
-        return lax.ppermute(x, axis, pairs)
-
+    packed = pack(flat, panel_map.reshape(-1, shape[3]), flags, pair_x, height)
+    recon, turned, table = packed[0], packed[1], packed[-1]
+    xs, ys, zs = packed[2:-5], packed[-5:-3], packed[-3:-1]
+    slots = BAL * min(4, sizes[0])
+    layer_rows, edge_rows = COMPS * 24, 40
+
+    got = [swap(x, "gx", m) for m, x in enumerate(xs)]
+    hidden, row_slot, hit = chem_in(recon, reacting.reshape(-1, shape[3]), layer_one.T, slots)
     if pair_x:
-        x_below = x_above = lax.ppermute(packed[2], "gx", [(0, 1), (1, 0)])
+        table = table + join_table(got[0][layer_rows:], height)
     else:
-        x_below, x_above = move(packed[3], "gx", True), move(packed[2], "gx", False)
-    y_below, y_above = move(y_hi, "gy", True), move(y_lo, "gy", False)
-    z_below, z_above = move(z_hi, "gz", True), move(z_lo, "gz", False)
-    layers = (layer_one, layer_two, layer_three, layer_four)
-    slots = BAL * min(4, sizes[0])
-    source = chem(recon, reacting.reshape(-1, shape[3]), layers, slots)
-    acc = flux_x(flags, recon, x_below, x_above)
-    acc = flux_y(flags, recon, y_below, y_above, acc)
-    new = flux_z(flags, flat, turned, z_below, z_above, acc, source)
-    for axis in ("gx", "gz", "gy"):
-        table = sum_over(table, axis)
+        table = sum_over(table, "gx")
+    ride_z, ride_y = sizes[2] in (2, 4), sizes[1] in (2, 4)
+    if not ride_z:
+        table = sum_over(table, "gz")
+    z_got = [swap(lax.dynamic_update_slice(zs[0], table, (edge_rows, 0)), "gz", 0)]
+    acc, token = flux_x(flags, recon, got, table)
+    if ride_z:
+        table = table + z_got[0][edge_rows : edge_rows + height] + token
+    if sizes[2] > 2:
+        z_got.append(swap(lax.dynamic_update_slice(zs[1], table, (edge_rows, 0)), "gz", 1))
+        if ride_z:
+            table = table + z_got[1][edge_rows : edge_rows + height]
+    hidden = chem_mid(hidden, layer_two, layer_three)
+    if not ride_y:
+        table = sum_over(table, "gy")
+    y_got = [swap(lax.dynamic_update_slice(ys[0], split_table(table), (layer_rows, 0)), "gy", 0)]
+    acc, token = flux_z(flags, turned, acc, z_got, table)
+    if ride_y:
+        table = table + join_table(y_got[0][layer_rows:], height) + token
+    if sizes[1] > 2:
+        y_got.append(
+            swap(lax.dynamic_update_slice(ys[1], split_table(table), (layer_rows, 0)), "gy", 1)
+        )
+        if ride_y:
+            table = table + join_table(y_got[1][layer_rows:], height)
+    source = chem_out(hidden, layer_four, row_slot, hit)
+    new = flux_y(flags, flat, recon, acc, source, y_got)
     own = panels_all // (sizes[0] * sizes[1] * sizes[2])
     place = (index[0] * sizes[1] + index[1]) * sizes[2] + index[2]
     result = lax.dynamic_slice_in_dim(table.reshape(-1), place * own, own)

time: 53.6 us -> 34.6 us (0.65)
  the two profiles are of different devices: /device:TPU:1 before, /device:TPU:0 now
where the time goes in v2:
time: 34.6 us; the launch traced here: 34.2 us
  Pallas kernels  11.6 us (34%)
  starting transfers between devices  10.9 us (32%)
  local copies, waits for them, and re-layouts  5.34 us (15%)
  waiting for transfers between devices  4.84 us (14%)
  between operations  0.81 us (2%)
  other arithmetic  0.7 us (2%)
    ppermute x5, starting transfers between devices, swap(): lax.ppermute(x, axis, [(a, b) for a, b in pairs] + [(b, a) for a, b in pa...  10.9 us
    unnamed x16, local copies, waits for them, and re-layouts  5.02 us
    ppermute x5, waiting for transfers between devices, swap(): lax.ppermute(x, axis, [(a, b) for a, b in pairs] + [(b, a) for a, b in pa...  4.84 us
    pallas_call x1, Pallas kernels, flux_y(): pl.pallas_call(lambda *a: flux_y_kernel(len(layers), *a), out_shape=jax.S...  3.03 us
    pallas_call x1, Pallas kernels, flux_z(): pl.pallas_call(lambda *a: flux_z_kernel(len(layers), *a), out_shape=[jax....  2.06 us
    pallas_call x1, Pallas kernels, flux_x(): pl.pallas_call(lambda *a: flux_x_kernel(len(layers), *a), out_shape=[jax....  1.69 us
    pallas_call x1, Pallas kernels, pack(): pl.pallas_call(lambda *a: pack_kernel(int(pair_x), *a), out_shape=outs, i...  1.48 us
    pallas_call x1, Pallas kernels, chem_mid(): pl.pallas_call(chem_mid_kernel, out_shape=jax.ShapeDtypeStruct((layer_thr...  1.48 us
  transfers between devices with their start and end apart: 5, of which 3 were waited for; matrix products, arithmetic and copies ran while one was open for 0% of the time, Pallas kernels for 21%

profile of v2, /device:TPU:0, one launch (start us, length us, event | category | flops | bytes accessed | tf_op | source)
XLA Modules:
  0.0 34.2 jit_solution(3184937628495470209)
XLA Ops:
  0.7 0.1 stack.63.a_0_
  0.8 1.0 %copy-done.1 = f32[12,8,8,128]{3,2,1,0:T(8,128)S(1)} copy-done((f32[12,8,8,128]{3,2,1,0:T(8,128)S(1)}, f32[12,8,8,128]{3,2,1,0:T(8,128)}, u32[]{:S(2)}) %copy-start.1) | copy-done | bytes 393240
  1.8 0.7 %copy-done.7 = s32[2,8,128]{2,1,0:T(8,128)S(1)} copy-done((s32[2,8,128]{2,1,0:T(8,128)S(1)}, s32[2,8,128]{2,1,0:T(8,128)}, u32[]{:S(2)}) %copy-start.7) | copy-done | bytes 8216
  2.5 1.5 %pack.1 = (f32[768,128]{1,0:T(8,128)S(1)}, f32[768,128]{1,0:T(8,128)S(1)}, bf16[304,128]{1,0:T(8,128)(2,1)S(1)}, bf16[304,128]{1,0:T(8,128)(2,1)S(1)}, bf16[304,...) custom-call(s32[9]{0:T(128)S(1)} %stack.63.a_0_, ...), custom_call_target="tpu_custom_call" | custom-call | bytes 7000000 | tf_op jit(solution)/shard_map/pack/pallas_call | solution.py:256
  3.9 3.0 %collective-permute-start = (bf16[304,128]{1,0:T(8,128)(2,1)S(1)}, bf16[304,128]{1,0:T(8,128)(2,1)S(1)}, u32[]{:S(2)}, u32[]{:S(2)}) collective-permute-start(bf16[304,128]{1,0:T(8,128)(2,1)S(1)} %get-tuple-element.19), channel_id=1, source_target_pairs={{0,16},{16,0},{1,17},{17,1},{2,18},{18,2},{3,19},{19,3},{4,20},{20... | collective-permute-start | bytes 233480 | tf_op jit(solution)/shard_map/ppermute | solution.py:554
  7.0 2.4 %collective-permute-done.a_2_ = bf16[304,128]{1,0:T(8,128)(2,1)S(1)} collective-permute-done((bf16[304,128]{1,0:T(8,128)(2,1)S(1)}, bf16[304,128]{1,0:T(8,128)(2,1)S(1)}, u32[]{:S(2)}, u32[]{:S(2)}) %collective-permute-start) | collective-permute-done | bytes 77856 | tf_op jit(solution)/shard_map/ppermute | solution.py:554
  9.4 0.1 collective-permute-start.1
  9.4 1.7 %flux_x.1 = (f32[768,128]{1,0:T(8,128)S(1)}, f32[2,128]{1,0:T(2,128)S(1)}) custom-call(s32[9]{0:T(128)S(1)} %stack.63.a_0_, f32[768,128]{1,0:T(8,128)S(1)} %get-tuple-element.17.a_1_.a_0_.a_2_, bf16[304,128]{1,0:T(8,128)(2,1)S(1)} %collective-permute-done.a_2_), custom_call_target="tpu_custom_call" | custom-call | bytes 7000000 | tf_op jit(solution)/shard_map/flux_x/pallas_call | solution.py:507
  11.2 2.2 %collective-permute-start.2 = (f32[48,128]{1,0:T(8,128)S(1)}, f32[48,128]{1,0:T(8,128)S(1)}, u32[]{:S(2)}, u32[]{:S(2)}) collective-permute-start(f32[48,128]{1,0:T(8,128)S(1)} %constant_dynamic-update-slice_fusion), channel_id=1, source_target_pairs={{1,2},{0,3},{2,1},{3,0},{5,6},{4,7},{6,5},{7,4},{9,10},{8,11},{10,... | collective-permute-start | bytes 73736 | tf_op jit(solution)/shard_map/ppermute | solution.py:554
  13.4 1.5 %collective-permute-done.2.a_4_ = f32[48,128]{1,0:T(8,128)S(1)} collective-permute-done((f32[48,128]{1,0:T(8,128)S(1)}, f32[48,128]{1,0:T(8,128)S(1)}, u32[]{:S(2)}, u32[]{:S(2)}) %collective-permute-start.2) | collective-permute-done | bytes 24608 | tf_op jit(solution)/shard_map/ppermute | solution.py:554
  14.9 0.1 dynamic_update_slice.14
  15.1 1.8 %collective-permute-start.3 = (bf16[304,128]{1,0:T(8,128)(2,1)S(1)}, bf16[304,128]{1,0:T(8,128)(2,1)S(1)}, u32[]{:S(2)}, u32[]{:S(2)}) collective-permute-start(bf16[304,128]{1,0:T(8,128)(2,1)S(1)} %dynamic_update_slice.14), channel_id=1, source_target_pairs={{0,4},{8,12},{4,0},{12,8},{1,5},{9,13},{5,1},{13,9},{2,6},{10,14},... | collective-permute-start | bytes 233480 | tf_op jit(solution)/shard_map/ppermute | solution.py:554
  16.8 2.1 %flux_z.1 = (f32[768,128]{1,0:T(8,128)S(1)}, f32[2,128]{1,0:T(2,128)S(1)}) custom-call(s32[9]{0:T(128)S(1)} %stack.63.a_0_, f32[768,128]{1,0:T(8,128)S(1)} %get-tuple-element.18.a_1_, f32[768,128]{1,0:T(8,128)S(1)} %get-tuple-element.20.a_2_, f32[48,128]{1,0:T(8,128)S(1)} %collective-permute-done.1.a_3_, f32[48,128]{1,0:T(8,128)S(1)} %collective-permute-done.2.a_4_), custom_call_target="tpu_custom_call" | custom-call | bytes 10500000 | tf_op jit(solution)/shard_map/flux_z/pallas_call | solution.py:535
  18.9 0.9 %collective-permute-done.3.a_5_ = bf16[304,128]{1,0:T(8,128)(2,1)S(1)} collective-permute-done((bf16[304,128]{1,0:T(8,128)(2,1)S(1)}, bf16[304,128]{1,0:T(8,128)(2,1)S(1)}, u32[]{:S(2)}, u32[]{:S(2)}) %collective-permute-start.3) | collective-permute-done | bytes 77856 | tf_op jit(solution)/shard_map/ppermute | solution.py:554
  19.9 0.1 dynamic_update_slice.15
  20.0 3.8 %collective-permute-start.4 = (bf16[304,128]{1,0:T(8,128)(2,1)S(1)}, bf16[304,128]{1,0:T(8,128)(2,1)S(1)}, u32[]{:S(2)}, u32[]{:S(2)}) collective-permute-start(bf16[304,128]{1,0:T(8,128)(2,1)S(1)} %dynamic_update_slice.15), channel_id=1, source_target_pairs={{4,8},{0,12},{8,4},{12,0},{5,9},{1,13},{9,5},{13,1},{6,10},{2,14},... | collective-permute-start | bytes 233480 | tf_op jit(solution)/shard_map/ppermute | solution.py:554
  23.8 0.8 %copy-done.4 = bf16[1600,12]{0,1:T(8,128)(2,1)S(1)} copy-done((bf16[1600,12]{0,1:T(8,128)(2,1)S(1)}, bf16[1600,12]{0,1:T(8,128)(2,1)}, u32[]{:S(2)}) %copy-start.4) | copy-done | bytes 38424
  24.6 0.8 %copy-done.5 = s32[8,8,128]{2,1,0:T(8,128)S(1)} copy-done((s32[8,8,128]{2,1,0:T(8,128)S(1)}, s32[8,8,128]{2,1,0:T(8,128)}, u32[]{:S(2)}) %copy-start.5) | copy-done | bytes 32792
  25.4 1.2 %chem_in.1 = (bf16[1600,128]{1,0:T(8,128)(2,1)S(1)}, bf16[64,128]{1,0:T(8,128)(2,1)S(1)}, bf16[128,128]{1,0:T(8,128)(2,1)S(1)}) custom-call(f32[768,128]{1,0:T(8,128)S(1)} %get-tuple-element.17.a_1_.a_0_.a_2_, s32[64,128]{1,0:T(8,128)S(1)} %bitcast.19, bf16[12,1600]{1,0:T(8,128)(2,1)S(1)} %bitcast.18), custom_call_target="tpu_custom_call" | custom-call | bytes 7000000 | tf_op jit(solution)/shard_map/chem_in/pallas_call | solution.py:326
  26.7 1.7 %copy-done = bf16[800,1600]{1,0:T(8,128)(2,1)S(1)} copy-done((bf16[800,1600]{1,0:T(8,128)(2,1)S(1)}, bf16[800,1600]{1,0:T(8,128)(2,1)}, u32[]{:S(2)}) %copy-start) | copy-done | bytes 2560024
  28.4 1.5 %chem_mid.1.h_ref = bf16[400,128]{1,0:T(8,128)(2,1)S(1)} custom-call(bf16[1600,128]{1,0:T(8,128)(2,1)S(1)} %get-tuple-element.26.h_ref, bf16[800,1600]{1,0:T(8,128)(2,1)S(1)} %copy-done, bf16[400,800]{1,0:T(8,128)(2,1)S(1)} %copy-done.3), custom_call_target="tpu_custom_call" | custom-call | bytes 7000000 | tf_op jit(solution)/shard_map/chem_mid/pallas_call | solution.py:347
  29.9 0.7 %chem_out.1.a_4_ = f32[768,128]{1,0:T(8,128)S(1)} custom-call(bf16[400,128]{1,0:T(8,128)(2,1)S(1)} %chem_mid.1.h_ref, bf16[12,400]{1,0:T(8,128)(2,1)S(1)} %copy-done.6, bf16[64,128]{1,0:T(8,128)(2,1)S(1)} %get-tuple-element.27.row_ref, bf16[128,128]{1,0:T(8,128)(2,1)S(1)} %get-tuple-element.28.hit_ref), custom_call_target="tpu_custom_call" | custom-call | bytes 7000000 | tf_op jit(solution)/shard_map/chem_out/pallas_call | solution.py:370
  30.6 0.6 %dynamic-slice_multiply_fusion = f32[8]{0:T(128)} fusion(f32[256]{0:T(256)S(1)} %add_bitcast_fusion, s32[]{:T(128)S(6)} %select_n.21), kind=kLoop, calls=%fused_computation.23 | loop fusion | flops 8 | bytes 68 | tf_op jit(solution)/shard_map/div | solution.py:630
  31.2 3.0 %flux_y.1 = f32[768,128]{1,0:T(8,128)} custom-call(s32[9]{0:T(128)S(1)} %stack.63.a_0_, f32[768,128]{1,0:T(8,128)S(1)} %bitcast.17, f32[768,128]{1,0:T(8,128)S(1)} %get-tuple-element.17.a_1_.a_0_.a_2_, f32[768,128]{1,0:T(8,128)S(1)} %get-tuple-element.25.a_3_, f32[768,128]{1,0:T(8,128)S(1)} %chem_out.1.a_4_, ...), custom_call_target="tpu_custom_call" | custom-call | bytes 7000000 | tf_op jit(solution)/shard_map/flux_y/pallas_call | solution.py:520
  (25 shorter events, 0.1 us)
Async XLA Ops:
  0.8 1.0 %copy-start.1 = (f32[12,8,8,128]{3,2,1,0:T(8,128)S(1)}, f32[12,8,8,128]{3,2,1,0:T(8,128)}, u32[]{:S(2)}) copy-start(f32[12,8,8,128]{3,2,1,0:T(8,128)} %param.7) | copy-start | bytes 1179652
  1.8 0.7 %copy-start.7 = (s32[2,8,128]{2,1,0:T(8,128)S(1)}, s32[2,8,128]{2,1,0:T(8,128)}, u32[]{:S(2)}) copy-start(s32[2,8,128]{2,1,0:T(8,128)} %param.9) | copy-start | bytes 24580
  2.5 24.2 %copy-start.3 = (bf16[400,800]{1,0:T(8,128)(2,1)S(1)}, bf16[400,800]{1,0:T(8,128)(2,1)}, u32[]{:S(2)}) copy-start(bf16[400,800]{1,0:T(8,128)(2,1)} %w3_ref.1) | copy-start | bytes 1920004
  3.9 5.4 %collective-permute-start = (bf16[304,128]{1,0:T(8,128)(2,1)S(1)}, bf16[304,128]{1,0:T(8,128)(2,1)S(1)}, u32[]{:S(2)}, u32[]{:S(2)}) collective-permute-start(bf16[304,128]{1,0:T(8,128)(2,1)S(1)} %get-tuple-element.19), channel_id=1, source_target_pairs={{0,16},{16,0},{1,17},{17,1},{2,18},{18,2},{3,19},{19,3},{4,20},{20... | collective-permute-start | bytes 233480 | tf_op jit(solution)/shard_map/ppermute | solution.py:554
  9.4 1.8 %collective-permute-start.1 = (f32[48,128]{1,0:T(8,128)S(1)}, f32[48,128]{1,0:T(8,128)S(1)}, u32[]{:S(2)}, u32[]{:S(2)}) collective-permute-start(f32[48,128]{1,0:T(8,128)S(1)} %get-tuple-element.36), channel_id=1, source_target_pairs={{0,1},{2,3},{1,0},{3,2},{4,5},{6,7},{5,4},{7,6},{8,9},{10,11},{9,8... | collective-permute-start | bytes 73736 | tf_op jit(solution)/shard_map/ppermute | solution.py:554
  11.1 18.8 %copy-start.6 = (bf16[12,400]{1,0:T(8,128)(2,1)S(1)}, bf16[12,400]{1,0:T(8,128)(2,1)}, u32[]{:S(2)}) copy-start(bf16[12,400]{1,0:T(8,128)(2,1)} %w4_ref.1) | copy-start | bytes 28804
  11.2 3.7 %collective-permute-start.2 = (f32[48,128]{1,0:T(8,128)S(1)}, f32[48,128]{1,0:T(8,128)S(1)}, u32[]{:S(2)}, u32[]{:S(2)}) collective-permute-start(f32[48,128]{1,0:T(8,128)S(1)} %constant_dynamic-update-slice_fusion), channel_id=1, source_target_pairs={{1,2},{0,3},{2,1},{3,0},{5,6},{4,7},{6,5},{7,4},{9,10},{8,11},{10,... | collective-permute-start | bytes 73736 | tf_op jit(solution)/shard_map/ppermute | solution.py:554
  15.1 4.8 %collective-permute-start.3 = (bf16[304,128]{1,0:T(8,128)(2,1)S(1)}, bf16[304,128]{1,0:T(8,128)(2,1)S(1)}, u32[]{:S(2)}, u32[]{:S(2)}) collective-permute-start(bf16[304,128]{1,0:T(8,128)(2,1)S(1)} %dynamic_update_slice.14), channel_id=1, source_target_pairs={{0,4},{8,12},{4,0},{12,8},{1,5},{9,13},{5,1},{13,9},{2,6},{10,14},... | collective-permute-start | bytes 233480 | tf_op jit(solution)/shard_map/ppermute | solution.py:554
  18.9 12.3 %copy-start.2 = (f32[12,8,8,128]{3,2,1,0:T(8,128)S(1)}, f32[12,8,8,128]{3,2,1,0:T(8,128)}, u32[]{:S(2)}) copy-start(f32[12,8,8,128]{3,2,1,0:T(8,128)} %param.7) | copy-start | bytes 1179652
  20.0 10.6 %collective-permute-start.4 = (bf16[304,128]{1,0:T(8,128)(2,1)S(1)}, bf16[304,128]{1,0:T(8,128)(2,1)S(1)}, u32[]{:S(2)}, u32[]{:S(2)}) collective-permute-start(bf16[304,128]{1,0:T(8,128)(2,1)S(1)} %dynamic_update_slice.15), channel_id=1, source_target_pairs={{4,8},{0,12},{8,4},{12,0},{5,9},{1,13},{9,5},{13,1},{6,10},{2,14},... | collective-permute-start | bytes 233480 | tf_op jit(solution)/shard_map/ppermute | solution.py:554
  23.8 0.8 %copy-start.4 = (bf16[1600,12]{0,1:T(8,128)(2,1)S(1)}, bf16[1600,12]{0,1:T(8,128)(2,1)}, u32[]{:S(2)}) copy-start(bf16[1600,12]{0,1:T(8,128)(2,1)} %param.10) | copy-start | bytes 115204
  24.6 0.8 %copy-start.5 = (s32[8,8,128]{2,1,0:T(8,128)S(1)}, s32[8,8,128]{2,1,0:T(8,128)}, u32[]{:S(2)}) copy-start(s32[8,8,128]{2,1,0:T(8,128)} %param.8) | copy-start | bytes 98308
  26.7 1.8 %copy-start = (bf16[800,1600]{1,0:T(8,128)(2,1)S(1)}, bf16[800,1600]{1,0:T(8,128)(2,1)}, u32[]{:S(2)}) copy-start(bf16[800,1600]{1,0:T(8,128)(2,1)} %w2_ref.1) | copy-start | bytes 7680004

commit v3 on v2

--- a/solution.py
+++ b/solution.py
@@ -20,7 +20,7 @@
 GRANT = pltpu.CompilerParams(vmem_limit_bytes=12 * 2**20)
 VM = pl.BlockSpec(memory_space=pltpu.VMEM)
 SM = pl.BlockSpec(memory_space=pltpu.SMEM)
-ANY = pl.BlockSpec(memory_space=pl.ANY)
+HBM = pl.BlockSpec(memory_space=pltpu.HBM)
 
 
 def weno_line(v):
@@ -143,9 +143,7 @@
     return hi, mid, x - hi - mid
 
 
-def pack_kernel(pair_x, flags, f_hbm, map_hbm, r_ref, zt_ref, *refs):
-    x_refs, refs = refs[:2 - pair_x], refs[2 - pair_x :]
-    y_refs, z_refs, table_ref, buf, f_ref, map_ref, sems = refs[:2], refs[2:4], *refs[4:]
+def pack_kernel(flags, f_hbm, map_hbm, f_ref, r_ref, y1_ref, y2_ref, table_ref, buf, map_ref, sems):
     copies = [
         pltpu.make_async_copy(f_hbm, f_ref, sems.at[0]),
         pltpu.make_async_copy(map_hbm, map_ref, sems.at[1]),
@@ -211,19 +209,93 @@
         def row(i, y):
             return r_ref[pl.ds((c + i) * 64 + y, 8, stride=8), :]
 
+        lo = jnp.concatenate([row(i, y) for i in (0, 1) for y in range(3)], axis=0)
+        hi = jnp.concatenate([row(i, y) for i in (0, 1) for y in range(5, 8)], axis=0)
+        store_layers((y1_ref, y2_ref), c, lo, hi, flags[7])
+    rows = y1_ref.shape[0] - COMPS * 24
+    pieces = [piece[j] for piece in zip(*map(split3, table)) for j in range(len(table))]
+    if rows > len(pieces):
+        pieces.append(jnp.zeros((rows - len(pieces), 128), F32))
+    y1_ref[pl.ds(COMPS * 24, rows), :] = jnp.concatenate(pieces, axis=0).astype(BF16)
+
+
+def store_layers(refs, c, lo, hi, parity):
+    for m, ref in enumerate(refs):
+        ref[pl.ds(c * 24, 48), :] = jnp.where(parity == m, hi, lo).astype(BF16)
+
+
+def merge_kernel(height, start, table_ref, got_ref, token_ref, x_ref, out_ref, sum_ref):
+    rows = got_ref[pl.ds(COMPS * 24, 8), :] if height == 2 else got_ref[pl.ds(COMPS * 24, 3 * height), :]
+    rows = rows.astype(F32)
+    total = table_ref[...] + token_ref[...]
+    for piece in range(3):
+        total = total + rows[piece * height : (piece + 1) * height]
+    sum_ref[...] = total
+    pieces = list(split3(total))
+    if x_ref.shape[0] - start > 3 * height:
+        pieces.append(jnp.zeros((x_ref.shape[0] - start - 3 * height, 128), F32))
+    out_ref[pl.ds(start, x_ref.shape[0] - start), :] = jnp.concatenate(pieces, axis=0).astype(BF16)
+
+
+def merge(table, got, token, x):
+    height = table.shape[0]
+    return pl.pallas_call(
+        lambda *a: merge_kernel(height, COMPS * 24, *a),
+        out_shape=[jax.ShapeDtypeStruct(x.shape, x.dtype), token_shape(table)],
+        in_specs=[VM] * 4,
+        out_specs=[VM] * 2,
+        input_output_aliases={3: 0},
+        compiler_params=GRANT,
+        cost_estimate=cost(0.2),
+        name="merge",
+    )(table, got, token, x)
+
+
+def in_hbm(x):
+    return pltpu.with_memory_space_constraint(x, pltpu.HBM)
+
+
+def load_rows(height):
+    return -(-3 * height // 16) * 16
+
+
+def pack(fields, panels, flags, height):
+    whole = jax.ShapeDtypeStruct((COMPS * 64, 128), F32)
+    outs = [whole, whole]
+    outs.append(jax.ShapeDtypeStruct((COMPS * 24 + load_rows(height), 128), BF16))
+    outs.append(jax.ShapeDtypeStruct((COMPS * 24, 128), BF16))
+    outs.append(jax.ShapeDtypeStruct((height, 128), F32))
+    return pl.pallas_call(
+        pack_kernel,
+        out_shape=outs,
+        in_specs=[SM, HBM, HBM],
+        out_specs=[VM] * len(outs),
+        scratch_shapes=[
+            pltpu.VMEM((128, 128), F32),
+            pltpu.VMEM(panels.shape, jnp.int32),
+            pltpu.SemaphoreType.DMA((2,)),
+        ],
+        compiler_params=GRANT,
+        cost_estimate=cost(2),
+        name="pack",
+    )(flags, in_hbm(fields), in_hbm(panels))
+
+
+def turn_kernel(pair_x, slots, flags, r_ref, *refs):
+    sources, refs = refs[:5], refs[5:]
+    (zt_ref, *x_refs), refs = refs[: 3 - pair_x], refs[3 - pair_x :]
+    z_refs, (h_ref, row_ref, hit_ref), kept, token = refs[:2], refs[2:5], refs[5:8], refs[8]
+    react_ref, w1_ref, sems = refs[9:]
+    copies = [
+        pltpu.make_async_copy(a, b, sems.at[i])
+        for i, (a, b) in enumerate(zip(sources, (react_ref, w1_ref, *kept)))
+    ]
+    for copy in copies:
+        copy.start()
+    for c in range(0, COMPS, 2):
         lo = jnp.concatenate([r_ref[pl.ds((c + i) * 64, 24), :] for i in (0, 1)], axis=0)
         hi = jnp.concatenate([r_ref[pl.ds((c + i) * 64 + 40, 24), :] for i in (0, 1)], axis=0)
         store_layers(x_refs, c, lo, hi, flags[6])
-        lo = jnp.concatenate([row(i, y) for i in (0, 1) for y in range(3)], axis=0)
-        hi = jnp.concatenate([row(i, y) for i in (0, 1) for y in range(5, 8)], axis=0)
-        store_layers(y_refs, c, lo, hi, flags[7])
-    for ref in (*x_refs, *y_refs):
-        rows = ref.shape[0] - COMPS * 24
-        if rows:
-            pieces = [piece[j] for piece in zip(*map(split3, table)) for j in range(len(table))]
-            if rows > len(pieces):
-                pieces.append(jnp.zeros((rows - len(pieces), 128), F32))
-            ref[pl.ds(COMPS * 24, rows), :] = jnp.concatenate(pieces, axis=0).astype(BF16)
     low = half_lanes((64, 128))
     for c in range(0, COMPS, 2):
         t = jnp.transpose(r_ref[pl.ds(c * 64, 128), :])
@@ -235,39 +307,46 @@
             for m, ref in enumerate(z_refs):
                 up = flags[8] == m
                 ref[pl.ds((c + i) * 3, 3), :] = jnp.where(up, x[61:], x[:3])
-    for ref in z_refs:
-        rows = ref.shape[0] - COMPS * 3
-        ref[pl.ds(COMPS * 3, rows), :] = jnp.zeros((rows, 128), F32)
-
-
-def store_layers(refs, c, lo, hi, parity):
-    for m, ref in enumerate(refs):
-        ref[pl.ds(c * 24, 48), :] = jnp.where(parity == m, hi, lo).astype(BF16)
-
-
-def pack(fields, panels, flags, pair_x, table_rows):
-    load_rows = -(-3 * table_rows // 16) * 16
-    layer_x = jax.ShapeDtypeStruct((COMPS * 24 + (load_rows if pair_x else 0), 128), BF16)
-    layer_y = jax.ShapeDtypeStruct((COMPS * 24 + load_rows, 128), BF16)
-    edge = jax.ShapeDtypeStruct((40 + -(-table_rows // 8) * 8, 128), F32)
-    whole = jax.ShapeDtypeStruct((COMPS * 64, 128), F32)
-    outs = [whole, whole] + [layer_x] * (2 - pair_x) + [layer_y] * 2 + [edge] * 2
-    outs.append(jax.ShapeDtypeStruct((table_rows, 128), F32))
+    for ref, start in [(x, COMPS * 24) for x in x_refs] + [(z, COMPS * 3) for z in z_refs]:
+        if ref.shape[0] > start:
+            ref[pl.ds(start, ref.shape[0] - start), :] = jnp.zeros(
+                (ref.shape[0] - start, 128), ref.dtype
+            )
+    copies[0].wait()
+    copies[1].wait()
+    chem_in_kernel(slots, r_ref, react_ref, w1_ref, h_ref, row_ref, hit_ref)
+    token[...] = jnp.zeros(token.shape, F32)
+    for copy in copies[2:]:
+        copy.wait()
+
+
+def turn(flags, recon, react, layers, slots, pair_x, height):
+    def struct(like):
+        return jax.ShapeDtypeStruct(like.shape, like.dtype)
+
+    layer_x = jax.ShapeDtypeStruct((COMPS * 24 + (load_rows(height) if pair_x else 0), 128), BF16)
+    edge = jax.ShapeDtypeStruct((40 + -(-height // 8) * 8, 128), F32)
+    outs = [struct(recon)] + [layer_x] * (2 - pair_x) + [edge] * 2
+    outs += [
+        jax.ShapeDtypeStruct((layers[0].shape[1], slots), BF16),
+        jax.ShapeDtypeStruct((64, slots), BF16),
+        jax.ShapeDtypeStruct((slots, 128), BF16),
+    ]
+    outs += [struct(x) for x in layers[1:]] + [jax.ShapeDtypeStruct((height, 128), F32)]
     return pl.pallas_call(
-        lambda *a: pack_kernel(int(pair_x), *a),
+        lambda *a: turn_kernel(int(pair_x), slots, *a),
         out_shape=outs,
-        in_specs=[SM, ANY, ANY],
+        in_specs=[SM, VM] + [HBM] * 5,
         out_specs=[VM] * len(outs),
         scratch_shapes=[
-            pltpu.VMEM((128, 128), F32),
-            pltpu.VMEM(fields.shape, F32),
-            pltpu.VMEM(panels.shape, jnp.int32),
-            pltpu.SemaphoreType.DMA((2,)),
+            pltpu.VMEM(react.shape, react.dtype),
+            pltpu.VMEM(layers[0].shape, layers[0].dtype),
+            pltpu.SemaphoreType.DMA((5,)),
         ],
         compiler_params=GRANT,
         cost_estimate=cost(2),
-        name="pack",
-    )(flags, fields, panels)
+        name="turn",
+    )(flags, recon, in_hbm(react), *map(in_hbm, layers))
 
 
 def cost(us):
@@ -322,41 +401,10 @@
     h_ref[...] = jax.nn.gelu(one).astype(BF16)
 
 
-def chem_in(recon, react, layer_one, slots):
-    return pl.pallas_call(
-        lambda *a: chem_in_kernel(slots, *a),
-        out_shape=[
-            jax.ShapeDtypeStruct((layer_one.shape[1], slots), BF16),
-            jax.ShapeDtypeStruct((64, slots), BF16),
-            jax.ShapeDtypeStruct((slots, 128), BF16),
-        ],
-        in_specs=[VM] * 3,
-        out_specs=[VM] * 3,
-        compiler_params=GRANT,
-        cost_estimate=cost(2),
-        name="chem_in",
-    )(recon, react, layer_one)
-
-
-def chem_mid_kernel(h_ref, w2_ref, w3_ref, out_ref):
+def chem_kernel(h_ref, w2_ref, w3_ref, w4_ref, row_ref, hit_ref, out_ref, token):
     two = jax.nn.gelu(dot(w2_ref[...], h_ref[...])).astype(BF16)
-    out_ref[...] = jax.nn.gelu(dot(w3_ref[...], two)).astype(BF16)
-
-
-def chem_mid(hidden, layer_two, layer_three):
-    return pl.pallas_call(
-        chem_mid_kernel,
-        out_shape=jax.ShapeDtypeStruct((layer_three.shape[0], hidden.shape[1]), BF16),
-        in_specs=[VM] * 3,
-        out_specs=VM,
-        compiler_params=GRANT,
-        cost_estimate=cost(2),
-        name="chem_mid",
-    )(hidden, layer_two, layer_three)
-
-
-def chem_out_kernel(h_ref, w4_ref, row_ref, hit_ref, out_ref):
-    rates = dot(w4_ref[...], h_ref[...])
+    three = jax.nn.gelu(dot(w3_ref[...], two)).astype(BF16)
+    rates = dot(w4_ref[...], three)
     slots = rates.shape[1]
     rates = jnp.concatenate([rates, jnp.zeros((128 - COMPS, slots), F32)], axis=0)
     rates_t = jnp.transpose(rates).astype(BF16)
@@ -364,18 +412,19 @@
     for c in range(COMPS):
         spread = hit * dot(rates_t, where1(iota((128, 128), 0) == c))
         out_ref[pl.ds(c * 64, 64), :] = dot(row_slot, spread.astype(BF16))
-
-
-def chem_out(hidden, layer_four, row_slot, hit):
+    token[...] = jnp.zeros(token.shape, F32)
+
+
+def chem(hidden, layers, row_slot, hit, table):
     return pl.pallas_call(
-        chem_out_kernel,
-        out_shape=jax.ShapeDtypeStruct((COMPS * 64, 128), F32),
-        in_specs=[VM] * 4,
-        out_specs=VM,
+        chem_kernel,
+        out_shape=[jax.ShapeDtypeStruct((COMPS * 64, 128), F32), token_shape(table)],
+        in_specs=[VM] * 6,
+        out_specs=[VM] * 2,
         compiler_params=GRANT,
         cost_estimate=cost(2),
-        name="chem_out",
-    )(hidden, layer_four, row_slot, hit)
+        name="chem",
+    )(hidden, *layers, row_slot, hit)
 
 
 def halo_lines(refs, scratch, own, sign_comp, at_wall, order, second):
@@ -417,12 +466,8 @@
     token[...] = jnp.zeros(token.shape, F32)
 
 
-def flux_y_kernel(
-    count, flags, f_hbm, r_ref, acc_ref, src_ref, *refs
-):
-    layers, (out_ref, lo_s, hi_s, left, right, f_ref, sem) = refs[:count], refs[count:]
-    copy = pltpu.make_async_copy(f_hbm, f_ref, sem)
-    copy.start()
+def flux_y_kernel(count, flags, r_ref, acc_ref, *refs):
+    layers, (out_ref, lo_s, hi_s, left, right) = refs[:count], refs[count:]
 
     def own(c, y):
         return r_ref[pl.ds(c * 64 + y, 8, stride=8), :]
@@ -438,19 +483,21 @@
         )
 
     face_states(line, left, right, 9)
-    copy.wait()
 
     def emit(c, y, change):
         at = pl.ds(c * 64 + y, 8, stride=8)
-        out_ref[at, :] = (
-            f_ref[at, :] - TIME_STEP * (acc_ref[at, :] + change) + CHEM_STEP * src_ref[at, :]
-        )
+        out_ref[at, :] = acc_ref[at, :] + change
 
     line_changes(left, right, 9, 1, emit)
 
 
-def flux_z_kernel(count, flags, zt_ref, acc_ref, *refs):
-    layers, (out_ref, token, ext, left, right, back) = refs[:count], refs[count:]
+def flux_z_kernel(count, own_count, flags, f_ref, zt_ref, acc_ref, src_ref, table_ref, *refs):
+    layers, (out_hbm, impulse_ref) = refs[:count], refs[count : count + 2]
+    ext, left, right, back, out_ref, sems = refs[count + 2 :]
+    place = flags[9] * own_count
+    loads = jnp.broadcast_to(table_ref[pl.ds(place // 128, 1), :], (8, 128))
+    loads = pltpu.roll(loads, (128 - place % 128) % 128, 1)
+    impulse_ref[...] = loads[:1, :own_count] * (1.0 / (PATCH * PATCH))
     low3, low = half_lanes((3, 128)), half_lanes((64, 128))
 
     def got(c, second):
@@ -480,6 +527,7 @@
         back[pl.ds(c * 64 + z, 8, stride=8), :] = change
 
     line_changes(left, right, 9, 2, emit)
+    copies = []
     for c in range(0, COMPS, 2):
         even, odd = back[pl.ds(c * 64, 64), :], back[pl.ds(c * 64 + 64, 64), :]
         t = jnp.concatenate(
@@ -487,8 +535,12 @@
             axis=0,
         )
         at = pl.ds(c * 64, 128)
-        out_ref[at, :] = acc_ref[at, :] + jnp.transpose(t)
-    token[...] = jnp.zeros(token.shape, F32)
+        change = acc_ref[at, :] + jnp.transpose(t)
+        out_ref[at, :] = f_ref[at, :] - TIME_STEP * change + CHEM_STEP * src_ref[at, :]
+        copies.append(pltpu.make_async_copy(out_ref.at[at], out_hbm.at[at], sems.at[c // 2]))
+        copies[-1].start()
+    for copy in copies:
+        copy.wait()
 
 
 def state_scratch():
@@ -516,49 +568,50 @@
     )(flags, recon, *layers)
 
 
-def flux_y(flags, fields, recon, acc, source, layers):
+def flux_y(flags, recon, acc, layers):
     return pl.pallas_call(
         lambda *a: flux_y_kernel(len(layers), *a),
         out_shape=jax.ShapeDtypeStruct(recon.shape, F32),
-        in_specs=[SM, ANY] + [VM] * (3 + len(layers)),
+        in_specs=[SM] + [VM] * (2 + len(layers)),
         out_specs=VM,
-        scratch_shapes=halo_scratch()
-        + state_scratch()
-        + [pltpu.VMEM(fields.shape, F32), pltpu.SemaphoreType.DMA],
+        scratch_shapes=halo_scratch() + state_scratch(),
         compiler_params=GRANT,
         cost_estimate=cost(2),
         name="flux_y",
-    )(flags, fields, recon, acc, source, *layers)
-
-
-def flux_z(flags, turned, acc, layers, table):
+    )(flags, recon, acc, *layers)
+
+
+def flux_z(flags, fields, turned, acc, source, table, layers, own_count):
     return pl.pallas_call(
-        lambda *a: flux_z_kernel(len(layers), *a),
-        out_shape=[jax.ShapeDtypeStruct(acc.shape, F32), token_shape(table)],
-        in_specs=[SM] + [VM] * (2 + len(layers)),
-        out_specs=[VM] * 2,
+        lambda *a: flux_z_kernel(len(layers), own_count, *a),
+        out_shape=[
+            jax.ShapeDtypeStruct(fields.shape, F32),
+            jax.ShapeDtypeStruct((1, own_count), F32),
+        ],
+        in_specs=[SM] + [VM] * (5 + len(layers)),
+        out_specs=[HBM, VM],
         scratch_shapes=[pltpu.VMEM((COMPS * 72, 128), F32)]
         + state_scratch()
-        + [pltpu.VMEM(acc.shape, F32)],
+        + [pltpu.VMEM(fields.shape, F32)] * 2
+        + [pltpu.SemaphoreType.DMA((COMPS // 2,))],
         compiler_params=GRANT,
         cost_estimate=cost(3),
         name="flux_z",
-    )(flags, turned, acc, *layers)
-
-
-def swap(x, axis, second):
+    )(flags, fields, turned, acc, source, table, *layers)
+
+
+def swap(x, axis, second, outer=False):
     n = lax.axis_size(axis)
     pairs = [(i, i + 1) for i in range(int(second), n - 1, 2)]
-    if second and n == 4:
+    if outer:
         pairs.append((0, n - 1))
     return lax.ppermute(x, axis, [(a, b) for a, b in pairs] + [(b, a) for a, b in pairs])
 
 
-def sum_over(table, axis):
+def sum_over(table, axis, step=1):
     size = lax.axis_size(axis)
     if size & (size - 1):
         return lax.psum(table, axis)
-    step = 1
     while step < size:
         table = table + lax.ppermute(table, axis, [(i, i ^ step) for i in range(size)])
         step *= 2
@@ -580,54 +633,63 @@
     shape = fields.shape
     sizes = [lax.axis_size(a) for a in AXES]
     index = [lax.axis_index(a) for a in AXES]
+    place = (index[0] * sizes[1] + index[1]) * sizes[2] + index[2]
     flags = [f for i, n in zip(index, sizes) for f in (i == 0, i == n - 1)]
-    flags = jnp.stack([f.astype(jnp.int32) for f in flags] + [i % 2 for i in index])
+    flags = jnp.stack([f.astype(jnp.int32) for f in flags] + [i % 2 for i in index] + [place])
     pair_x = sizes[0] == 2
     panels_all = 2 * (shape[1] * sizes[0] // PATCH) * (shape[3] * sizes[2] // PATCH)
+    own = panels_all // (sizes[0] * sizes[1] * sizes[2])
     height = panels_all // 128
-    flat = fields.reshape(-1, shape[3])
-    packed = pack(flat, panel_map.reshape(-1, shape[3]), flags, pair_x, height)
-    recon, turned, table = packed[0], packed[1], packed[-1]
-    xs, ys, zs = packed[2:-5], packed[-5:-3], packed[-3:-1]
     slots = BAL * min(4, sizes[0])
     layer_rows, edge_rows = COMPS * 24, 40
-
-    got = [swap(x, "gx", m) for m, x in enumerate(xs)]
-    hidden, row_slot, hit = chem_in(recon, reacting.reshape(-1, shape[3]), layer_one.T, slots)
+    ride_y, ride_z = sizes[1] & (sizes[1] - 1) == 0, sizes[2] in (2, 4)
+
+    flat = fields.reshape(-1, shape[3])
+    flat, recon, y_first, y_second, table = pack(
+        flat, panel_map.reshape(-1, shape[3]), flags, height
+    )
+    y_got = [swap(y_first, "gy", 0)]
+    if sizes[1] > 2:
+        y_got.append(swap(y_second, "gy", 1))
+    layers = (layer_one.T, layer_two, layer_three, layer_four)
+    turned, *xs, z_first, z_second, hidden, row_slot, hit, w2, w3, w4, token = turn(
+        flags, recon, reacting.reshape(-1, shape[3]), layers, slots, pair_x, height
+    )
+    if pair_x and ride_y:
+        merged, table = merge(table, y_got[0], token, xs[0])
+        xs = [merged]
+    else:
+        table = table + token
+        if ride_y:
+            table = table + join_table(y_got[0][layer_rows:], height)
+        else:
+            table = lax.psum(table, "gy")
+        if pair_x:
+            xs = [lax.dynamic_update_slice(xs[0], split_table(table), (layer_rows, 0))]
+    x_got = [swap(x, "gx", m) for m, x in enumerate(xs)]
+    source, token = chem(hidden, (w2, w3, w4), row_slot, hit, table)
     if pair_x:
-        table = table + join_table(got[0][layer_rows:], height)
+        table = table + join_table(x_got[0][layer_rows:], height)
     else:
         table = sum_over(table, "gx")
-    ride_z, ride_y = sizes[2] in (2, 4), sizes[1] in (2, 4)
+    table = table + token
     if not ride_z:
         table = sum_over(table, "gz")
-    z_got = [swap(lax.dynamic_update_slice(zs[0], table, (edge_rows, 0)), "gz", 0)]
-    acc, token = flux_x(flags, recon, got, table)
+    z_got = [swap(lax.dynamic_update_slice(z_first, table, (edge_rows, 0)), "gz", 0)]
     if ride_z:
-        table = table + z_got[0][edge_rows : edge_rows + height] + token
+        table = table + z_got[0][edge_rows : edge_rows + height]
     if sizes[2] > 2:
-        z_got.append(swap(lax.dynamic_update_slice(zs[1], table, (edge_rows, 0)), "gz", 1))
+        z_second = lax.dynamic_update_slice(z_second, table, (edge_rows, 0))
+        z_got.append(swap(z_second, "gz", 1, ride_z))
         if ride_z:
             table = table + z_got[1][edge_rows : edge_rows + height]
-    hidden = chem_mid(hidden, layer_two, layer_three)
-    if not ride_y:
-        table = sum_over(table, "gy")
-    y_got = [swap(lax.dynamic_update_slice(ys[0], split_table(table), (layer_rows, 0)), "gy", 0)]
-    acc, token = flux_z(flags, turned, acc, z_got, table)
+    acc, token = flux_x(flags, recon, x_got, table)
+    table = table + token
     if ride_y:
-        table = table + join_table(y_got[0][layer_rows:], height) + token
-    if sizes[1] > 2:
-        y_got.append(
-            swap(lax.dynamic_update_slice(ys[1], split_table(table), (layer_rows, 0)), "gy", 1)
-        )
-        if ride_y:
-            table = table + join_table(y_got[1][layer_rows:], height)
-    source = chem_out(hidden, layer_four, row_slot, hit)
-    new = flux_y(flags, flat, recon, acc, source, y_got)
-    own = panels_all // (sizes[0] * sizes[1] * sizes[2])
-    place = (index[0] * sizes[1] + index[1]) * sizes[2] + index[2]
-    result = lax.dynamic_slice_in_dim(table.reshape(-1), place * own, own)
-    return new.reshape(shape), result / float(PATCH * PATCH)
+        table = sum_over(table, "gy", 2)
+    acc = flux_y(flags, recon, acc, y_got)
+    new, impulse = flux_z(flags, flat, turned, acc, source, table, z_got, own)
+    return new.reshape(shape), impulse.reshape(own)
 
 
 def solution(mesh):

time: 34.6 us -> 28.9 us (0.84)
  local copies, waits for them, and re-layouts: 5.34 us -> 0.09 us
  Pallas kernels: 11.6 us -> 15.5 us
  waiting for transfers between devices: 4.84 us -> 1.2 us
  other arithmetic: 0.7 us -> 0.04 us
    unnamed x16 -> x0, local copies, waits for them, and re-layouts: 5.02 us -> none
    pallas_call x5, Pallas kernels: 6.91 us -> 11.9 us  [the longest x1 3.83 us: chem(): pl.pallas_call(chem_kernel, out_shape=[jax.ShapeDtypeStruct((COMPS * 64,...]
    ppermute x0 -> x1, starting transfers between devices: none -> 4.35 us  [sum_over(): lax.ppermute(table, axis, [(i, i ^ step) for i in range(size)])]
    ppermute x5, starting transfers between devices: 10.9 us -> 6.83 us  [swap(): lax.ppermute(x, axis, [(a, b) for a, b in pairs] + [(b, a) for a, b in pa...]
    ppermute x5, waiting for transfers between devices: 4.84 us -> 1.19 us  [swap(): lax.ppermute(x, axis, [(a, b) for a, b in pairs] + [(b, a) for a, b in pa...]
    pallas_call x1, Pallas kernels: 3.03 us -> 1.87 us  [flux_y(): pl.pallas_call(lambda *a: flux_y_kernel(len(layers), *a), out_shape=jax.S...]
    div x1 -> x0, other arithmetic: 0.59 us -> none  [body(): return (new.reshape(shape), result / float(PATCH * PATCH))]
  transfers between devices with their start and end apart: 5 -> 6, of which waited for: 3 -> 1; matrix products, arithmetic and copies ran while one was open for 0% -> 0% of each run, Pallas kernels for 21% -> 35%
where the time goes in v3:
time: 28.9 us; the launch traced here: 28.7 us
  Pallas kernels  15.5 us (54%)
  starting transfers between devices  11.2 us (39%)
  waiting for transfers between devices  1.2 us (4%)
  between operations  0.77 us (3%)
    ppermute x5, starting transfers between devices, swap(): lax.ppermute(x, axis, [(a, b) for a, b in pairs] + [(b, a) for a, b in pa...  6.83 us
    ppermute x1, starting transfers between devices, sum_over(): lax.ppermute(table, axis, [(i, i ^ step) for i in range(size)])  4.35 us
    pallas_call x1, Pallas kernels, chem(): pl.pallas_call(chem_kernel, out_shape=[jax.ShapeDtypeStruct((COMPS * 64,...  3.83 us
    pallas_call x1, Pallas kernels, flux_z(): pl.pallas_call(lambda *a: flux_z_kernel(len(layers), own_count, *a), out_...  3.3 us
    pallas_call x1, Pallas kernels, turn(): pl.pallas_call(lambda *a: turn_kernel(int(pair_x), slots, *a), out_shape=...  2.65 us
    pallas_call x1, Pallas kernels, pack(): pl.pallas_call(pack_kernel, out_shape=outs, in_specs=[SM, HBM, HBM], out_...  2.1 us
    pallas_call x1, Pallas kernels, flux_y(): pl.pallas_call(lambda *a: flux_y_kernel(len(layers), *a), out_shape=jax.S...  1.87 us
    pallas_call x1, Pallas kernels, flux_x(): pl.pallas_call(lambda *a: flux_x_kernel(len(layers), *a), out_shape=[jax....  1.69 us
  transfers between devices with their start and end apart: 6, of which 1 were waited for; matrix products, arithmetic and copies ran while one was open for 0% of the time, Pallas kernels for 35%

profile of v3, /device:TPU:0, one launch (start us, length us, event | category | flops | bytes accessed | tf_op | source)
XLA Modules:
  0.0 28.7 jit_solution(8026272646495706696)
XLA Ops:
  0.7 0.1 stack.67.flags.a_0_
  0.8 2.1 %pack.1 = (f32[768,128]{1,0:T(8,128)S(1)}, f32[768,128]{1,0:T(8,128)S(1)}, bf16[304,128]{1,0:T(8,128)(2,1)S(1)}, bf16[288,128]{1,0:T(8,128)(2,1)S(1)}, f32[2,128]{1,0:T(2,128)S(1)}) custom-call(s32[10]{0:T(128)S(1)} %stack.67.flags.a_0_, f32[768,128]{1,0:T(8,128)} %bitcast.16, s32[16,128]{1,0:T(8,128)} %bitcast.19), custom_call_target="tpu_custom_call" | custom-call | bytes 7000000 | tf_op jit(solution)/shard_map/pack/pallas_call | solution.py:268
  2.9 3.1 %collective-permute-start = (bf16[304,128]{1,0:T(8,128)(2,1)S(1)}, bf16[304,128]{1,0:T(8,128)(2,1)S(1)}, u32[]{:S(2)}, u32[]{:S(2)}) collective-permute-start(bf16[304,128]{1,0:T(8,128)(2,1)S(1)} %get-tuple-element.30), channel_id=1, source_target_pairs={{0,4},{8,12},{4,0},{12,8},{1,5},{9,13},{5,1},{13,9},{2,6},{10,14},... | collective-permute-start | bytes 233480 | tf_op jit(solution)/shard_map/ppermute | solution.py:608
  6.0 2.7 %turn.1 = (f32[768,128]{1,0:T(8,128)S(1)}, bf16[304,128]{1,0:T(8,128)(2,1)S(1)}, f32[48,128]{1,0:T(8,128)S(1)}, f32[48,128]{1,0:T(8,128)S(1)}, bf16[1600,128]{1,...) custom-call(s32[10]{0:T(128)S(1)} %stack.67.flags.a_0_, ...), custom_call_target="tpu_custom_call" | custom-call | bytes 7000000 | tf_op jit(solution)/shard_map/turn/pallas_call | solution.py:336
  8.6 0.0 collective-permute-done.a_1_.a_3_
  8.7 1.7 %collective-permute-start.1 = (bf16[304,128]{1,0:T(8,128)(2,1)S(1)}, bf16[304,128]{1,0:T(8,128)(2,1)S(1)}, u32[]{:S(2)}, u32[]{:S(2)}) collective-permute-start(bf16[304,128]{1,0:T(8,128)(2,1)S(1)} %get-tuple-element.33), channel_id=1, source_target_pairs={{0,16},{16,0},{1,17},{17,1},{2,18},{18,2},{3,19},{19,3},{4,20},{20... | collective-permute-start | bytes 233480 | tf_op jit(solution)/shard_map/ppermute | solution.py:608
  10.4 3.8 %chem.1 = (f32[768,128]{1,0:T(8,128)S(1)}, f32[2,128]{1,0:T(2,128)S(1)}) custom-call(bf16[1600,128]{1,0:T(8,128)(2,1)S(1)} %get-tuple-element.36.h_ref, bf16[800,1600]{1,0:T(8,128)(2,1)S(1)} %get-tuple-element.37.w2_ref, bf16[400,800]{1,0:T(8,128)(2,1)S(1)} %get-tuple-element.38.w3_ref, bf16[12,400]{1,0:T(8,128)(2,1)S(1)} %get-tuple-element.39.w4_ref, ...), custom_call_target="tpu_custom_call" | custom-call | bytes 7000000 | tf_op jit(solution)/shard_map/chem/pallas_call | solution.py:419
  14.2 0.0 collective-permute-done.1.a_2_
  14.2 0.1 collective-permute-start.3
  14.3 1.2 %collective-permute-done.3.a_6_ = f32[48,128]{1,0:T(8,128)S(1)} collective-permute-done((f32[48,128]{1,0:T(8,128)S(1)}, f32[48,128]{1,0:T(8,128)S(1)}, u32[]{:S(2)}, u32[]{:S(2)}) %collective-permute-start.3) | collective-permute-done | bytes 24608 | tf_op jit(solution)/shard_map/ppermute | solution.py:608
  15.5 1.3 %collective-permute-start.4 = (f32[48,128]{1,0:T(8,128)S(1)}, f32[48,128]{1,0:T(8,128)S(1)}, u32[]{:S(2)}, u32[]{:S(2)}) collective-permute-start(f32[48,128]{1,0:T(8,128)S(1)} %constant_dynamic-update-slice_fusion), channel_id=1, source_target_pairs={{1,2},{0,3},{2,1},{3,0},{5,6},{4,7},{6,5},{7,4},{9,10},{8,11},{10,... | collective-permute-start | bytes 73736 | tf_op jit(solution)/shard_map/ppermute | solution.py:608
  16.8 0.7 %collective-permute-start.2 = (bf16[288,128]{1,0:T(8,128)(2,1)S(1)}, bf16[288,128]{1,0:T(8,128)(2,1)S(1)}, u32[]{:S(2)}, u32[]{:S(2)}) collective-permute-start(bf16[288,128]{1,0:T(8,128)(2,1)S(1)} %get-tuple-element.35), channel_id=1, source_target_pairs={{4,8},{8,4},{5,9},{9,5},{6,10},{10,6},{7,11},{11,7},{20,24},{24,20... | collective-permute-start | bytes 221192 | tf_op jit(solution)/shard_map/ppermute | solution.py:608
  17.5 1.7 %flux_x.1 = (f32[768,128]{1,0:T(8,128)S(1)}, f32[2,128]{1,0:T(2,128)S(1)}) custom-call(s32[10]{0:T(128)S(1)} %stack.67.flags.a_0_, f32[768,128]{1,0:T(8,128)S(1)} %get-tuple-element.27.a_1_, bf16[304,128]{1,0:T(8,128)(2,1)S(1)} %collective-permute-done.1.a_2_), custom_call_target="tpu_custom_call" | custom-call | bytes 7000000 | tf_op jit(solution)/shard_map/flux_x/pallas_call | solution.py:559
  19.2 0.0 collective-permute-done.4.a_7_
  19.2 4.3 %collective-permute-start.5 = (f32[2,128]{1,0:T(2,128)S(1)}, f32[2,128]{1,0:T(2,128)S(1)}, u32[]{:S(2)}, u32[]{:S(2)}) collective-permute-start(f32[2,128]{1,0:T(2,128)S(1)} %fusion), channel_id=1, source_target_pairs={{0,8},{4,12},{8,0},{12,4},{1,9},{5,13},{9,1},{13,5},{2,10},{6,14},... | collective-permute-start | bytes 3080 | tf_op jit(solution)/shard_map/ppermute | solution.py:616
  23.5 0.0 collective-permute-done.2.a_4_
  23.5 1.9 %flux_y.1.a_3_ = f32[768,128]{1,0:T(8,128)S(1)} custom-call(s32[10]{0:T(128)S(1)} %stack.67.flags.a_0_, f32[768,128]{1,0:T(8,128)S(1)} %get-tuple-element.27.a_1_, f32[768,128]{1,0:T(8,128)S(1)} %get-tuple-element.34.a_2_, bf16[304,128]{1,0:T(8,128)(2,1)S(1)} %collective-permute-done.a_1_.a_3_, bf16[288,128]{1,0:T(8,128)(2,1)S(1)} %collective-permute-done.2.a_4_), custom_call_target="tpu_custom_call" | custom-call | bytes 7000000 | tf_op jit(solution)/shard_map/flux_y/pallas_call | solution.py:572
  25.4 0.0 collective-permute-done.5
  25.4 3.3 %flux_z.1 = (f32[768,128]{1,0:T(8,128)}, f32[1,8]{1,0:T(1,128)}) custom-call(s32[10]{0:T(128)S(1)} %stack.67.flags.a_0_, f32[768,128]{1,0:T(8,128)S(1)} %get-tuple-element.26.a_1_, f32[768,128]{1,0:T(8,128)S(1)} %get-tuple-element.28.a_2_, f32[768,128]{1,0:T(8,128)S(1)} %flux_y.1.a_3_, f32[768,128]{1,0:T(8,128)S(1)} %get-tuple-element.42.a_4_, ...), custom_call_target="tpu_custom_call" | custom-call | bytes 10500000 | tf_op jit(solution)/shard_map/flux_z/pallas_call | solution.py:585
  (6 shorter events, 0.1 us)
Async XLA Ops:
  2.9 5.8 %collective-permute-start = (bf16[304,128]{1,0:T(8,128)(2,1)S(1)}, bf16[304,128]{1,0:T(8,128)(2,1)S(1)}, u32[]{:S(2)}, u32[]{:S(2)}) collective-permute-start(bf16[304,128]{1,0:T(8,128)(2,1)S(1)} %get-tuple-element.30), channel_id=1, source_target_pairs={{0,4},{8,12},{4,0},{12,8},{1,5},{9,13},{5,1},{13,9},{2,6},{10,14},... | collective-permute-start | bytes 233480 | tf_op jit(solution)/shard_map/ppermute | solution.py:608
  8.7 5.5 %collective-permute-start.1 = (bf16[304,128]{1,0:T(8,128)(2,1)S(1)}, bf16[304,128]{1,0:T(8,128)(2,1)S(1)}, u32[]{:S(2)}, u32[]{:S(2)}) collective-permute-start(bf16[304,128]{1,0:T(8,128)(2,1)S(1)} %get-tuple-element.33), channel_id=1, source_target_pairs={{0,16},{16,0},{1,17},{17,1},{2,18},{18,2},{3,19},{19,3},{4,20},{20... | collective-permute-start | bytes 233480 | tf_op jit(solution)/shard_map/ppermute | solution.py:608
  14.2 1.3 %collective-permute-start.3 = (f32[48,128]{1,0:T(8,128)S(1)}, f32[48,128]{1,0:T(8,128)S(1)}, u32[]{:S(2)}, u32[]{:S(2)}) collective-permute-start(f32[48,128]{1,0:T(8,128)S(1)} %get-tuple-element.50), channel_id=1, source_target_pairs={{0,1},{2,3},{1,0},{3,2},{4,5},{6,7},{5,4},{7,6},{8,9},{10,11},{9,8... | collective-permute-start | bytes 73736 | tf_op jit(solution)/shard_map/ppermute | solution.py:608
  15.5 3.6 %collective-permute-start.4 = (f32[48,128]{1,0:T(8,128)S(1)}, f32[48,128]{1,0:T(8,128)S(1)}, u32[]{:S(2)}, u32[]{:S(2)}) collective-permute-start(f32[48,128]{1,0:T(8,128)S(1)} %constant_dynamic-update-slice_fusion), channel_id=1, source_target_pairs={{1,2},{0,3},{2,1},{3,0},{5,6},{4,7},{6,5},{7,4},{9,10},{8,11},{10,... | collective-permute-start | bytes 73736 | tf_op jit(solution)/shard_map/ppermute | solution.py:608
  16.8 6.7 %collective-permute-start.2 = (bf16[288,128]{1,0:T(8,128)(2,1)S(1)}, bf16[288,128]{1,0:T(8,128)(2,1)S(1)}, u32[]{:S(2)}, u32[]{:S(2)}) collective-permute-start(bf16[288,128]{1,0:T(8,128)(2,1)S(1)} %get-tuple-element.35), channel_id=1, source_target_pairs={{4,8},{8,4},{5,9},{9,5},{6,10},{10,6},{7,11},{11,7},{20,24},{24,20... | collective-permute-start | bytes 221192 | tf_op jit(solution)/shard_map/ppermute | solution.py:608
  19.2 6.2 %collective-permute-start.5 = (f32[2,128]{1,0:T(2,128)S(1)}, f32[2,128]{1,0:T(2,128)S(1)}, u32[]{:S(2)}, u32[]{:S(2)}) collective-permute-start(f32[2,128]{1,0:T(2,128)S(1)} %fusion), channel_id=1, source_target_pairs={{0,8},{4,12},{8,0},{12,4},{1,9},{5,13},{9,1},{13,5},{2,10},{6,14},... | collective-permute-start | bytes 3080 | tf_op jit(solution)/shard_map/ppermute | solution.py:616

commit v4 on v3

--- a/solution.py
+++ b/solution.py
@@ -4,6 +4,7 @@
 from jax.experimental import pallas as pl
 from jax.experimental.pallas import tpu as pltpu
 from jax.sharding import PartitionSpec as P
+
 
 BAL = 64
 COMPS = 12
@@ -19,7 +20,6 @@
 BF16 = jnp.bfloat16
 GRANT = pltpu.CompilerParams(vmem_limit_bytes=12 * 2**20)
 VM = pl.BlockSpec(memory_space=pltpu.VMEM)
-SM = pl.BlockSpec(memory_space=pltpu.SMEM)
 HBM = pl.BlockSpec(memory_space=pltpu.HBM)
 
 
@@ -102,6 +102,14 @@
     return flux
 
 
+def place_flags():
+    sizes = [lax.axis_size(a) for a in AXES]
+    index = [lax.axis_index(a) for a in AXES]
+    place = (index[0] * sizes[1] + index[1]) * sizes[2] + index[2]
+    flags = [f for i, n in zip(index, sizes) for f in (i == 0, i == n - 1)]
+    return flags + [lax.rem(i, 2) for i in index] + [place]
+
+
 def rows8(index):
     return pl.ds(pl.multiple_of(index * 8, 8), 8)
 
@@ -143,13 +151,21 @@
     return hi, mid, x - hi - mid
 
 
-def pack_kernel(flags, f_hbm, map_hbm, f_ref, r_ref, y1_ref, y2_ref, table_ref, buf, map_ref, sems):
-    copies = [
-        pltpu.make_async_copy(f_hbm, f_ref, sems.at[0]),
-        pltpu.make_async_copy(map_hbm, map_ref, sems.at[1]),
-    ]
+def fetch(pairs, sems):
+    copies = [pltpu.make_async_copy(a, b, sems.at[i]) for i, (a, b) in enumerate(pairs)]
     for copy in copies:
         copy.start()
+    return copies
+
+
+def pack_kernel(*refs):
+    f_hbm, map_hbm, *sources = refs[:7]
+    f_ref, r_ref, y1_ref, y2_ref, table_ref, *kept = refs[7:17]
+    buf, map_ref, sems = refs[17:]
+    half = kept[2].shape[0]
+    sources[2] = sources[2].at[pl.ds(0, half)]
+    copies = fetch([(f_hbm, f_ref), (map_hbm, map_ref), *zip(sources, kept)], sems)
+    flags = place_flags()
     copies[0].wait()
     for x in range(8):
         def at(c):
@@ -177,7 +193,7 @@
         out_speed = -state[1] if wall == 0 else state[1]
         speed = jnp.abs(out_speed) + jnp.sqrt(HEAT_RATIO * p / rho)
         push = p + rho * out_speed * (out_speed + speed)
-        x = jnp.where(flags[2 + wall] == 1, push, 0.0)
+        x = jnp.where(flags[2 + wall], push, 0.0)
         for s in (1, 2, 4):
             x = x + pltpu.roll(x, 128 - s, 1)
         for s in (1, 2):
@@ -217,6 +233,8 @@
     if rows > len(pieces):
         pieces.append(jnp.zeros((rows - len(pieces), 128), F32))
     y1_ref[pl.ds(COMPS * 24, rows), :] = jnp.concatenate(pieces, axis=0).astype(BF16)
+    for copy in copies[2:]:
+        copy.wait()
 
 
 def store_layers(refs, c, lo, hi, parity):
@@ -224,31 +242,27 @@
         ref[pl.ds(c * 24, 48), :] = jnp.where(parity == m, hi, lo).astype(BF16)
 
 
-def merge_kernel(height, start, table_ref, got_ref, token_ref, x_ref, out_ref, sum_ref):
-    rows = got_ref[pl.ds(COMPS * 24, 8), :] if height == 2 else got_ref[pl.ds(COMPS * 24, 3 * height), :]
-    rows = rows.astype(F32)
-    total = table_ref[...] + token_ref[...]
-    for piece in range(3):
-        total = total + rows[piece * height : (piece + 1) * height]
-    sum_ref[...] = total
-    pieces = list(split3(total))
-    if x_ref.shape[0] - start > 3 * height:
-        pieces.append(jnp.zeros((x_ref.shape[0] - start - 3 * height, 128), F32))
-    out_ref[pl.ds(start, x_ref.shape[0] - start), :] = jnp.concatenate(pieces, axis=0).astype(BF16)
-
-
-def merge(table, got, token, x):
-    height = table.shape[0]
-    return pl.pallas_call(
-        lambda *a: merge_kernel(height, COMPS * 24, *a),
-        out_shape=[jax.ShapeDtypeStruct(x.shape, x.dtype), token_shape(table)],
-        in_specs=[VM] * 4,
-        out_specs=[VM] * 2,
-        input_output_aliases={3: 0},
+def put_table_kernel(table_ref, x_ref, out_ref):
+    start = COMPS * 24
+    rows = x_ref.shape[0] - start
+    pieces = list(split3(table_ref[...]))
+    used = 3 * table_ref.shape[0]
+    if rows > used:
+        pieces.append(jnp.zeros((rows - used, 128), F32))
+    out_ref[pl.ds(start, rows), :] = jnp.concatenate(pieces, axis=0).astype(BF16)
+
+
+def put_table(table, x):
+    return pl.pallas_call(
+        put_table_kernel,
+        out_shape=jax.ShapeDtypeStruct(x.shape, x.dtype),
+        in_specs=[VM] * 2,
+        out_specs=VM,
+        input_output_aliases={1: 0},
         compiler_params=GRANT,
         cost_estimate=cost(0.2),
-        name="merge",
-    )(table, got, token, x)
+        name="put_table",
+    )(table, x)
 
 
 def in_hbm(x):
@@ -259,39 +273,36 @@
     return -(-3 * height // 16) * 16
 
 
-def pack(fields, panels, flags, height):
+def pack(fields, panels, react, layers, height):
     whole = jax.ShapeDtypeStruct((COMPS * 64, 128), F32)
     outs = [whole, whole]
     outs.append(jax.ShapeDtypeStruct((COMPS * 24 + load_rows(height), 128), BF16))
     outs.append(jax.ShapeDtypeStruct((COMPS * 24, 128), BF16))
     outs.append(jax.ShapeDtypeStruct((height, 128), F32))
+    one, two, three, four = layers
+    kept = [jax.ShapeDtypeStruct(x.shape, x.dtype) for x in (react, one, two, three, four)]
+    kept[2] = jax.ShapeDtypeStruct((two.shape[0] // 2, two.shape[1]), two.dtype)
+    outs += kept
     return pl.pallas_call(
         pack_kernel,
         out_shape=outs,
-        in_specs=[SM, HBM, HBM],
+        in_specs=[HBM] * 7,
         out_specs=[VM] * len(outs),
         scratch_shapes=[
             pltpu.VMEM((128, 128), F32),
             pltpu.VMEM(panels.shape, jnp.int32),
-            pltpu.SemaphoreType.DMA((2,)),
+            pltpu.SemaphoreType.DMA((7,)),
         ],
         compiler_params=GRANT,
         cost_estimate=cost(2),
         name="pack",
-    )(flags, in_hbm(fields), in_hbm(panels))
-
-
-def turn_kernel(pair_x, slots, flags, r_ref, *refs):
-    sources, refs = refs[:5], refs[5:]
-    (zt_ref, *x_refs), refs = refs[: 3 - pair_x], refs[3 - pair_x :]
-    z_refs, (h_ref, row_ref, hit_ref), kept, token = refs[:2], refs[2:5], refs[5:8], refs[8]
-    react_ref, w1_ref, sems = refs[9:]
-    copies = [
-        pltpu.make_async_copy(a, b, sems.at[i])
-        for i, (a, b) in enumerate(zip(sources, (react_ref, w1_ref, *kept)))
-    ]
-    for copy in copies:
-        copy.start()
+    )(*map(in_hbm, (fields, panels, react, *layers)))
+
+
+def turn_kernel(pair_x, r_ref, zt_ref, *refs):
+    x_refs, (z1_ref, z2_ref, token) = refs[: 2 - pair_x], refs[2 - pair_x :]
+    z_refs = (z1_ref, z2_ref)
+    flags = place_flags()
     for c in range(0, COMPS, 2):
         lo = jnp.concatenate([r_ref[pl.ds((c + i) * 64, 24), :] for i in (0, 1)], axis=0)
         hi = jnp.concatenate([r_ref[pl.ds((c + i) * 64 + 40, 24), :] for i in (0, 1)], axis=0)
@@ -312,41 +323,23 @@
             ref[pl.ds(start, ref.shape[0] - start), :] = jnp.zeros(
                 (ref.shape[0] - start, 128), ref.dtype
             )
-    copies[0].wait()
-    copies[1].wait()
-    chem_in_kernel(slots, r_ref, react_ref, w1_ref, h_ref, row_ref, hit_ref)
     token[...] = jnp.zeros(token.shape, F32)
-    for copy in copies[2:]:
-        copy.wait()
-
-
-def turn(flags, recon, react, layers, slots, pair_x, height):
-    def struct(like):
-        return jax.ShapeDtypeStruct(like.shape, like.dtype)
-
+
+
+def turn(recon, pair_x, height):
     layer_x = jax.ShapeDtypeStruct((COMPS * 24 + (load_rows(height) if pair_x else 0), 128), BF16)
     edge = jax.ShapeDtypeStruct((40 + -(-height // 8) * 8, 128), F32)
-    outs = [struct(recon)] + [layer_x] * (2 - pair_x) + [edge] * 2
-    outs += [
-        jax.ShapeDtypeStruct((layers[0].shape[1], slots), BF16),
-        jax.ShapeDtypeStruct((64, slots), BF16),
-        jax.ShapeDtypeStruct((slots, 128), BF16),
-    ]
-    outs += [struct(x) for x in layers[1:]] + [jax.ShapeDtypeStruct((height, 128), F32)]
-    return pl.pallas_call(
-        lambda *a: turn_kernel(int(pair_x), slots, *a),
+    outs = [jax.ShapeDtypeStruct(recon.shape, F32)] + [layer_x] * (2 - pair_x) + [edge] * 2
+    outs.append(jax.ShapeDtypeStruct((height, 128), F32))
+    return pl.pallas_call(
+        lambda *a: turn_kernel(int(pair_x), *a),
         out_shape=outs,
-        in_specs=[SM, VM] + [HBM] * 5,
+        in_specs=[VM],
         out_specs=[VM] * len(outs),
-        scratch_shapes=[
-            pltpu.VMEM(react.shape, react.dtype),
-            pltpu.VMEM(layers[0].shape, layers[0].dtype),
-            pltpu.SemaphoreType.DMA((5,)),
-        ],
-        compiler_params=GRANT,
-        cost_estimate=cost(2),
+        compiler_params=GRANT,
+        cost_estimate=cost(1),
         name="turn",
-    )(flags, recon, in_hbm(react), *map(in_hbm, layers))
+    )(recon)
 
 
 def cost(us):
@@ -365,7 +358,11 @@
     return jnp.where(mask, 1.0, 0.0).astype(BF16)
 
 
-def chem_in_kernel(slots, r_ref, react_ref, w1_ref, h_ref, row_ref, hit_ref):
+def chem_in_kernel(
+    slots, r_ref, react_ref, w1_ref, w2_hbm, h_ref, row_ref, hit_ref, w2_ref, token, sems
+):
+    half = w2_ref.shape[0]
+    (copy,) = fetch([(w2_hbm.at[pl.ds(half, half)], w2_ref)], sems)
     react = react_ref[...].astype(F32)
     react_b = react.astype(BF16)
     upper = where1(iota((128, 128), 0) <= iota((128, 128), 1))
@@ -399,12 +396,53 @@
     tn = (((0,), (0,)), ((), ()))
     one = lax.dot_general(w1_ref[...], feat, tn, preferred_element_type=F32)
     h_ref[...] = jax.nn.gelu(one).astype(BF16)
-
-
-def chem_kernel(h_ref, w2_ref, w3_ref, w4_ref, row_ref, hit_ref, out_ref, token):
-    two = jax.nn.gelu(dot(w2_ref[...], h_ref[...])).astype(BF16)
-    three = jax.nn.gelu(dot(w3_ref[...], two)).astype(BF16)
-    rates = dot(w4_ref[...], three)
+    token[...] = jnp.zeros(token.shape, F32)
+    copy.wait()
+
+
+def chem_in(recon, react, layer_one, layer_two, slots, table):
+    return pl.pallas_call(
+        lambda *a: chem_in_kernel(slots, *a),
+        out_shape=[
+            jax.ShapeDtypeStruct((layer_one.shape[1], slots), BF16),
+            jax.ShapeDtypeStruct((64, slots), BF16),
+            jax.ShapeDtypeStruct((slots, 128), BF16),
+            jax.ShapeDtypeStruct((layer_two.shape[0] // 2, layer_two.shape[1]), BF16),
+            token_shape(table),
+        ],
+        in_specs=[VM] * 3 + [HBM],
+        out_specs=[VM] * 5,
+        scratch_shapes=[pltpu.SemaphoreType.DMA((1,))],
+        compiler_params=GRANT,
+        cost_estimate=cost(1),
+        name="chem_in",
+    )(recon, react, layer_one, in_hbm(layer_two))
+
+
+def chem_mid_kernel(h_ref, w2_ref, w2b_ref, w3_ref, out_ref, token):
+    two = [jax.nn.gelu(dot(w[...], h_ref[...])).astype(BF16) for w in (w2_ref, w2b_ref)]
+    two = jnp.concatenate(two, axis=0)
+    out_ref[...] = jax.nn.gelu(dot(w3_ref[...], two)).astype(BF16)
+    token[...] = jnp.zeros(token.shape, F32)
+
+
+def chem_mid(hidden, halves, layer_three, table):
+    return pl.pallas_call(
+        chem_mid_kernel,
+        out_shape=[
+            jax.ShapeDtypeStruct((layer_three.shape[0], hidden.shape[1]), BF16),
+            token_shape(table),
+        ],
+        in_specs=[VM] * 4,
+        out_specs=[VM] * 2,
+        compiler_params=GRANT,
+        cost_estimate=cost(2),
+        name="chem_mid",
+    )(hidden, *halves, layer_three)
+
+
+def chem_out_kernel(h_ref, w4_ref, row_ref, hit_ref, out_ref, token):
+    rates = dot(w4_ref[...], h_ref[...])
     slots = rates.shape[1]
     rates = jnp.concatenate([rates, jnp.zeros((128 - COMPS, slots), F32)], axis=0)
     rates_t = jnp.transpose(rates).astype(BF16)
@@ -415,16 +453,16 @@
     token[...] = jnp.zeros(token.shape, F32)
 
 
-def chem(hidden, layers, row_slot, hit, table):
-    return pl.pallas_call(
-        chem_kernel,
+def chem_out(hidden, layer_four, row_slot, hit, table):
+    return pl.pallas_call(
+        chem_out_kernel,
         out_shape=[jax.ShapeDtypeStruct((COMPS * 64, 128), F32), token_shape(table)],
-        in_specs=[VM] * 6,
+        in_specs=[VM] * 4,
         out_specs=[VM] * 2,
         compiler_params=GRANT,
-        cost_estimate=cost(2),
-        name="chem",
-    )(hidden, *layers, row_slot, hit)
+        cost_estimate=cost(1),
+        name="chem_out",
+    )(hidden, layer_four, row_slot, hit)
 
 
 def halo_lines(refs, scratch, own, sign_comp, at_wall, order, second):
@@ -441,14 +479,15 @@
                 scratch[pl.ds(((c + i) * 3 + k) * 8, 8), :] = jnp.where(at_wall, mirror, got)
 
 
-def flux_x_kernel(count, flags, r_ref, *refs):
+def flux_x_kernel(count, r_ref, acc_ref, *refs):
+    flags = place_flags()
     layers, (out_ref, token, lo_s, hi_s, left, right) = refs[:count], refs[count:]
 
     def own(c, x):
         return r_ref[pl.ds(c * 64 + x * 8, 8), :]
 
-    halo_lines(layers, lo_s, own, 1, flags[0] == 1, (2, 1, 0), flags[6] == 0)
-    halo_lines(layers, hi_s, own, 1, flags[1] == 1, (7, 6, 5), flags[6] == 1)
+    halo_lines(layers, lo_s, own, 1, flags[0], (2, 1, 0), flags[6] == 0)
+    halo_lines(layers, hi_s, own, 1, flags[1], (7, 6, 5), flags[6] == 1)
 
     def line(c):
         return (
@@ -460,20 +499,22 @@
     face_states(line, left, right, 9)
 
     def emit(c, x, change):
-        out_ref[pl.ds(c * 64 + x * 8, 8), :] = change
+        at = pl.ds(c * 64 + x * 8, 8)
+        out_ref[at, :] = acc_ref[at, :] + change
 
     line_changes(left, right, 9, 0, emit)
     token[...] = jnp.zeros(token.shape, F32)
 
 
-def flux_y_kernel(count, flags, r_ref, acc_ref, *refs):
-    layers, (out_ref, lo_s, hi_s, left, right) = refs[:count], refs[count:]
+def flux_y_kernel(count, r_ref, *refs):
+    flags = place_flags()
+    layers, (out_ref, token, lo_s, hi_s, left, right) = refs[:count], refs[count:]
 
     def own(c, y):
         return r_ref[pl.ds(c * 64 + y, 8, stride=8), :]
 
-    halo_lines(layers, lo_s, own, 2, flags[2] == 1, (2, 1, 0), flags[7] == 0)
-    halo_lines(layers, hi_s, own, 2, flags[3] == 1, (7, 6, 5), flags[7] == 1)
+    halo_lines(layers, lo_s, own, 2, flags[2], (2, 1, 0), flags[7] == 0)
+    halo_lines(layers, hi_s, own, 2, flags[3], (7, 6, 5), flags[7] == 1)
 
     def line(c):
         return (
@@ -485,15 +526,16 @@
     face_states(line, left, right, 9)
 
     def emit(c, y, change):
-        at = pl.ds(c * 64 + y, 8, stride=8)
-        out_ref[at, :] = acc_ref[at, :] + change
+        out_ref[pl.ds(c * 64 + y, 8, stride=8), :] = change
 
     line_changes(left, right, 9, 1, emit)
-
-
-def flux_z_kernel(count, own_count, flags, f_ref, zt_ref, acc_ref, src_ref, table_ref, *refs):
+    token[...] = jnp.zeros(token.shape, F32)
+
+
+def flux_z_kernel(count, own_count, f_ref, zt_ref, acc_ref, src_ref, table_ref, *refs):
     layers, (out_hbm, impulse_ref) = refs[:count], refs[count : count + 2]
     ext, left, right, back, out_ref, sems = refs[count + 2 :]
+    flags = place_flags()
     place = flags[9] * own_count
     loads = jnp.broadcast_to(table_ref[pl.ds(place // 128, 1), :], (8, 128))
     loads = pltpu.roll(loads, (128 - place % 128) % 128, 1)
@@ -512,8 +554,8 @@
         first, last = own[:3], own[61:]
         mirror_lo = sign * jnp.concatenate([first[2:3], first[1:2], first[0:1]], axis=0)
         mirror_hi = sign * jnp.concatenate([last[2:3], last[1:2], last[0:1]], axis=0)
-        below = jnp.where(flags[4] == 1, mirror_lo, got(c, flags[8] == 0))
-        above = jnp.where(flags[5] == 1, mirror_hi, got(c, flags[8] == 1))
+        below = jnp.where(flags[4], mirror_lo, got(c, flags[8] == 0))
+        above = jnp.where(flags[5], mirror_hi, got(c, flags[8] == 1))
         ext[pl.ds(c * 72, 3), :] = jnp.where(low3, below, swap_halves(last))
         ext[pl.ds(c * 72 + 3, 64), :] = own
         ext[pl.ds(c * 72 + 67, 3), :] = jnp.where(low3, swap_halves(first), above)
@@ -555,40 +597,40 @@
     return jax.ShapeDtypeStruct(table.shape, F32)
 
 
-def flux_x(flags, recon, layers, table):
+def flux_x(recon, acc, layers, table):
     return pl.pallas_call(
         lambda *a: flux_x_kernel(len(layers), *a),
         out_shape=[jax.ShapeDtypeStruct(recon.shape, F32), token_shape(table)],
-        in_specs=[SM] + [VM] * (1 + len(layers)),
+        in_specs=[VM] * (2 + len(layers)),
         out_specs=[VM] * 2,
         scratch_shapes=halo_scratch() + state_scratch(),
         compiler_params=GRANT,
         cost_estimate=cost(2),
         name="flux_x",
-    )(flags, recon, *layers)
-
-
-def flux_y(flags, recon, acc, layers):
+    )(recon, acc, *layers)
+
+
+def flux_y(recon, layers, table):
     return pl.pallas_call(
         lambda *a: flux_y_kernel(len(layers), *a),
-        out_shape=jax.ShapeDtypeStruct(recon.shape, F32),
-        in_specs=[SM] + [VM] * (2 + len(layers)),
-        out_specs=VM,
+        out_shape=[jax.ShapeDtypeStruct(recon.shape, F32), token_shape(table)],
+        in_specs=[VM] * (1 + len(layers)),
+        out_specs=[VM] * 2,
         scratch_shapes=halo_scratch() + state_scratch(),
         compiler_params=GRANT,
         cost_estimate=cost(2),
         name="flux_y",
-    )(flags, recon, acc, *layers)
-
-
-def flux_z(flags, fields, turned, acc, source, table, layers, own_count):
+    )(recon, *layers)
+
+
+def flux_z(fields, turned, acc, source, table, layers, own_count):
     return pl.pallas_call(
         lambda *a: flux_z_kernel(len(layers), own_count, *a),
         out_shape=[
             jax.ShapeDtypeStruct(fields.shape, F32),
             jax.ShapeDtypeStruct((1, own_count), F32),
         ],
-        in_specs=[SM] + [VM] * (5 + len(layers)),
+        in_specs=[VM] * (5 + len(layers)),
         out_specs=[HBM, VM],
         scratch_shapes=[pltpu.VMEM((COMPS * 72, 128), F32)]
         + state_scratch()
@@ -597,7 +639,7 @@
         compiler_params=GRANT,
         cost_estimate=cost(3),
         name="flux_z",
-    )(flags, fields, turned, acc, source, table, *layers)
+    )(fields, turned, acc, source, table, *layers)
 
 
 def swap(x, axis, second, outer=False):
@@ -618,12 +660,6 @@
     return table
 
 
-def split_table(table):
-    hi = lax.reduce_precision(table, 8, 7)
-    mid = lax.reduce_precision(table - hi, 8, 7)
-    return jnp.concatenate([hi, mid, table - hi - mid], axis=0).astype(BF16)
-
-
 def join_table(rows, height):
     rows = rows[: 3 * height].astype(F32)
     return rows[:height] + rows[height : 2 * height] + rows[2 * height :]
@@ -632,10 +668,6 @@
 def body(fields, reacting, panel_map, layer_one, layer_two, layer_three, layer_four):
     shape = fields.shape
     sizes = [lax.axis_size(a) for a in AXES]
-    index = [lax.axis_index(a) for a in AXES]
-    place = (index[0] * sizes[1] + index[1]) * sizes[2] + index[2]
-    flags = [f for i, n in zip(index, sizes) for f in (i == 0, i == n - 1)]
-    flags = jnp.stack([f.astype(jnp.int32) for f in flags] + [i % 2 for i in index] + [place])
     pair_x = sizes[0] == 2
     panels_all = 2 * (shape[1] * sizes[0] // PATCH) * (shape[3] * sizes[2] // PATCH)
     own = panels_all // (sizes[0] * sizes[1] * sizes[2])
@@ -645,29 +677,27 @@
     ride_y, ride_z = sizes[1] & (sizes[1] - 1) == 0, sizes[2] in (2, 4)
 
     flat = fields.reshape(-1, shape[3])
-    flat, recon, y_first, y_second, table = pack(
-        flat, panel_map.reshape(-1, shape[3]), flags, height
-    )
+    panels, react = panel_map.reshape(-1, shape[3]), reacting.reshape(-1, shape[3])
+    layers = (layer_one.T, layer_two, layer_three, layer_four)
+    packed = pack(flat, panels, react, layers, height)
+    flat, recon, y_first, y_second, table, react, one, two, three, four = packed
     y_got = [swap(y_first, "gy", 0)]
     if sizes[1] > 2:
         y_got.append(swap(y_second, "gy", 1))
-    layers = (layer_one.T, layer_two, layer_three, layer_four)
-    turned, *xs, z_first, z_second, hidden, row_slot, hit, w2, w3, w4, token = turn(
-        flags, recon, reacting.reshape(-1, shape[3]), layers, slots, pair_x, height
-    )
-    if pair_x and ride_y:
-        merged, table = merge(table, y_got[0], token, xs[0])
-        xs = [merged]
+    turned, *xs, z_first, z_second, token = turn(recon, pair_x, height)
+    hidden, row_slot, hit, two_b, token_in = chem_in(recon, react, one, layer_two, slots, table)
+    table = table + token + token_in
+    if ride_y:
+        table = table + join_table(y_got[0][layer_rows:], height)
+        table = sum_over(table, "gy", 2)
     else:
-        table = table + token
-        if ride_y:
-            table = table + join_table(y_got[0][layer_rows:], height)
-        else:
-            table = lax.psum(table, "gy")
-        if pair_x:
-            xs = [lax.dynamic_update_slice(xs[0], split_table(table), (layer_rows, 0))]
+        table = lax.psum(table, "gy")
+    hidden, token = chem_mid(hidden, (two, two_b), three, table)
+    table = table + token
+    if pair_x:
+        xs = [put_table(table, xs[0])]
     x_got = [swap(x, "gx", m) for m, x in enumerate(xs)]
-    source, token = chem(hidden, (w2, w3, w4), row_slot, hit, table)
+    acc, token = flux_y(recon, y_got, table)
     if pair_x:
         table = table + join_table(x_got[0][layer_rows:], height)
     else:
@@ -676,19 +706,16 @@
     if not ride_z:
         table = sum_over(table, "gz")
     z_got = [swap(lax.dynamic_update_slice(z_first, table, (edge_rows, 0)), "gz", 0)]
+    source, token = chem_out(hidden, four, row_slot, hit, table)
     if ride_z:
-        table = table + z_got[0][edge_rows : edge_rows + height]
+        table = table + z_got[0][edge_rows : edge_rows + height] + token
     if sizes[2] > 2:
         z_second = lax.dynamic_update_slice(z_second, table, (edge_rows, 0))
         z_got.append(swap(z_second, "gz", 1, ride_z))
         if ride_z:
             table = table + z_got[1][edge_rows : edge_rows + height]
-    acc, token = flux_x(flags, recon, x_got, table)
-    table = table + token
-    if ride_y:
-        table = sum_over(table, "gy", 2)
-    acc = flux_y(flags, recon, acc, y_got)
-    new, impulse = flux_z(flags, flat, turned, acc, source, table, z_got, own)
+    acc, token = flux_x(recon, acc, x_got, table)
+    new, impulse = flux_z(flat, turned, acc, source, table + token, z_got, own)
     return new.reshape(shape), impulse.reshape(own)
 
 

time: 28.9 us -> 28.3 us (0.979)
  the two profiles are of different devices: /device:TPU:0 before, /device:TPU:9 now
where the time goes in v4:
time: 28.3 us; the launch traced here: 28.2 us
  starting transfers between devices  12.4 us (44%)
  Pallas kernels  11.8 us (42%)
  waiting for transfers between devices  3.15 us (11%)
  between operations  0.73 us (3%)
    ppermute x5, starting transfers between devices, swap(): lax.ppermute(x, axis, [(a, b) for a, b in pairs] + [(b, a) for a, b in pa...  10 us
    ppermute x5, waiting for transfers between devices, swap(): lax.ppermute(x, axis, [(a, b) for a, b in pairs] + [(b, a) for a, b in pa...  3.15 us
    pallas_call x1, Pallas kernels, flux_z(): pl.pallas_call(lambda *a: flux_z_kernel(len(layers), own_count, *a), out_...  2.76 us
    ppermute x1, starting transfers between devices, sum_over(): lax.ppermute(table, axis, [(i, i ^ step) for i in range(size)])  2.37 us
    pallas_call x1, Pallas kernels, chem_in(): pl.pallas_call(lambda *a: chem_in_kernel(slots, *a), out_shape=[jax.Shape...  2.35 us
    pallas_call x1, Pallas kernels, pack(): pl.pallas_call(pack_kernel, out_shape=outs, in_specs=[HBM] * 7, out_specs...  1.76 us
    pallas_call x1, Pallas kernels, chem_mid(): pl.pallas_call(chem_mid_kernel, out_shape=[jax.ShapeDtypeStruct((layer_th...  1.51 us
    pallas_call x1, Pallas kernels, flux_y(): pl.pallas_call(lambda *a: flux_y_kernel(len(layers), *a), out_shape=[jax....  1.26 us
  transfers between devices with their start and end apart: 6, of which 4 were waited for; matrix products, arithmetic and copies ran while one was open for 0% of the time, Pallas kernels for 26%

profile of v4, /device:TPU:9, one launch (start us, length us, event | category | flops | bytes accessed | tf_op | source)
XLA Modules:
  0.0 28.2 jit_solution(14841021941428966052)
XLA Ops:
  0.6 1.8 %pack.1 = (f32[768,128]{1,0:T(8,128)S(1)}, f32[768,128]{1,0:T(8,128)S(1)}, bf16[304,128]{1,0:T(8,128)(2,1)S(1)}, bf16[288,128]{1,0:T(8,128)(2,1)S(1)}, f32[2,128...) custom-call(f32[768,128]{1,0:T(8,128)} %bitcast.6, ...), custom_call_target="tpu_custom_call" | custom-call | bytes 7000000 | tf_op jit(solution)/shard_map/pack/pallas_call | solution.py:286
  2.4 0.1 collective-permute-start
  2.5 0.3 %turn.1 = (f32[768,128]{1,0:T(8,128)S(1)}, bf16[304,128]{1,0:T(8,128)(2,1)S(1)}, f32[48,128]{1,0:T(8,128)S(1)}, f32[48,128]{1,0:T(8,128)S(1)}, f32[2,128]{1,0:T(2,128)S(1)}) custom-call(f32[768,128]{1,0:T(8,128)S(1)} %get-tuple-element.33.a_0_), custom_call_target="tpu_custom_call" | custom-call | bytes 3500000 | tf_op jit(solution)/shard_map/turn/pallas_call | solution.py:334
  2.8 2.3 %chem_in.1 = (bf16[1600,128]{1,0:T(8,128)(2,1)S(1)}, bf16[64,128]{1,0:T(8,128)(2,1)S(1)}, bf16[128,128]{1,0:T(8,128)(2,1)S(1)}, bf16[400,1600]{1,0:T(8,128)(2,1)S(1)}, f32[2,128]{1,0:T(2,128)S(1)}) custom-call(f32[768,128]{1,0:T(8,128)S(1)} %get-tuple-element.33.a_0_, s32[64,128]{1,0:T(8,128)S(1)} %get-tuple-element.40.a_1_, ...), custom_call_target="tpu_custom_call" | custom-call | bytes 3500000 | tf_op jit(solution)/shard_map/chem_in/pallas_call | solution.py:404
  5.2 0.5 %collective-permute-done.a_1_ = bf16[304,128]{1,0:T(8,128)(2,1)S(1)} collective-permute-done((bf16[304,128]{1,0:T(8,128)(2,1)S(1)}, bf16[304,128]{1,0:T(8,128)(2,1)S(1)}, u32[]{:S(2)}, u32[]{:S(2)}) %collective-permute-start) | collective-permute-done | bytes 77856 | tf_op jit(solution)/shard_map/ppermute | solution.py:650
  5.7 2.4 %collective-permute-start.2 = (f32[2,128]{1,0:T(2,128)S(1)}, f32[2,128]{1,0:T(2,128)S(1)}, u32[]{:S(2)}, u32[]{:S(2)}) collective-permute-start(f32[2,128]{1,0:T(2,128)S(1)} %add_add_fusion.2), channel_id=1, source_target_pairs={{0,8},{4,12},{8,0},{12,4},{1,9},{5,13},{9,1},{13,5},{2,10},{6,14},... | collective-permute-start | bytes 3080 | tf_op jit(solution)/shard_map/ppermute | solution.py:658
  8.1 1.5 %chem_mid.1 = (bf16[400,128]{1,0:T(8,128)(2,1)S(1)}, f32[2,128]{1,0:T(2,128)S(1)}) custom-call(bf16[1600,128]{1,0:T(8,128)(2,1)S(1)} %get-tuple-element.43.h_ref, bf16[400,1600]{1,0:T(8,128)(2,1)S(1)} %get-tuple-element.44.w2_ref, bf16[400,1600]{1,0:T(8,128)(2,1)S(1)} %get-tuple-element.45.w2b_ref, bf16[400,800]{1,0:T(8,128)(2,1)S(1)} %get-tuple-element.46.w3_ref), custom_call_target="tpu_custom_call" | custom-call | bytes 7000000 | tf_op jit(solution)/shard_map/chem_mid/pallas_call | solution.py:430
  9.6 0.0 collective-permute-done.2
  9.7 1.3 %collective-permute-start.3 = (bf16[304,128]{1,0:T(8,128)(2,1)S(1)}, bf16[304,128]{1,0:T(8,128)(2,1)S(1)}, u32[]{:S(2)}, u32[]{:S(2)}) collective-permute-start(bf16[304,128]{1,0:T(8,128)(2,1)S(1)} %put_table.1), channel_id=1, source_target_pairs={{0,16},{16,0},{1,17},{17,1},{2,18},{18,2},{3,19},{19,3},{4,20},{20... | collective-permute-start | bytes 233480 | tf_op jit(solution)/shard_map/ppermute | solution.py:650
  10.9 3.4 %collective-permute-start.1 = (bf16[288,128]{1,0:T(8,128)(2,1)S(1)}, bf16[288,128]{1,0:T(8,128)(2,1)S(1)}, u32[]{:S(2)}, u32[]{:S(2)}) collective-permute-start(bf16[288,128]{1,0:T(8,128)(2,1)S(1)} %get-tuple-element.36), channel_id=1, source_target_pairs={{4,8},{8,4},{5,9},{9,5},{6,10},{10,6},{7,11},{11,7},{20,24},{24,20... | collective-permute-start | bytes 221192 | tf_op jit(solution)/shard_map/ppermute | solution.py:650
  14.4 1.8 %collective-permute-done.1.a_2_ = bf16[288,128]{1,0:T(8,128)(2,1)S(1)} collective-permute-done((bf16[288,128]{1,0:T(8,128)(2,1)S(1)}, bf16[288,128]{1,0:T(8,128)(2,1)S(1)}, u32[]{:S(2)}, u32[]{:S(2)}) %collective-permute-start.1) | collective-permute-done | bytes 73760 | tf_op jit(solution)/shard_map/ppermute | solution.py:650
  16.2 1.3 %flux_y.1 = (f32[768,128]{1,0:T(8,128)S(1)}, f32[2,128]{1,0:T(2,128)S(1)}) custom-call(f32[768,128]{1,0:T(8,128)S(1)} %get-tuple-element.33.a_0_, bf16[304,128]{1,0:T(8,128)(2,1)S(1)} %collective-permute-done.a_1_, bf16[288,128]{1,0:T(8,128)(2,1)S(1)} %collective-permute-done.1.a_2_), custom_call_target="tpu_custom_call" | custom-call | bytes 7000000 | tf_op jit(solution)/shard_map/flux_y/pallas_call | solution.py:614
  17.4 0.0 collective-permute-done.3.a_2_
  17.5 3.8 %collective-permute-start.4 = (f32[48,128]{1,0:T(8,128)S(1)}, f32[48,128]{1,0:T(8,128)S(1)}, u32[]{:S(2)}, u32[]{:S(2)}) collective-permute-start(f32[48,128]{1,0:T(8,128)S(1)} %get-tuple-element.62), channel_id=1, source_target_pairs={{0,1},{2,3},{1,0},{3,2},{4,5},{6,7},{5,4},{7,6},{8,9},{10,11},{9,8... | collective-permute-start | bytes 73736 | tf_op jit(solution)/shard_map/ppermute | solution.py:650
  21.3 0.7 %chem_out.1 = (f32[768,128]{1,0:T(8,128)S(1)}, f32[2,128]{1,0:T(2,128)S(1)}) custom-call(bf16[400,128]{1,0:T(8,128)(2,1)S(1)} %get-tuple-element.50.h_ref, bf16[12,400]{1,0:T(8,128)(2,1)S(1)} %get-tuple-element.51.w4_ref, bf16[64,128]{1,0:T(8,128)(2,1)S(1)} %get-tuple-element.52.row_ref, bf16[128,128]{1,0:T(8,128)(2,1)S(1)} %get-tuple-element.53.hit_ref), custom_call_target="tpu_custom_call" | custom-call | bytes 3500000 | tf_op jit(solution)/shard_map/chem_out/pallas_call | solution.py:457
  21.9 0.2 collective-permute-done.4.a_5_
  22.1 1.5 %collective-permute-start.5 = (f32[48,128]{1,0:T(8,128)S(1)}, f32[48,128]{1,0:T(8,128)S(1)}, u32[]{:S(2)}, u32[]{:S(2)}) collective-permute-start(f32[48,128]{1,0:T(8,128)S(1)} %constant_dynamic-update-slice_fusion), channel_id=1, source_target_pairs={{1,2},{0,3},{2,1},{3,0},{5,6},{4,7},{6,5},{7,4},{9,10},{8,11},{10,... | collective-permute-start | bytes 73736 | tf_op jit(solution)/shard_map/ppermute | solution.py:650
  23.6 1.2 %flux_x.1 = (f32[768,128]{1,0:T(8,128)S(1)}, f32[2,128]{1,0:T(2,128)S(1)}) custom-call(f32[768,128]{1,0:T(8,128)S(1)} %get-tuple-element.33.a_0_, f32[768,128]{1,0:T(8,128)S(1)} %get-tuple-element.37.a_1_, bf16[304,128]{1,0:T(8,128)(2,1)S(1)} %collective-permute-done.3.a_2_), custom_call_target="tpu_custom_call" | custom-call | bytes 7000000 | tf_op jit(solution)/shard_map/flux_x/pallas_call | solution.py:601
  24.8 0.6 %collective-permute-done.5.a_6_ = f32[48,128]{1,0:T(8,128)S(1)} collective-permute-done((f32[48,128]{1,0:T(8,128)S(1)}, f32[48,128]{1,0:T(8,128)S(1)}, u32[]{:S(2)}, u32[]{:S(2)}) %collective-permute-start.5) | collective-permute-done | bytes 24608 | tf_op jit(solution)/shard_map/ppermute | solution.py:650
  25.4 2.8 %flux_z.1 = (f32[768,128]{1,0:T(8,128)}, f32[1,8]{1,0:T(1,128)}) custom-call(f32[768,128]{1,0:T(8,128)S(1)} %get-tuple-element.32.a_0_, f32[768,128]{1,0:T(8,128)S(1)} %get-tuple-element.34.a_1_, f32[768,128]{1,0:T(8,128)S(1)} %get-tuple-element.49.a_2_, f32[768,128]{1,0:T(8,128)S(1)} %get-tuple-element.54.a_3_, f32[2,128]{1,0:T(2,128)S(1)} %fusion.a_4_, ...), custom_call_target="tpu_custom_call" | custom-call | bytes 10500000 | tf_op jit(solution)/shard_map/flux_z/pallas_call | solution.py:627
  (8 shorter events, 0.1 us)
Async XLA Ops:
  2.4 3.3 %collective-permute-start = (bf16[304,128]{1,0:T(8,128)(2,1)S(1)}, bf16[304,128]{1,0:T(8,128)(2,1)S(1)}, u32[]{:S(2)}, u32[]{:S(2)}) collective-permute-start(bf16[304,128]{1,0:T(8,128)(2,1)S(1)} %get-tuple-element.35), channel_id=1, source_target_pairs={{0,4},{8,12},{4,0},{12,8},{1,5},{9,13},{5,1},{13,9},{2,6},{10,14},... | collective-permute-start | bytes 233480 | tf_op jit(solution)/shard_map/ppermute | solution.py:650
  5.7 3.9 %collective-permute-start.2 = (f32[2,128]{1,0:T(2,128)S(1)}, f32[2,128]{1,0:T(2,128)S(1)}, u32[]{:S(2)}, u32[]{:S(2)}) collective-permute-start(f32[2,128]{1,0:T(2,128)S(1)} %add_add_fusion.2), channel_id=1, source_target_pairs={{0,8},{4,12},{8,0},{12,4},{1,9},{5,13},{9,1},{13,5},{2,10},{6,14},... | collective-permute-start | bytes 3080 | tf_op jit(solution)/shard_map/ppermute | solution.py:658
  9.7 7.8 %collective-permute-start.3 = (bf16[304,128]{1,0:T(8,128)(2,1)S(1)}, bf16[304,128]{1,0:T(8,128)(2,1)S(1)}, u32[]{:S(2)}, u32[]{:S(2)}) collective-permute-start(bf16[304,128]{1,0:T(8,128)(2,1)S(1)} %put_table.1), channel_id=1, source_target_pairs={{0,16},{16,0},{1,17},{17,1},{2,18},{18,2},{3,19},{19,3},{4,20},{20... | collective-permute-start | bytes 233480 | tf_op jit(solution)/shard_map/ppermute | solution.py:650
  10.9 5.2 %collective-permute-start.1 = (bf16[288,128]{1,0:T(8,128)(2,1)S(1)}, bf16[288,128]{1,0:T(8,128)(2,1)S(1)}, u32[]{:S(2)}, u32[]{:S(2)}) collective-permute-start(bf16[288,128]{1,0:T(8,128)(2,1)S(1)} %get-tuple-element.36), channel_id=1, source_target_pairs={{4,8},{8,4},{5,9},{9,5},{6,10},{10,6},{7,11},{11,7},{20,24},{24,20... | collective-permute-start | bytes 221192 | tf_op jit(solution)/shard_map/ppermute | solution.py:650
  17.5 4.6 %collective-permute-start.4 = (f32[48,128]{1,0:T(8,128)S(1)}, f32[48,128]{1,0:T(8,128)S(1)}, u32[]{:S(2)}, u32[]{:S(2)}) collective-permute-start(f32[48,128]{1,0:T(8,128)S(1)} %get-tuple-element.62), channel_id=1, source_target_pairs={{0,1},{2,3},{1,0},{3,2},{4,5},{6,7},{5,4},{7,6},{8,9},{10,11},{9,8... | collective-permute-start | bytes 73736 | tf_op jit(solution)/shard_map/ppermute | solution.py:650
  22.1 3.3 %collective-permute-start.5 = (f32[48,128]{1,0:T(8,128)S(1)}, f32[48,128]{1,0:T(8,128)S(1)}, u32[]{:S(2)}, u32[]{:S(2)}) collective-permute-start(f32[48,128]{1,0:T(8,128)S(1)} %constant_dynamic-update-slice_fusion), channel_id=1, source_target_pairs={{1,2},{0,3},{2,1},{3,0},{5,6},{4,7},{6,5},{7,4},{9,10},{8,11},{10,... | collective-permute-start | bytes 73736 | tf_op jit(solution)/shard_map/ppermute | solution.py:650
